TPU v7x, 32 devices: a whole 2x2x4 slice. The times are simulated.
32 devices in a mesh: dp: 16 (over z, y, core), tensor: 2 (over x).
Axes of the slice: x: 2, y: 2, z: 4, core: 2. Of those that a mesh axis runs over, the one named last changes fastest.
Arguments:
- inputs: bfloat16 [8192, 1024], P('dp'), may hold values from -6 to 6
- first_values: bfloat16 [8192, 1024], P('dp', 'tensor'), may hold values from -6 to 6
- w_query: bfloat16 [1024, 1024], P(None, 'tensor'), may hold values from -0.1875 to 0.1875
- w_key: bfloat16 [1024, 1024], P(None, 'tensor'), may hold values from -0.1875 to 0.1875
- w_value: bfloat16 [1024, 1024], P(None, 'tensor'), may hold values from -0.1875 to 0.1875
- w_out: bfloat16 [1024, 1024], P('tensor'), may hold values from -4 to 4
- w_gate: bfloat16 [1024, 2816], P(None, 'tensor'), may hold values from -0.1875 to 0.1875
- w_up: bfloat16 [1024, 2816], P(None, 'tensor'), may hold values from -0.1875 to 0.1875
- w_down: bfloat16 [2816, 1024], P('tensor'), may hold values from -0.109375 to 0.109375
- norm_attn: bfloat16 [1024], replicated, may hold values from 0.5 to 1.5
- norm_ffn: bfloat16 [1024], replicated, may hold values from 0.5 to 1.5
- cotangent: bfloat16 [8192, 1024], P('dp'), may hold values from -6 to 6
- parents: int32 [16], replicated, may hold values from -1 to 7, as said below
- depth_pos: int32 [16], replicated, may hold values from 0 to 2560, as said below
- assignment: int32 [16], replicated, may hold values from 0 to 15, as said below
Outputs:
- output: bfloat16 [8192, 1024], P('dp')
- grad_inputs: float32 [8192, 1024], P('dp')
- grad_first_values: float32 [8192, 1024], P('dp', 'tensor')
- grad_w_query: float32 [1024, 1024], P(None, 'tensor')
- grad_w_key: float32 [1024, 1024], P(None, 'tensor')
- grad_w_value: float32 [1024, 1024], P(None, 'tensor')
- grad_w_out: float32 [1024, 1024], P('tensor')
- grad_w_gate: float32 [1024, 2816], P(None, 'tensor')
- grad_w_up: float32 [1024, 2816], P(None, 'tensor')
- grad_w_down: float32 [2816, 1024], P('tensor')
- grad_norm_attn: float32 [1024], replicated
- grad_norm_ffn: float32 [1024], replicated
Inputs may be any that keep to these rules, and one draw needn't show every extreme that they name: `parents`: the tree-ordered segments form 1 trees of 16: segment 16 k is a root, 16 k + j has parent 16 k + j - 1 for j = 1, 2, 3, segments 16 k + 4 to 16 k + 7 have parent 16 k + 3, and each of 16 k + 8 to 16 k + 15 has one of 16 k + 4 to 16 k + 7 as parent, each of those the parent of exactly two. A permutation: tree-ordered segment g lies in slot assignment[g], that is in rows assignment[g] * 512 to assignment[g] * 512 + 511. depth_pos[s] is 512 times the number of strict ancestors of the segment in slot s.
All inputs are finite; a program needn't handle non-finite values.
Results may differ from a plain program's by a relative error of at most 0.025.
Values may be sent and summed in bfloat16 or wider, within the bound.
No kernel may reach another device: no remote copies, remote signals or barrier semaphores. Data moves between devices by JAX's collectives and lax.ppermute only.
A program may use at most 256 MiB of HBM per device.

v0:
```python
import jax
import jax.numpy as jnp
from jax import lax
from jax.sharding import PartitionSpec as P

HEAD_DIM = 64
SEG = 512


epsilon = 1e-06
rope_base = 10000.0
climb_steps = 5
masked_score = -1e30


def rms_scale(values):
    return lax.rsqrt(jnp.mean(values * values, axis=-1, keepdims=True) + epsilon)


def rotary_tables(positions, head_dim):
    half_dim = head_dim // 2
    frequency = rope_base ** (-jnp.arange(half_dim, dtype=jnp.float32) * 2.0 / head_dim)
    angles = positions.astype(jnp.float32)[:, None] * frequency[None, :]
    return (jnp.cos(angles)[:, None, :], jnp.sin(angles)[:, None, :])


def rotate(values, cosine, sine_table):
    half_dim = values.shape[-1] // 2
    first_half = values[..., :half_dim]
    second_half = values[..., half_dim:]
    return jnp.concatenate(
        [
            first_half * cosine - second_half * sine_table,
            second_half * cosine + first_half * sine_table,
        ],
        axis=-1,
    )


def rotate_back(gradient, cosine, sine_table):
    half_dim = gradient.shape[-1] // 2
    first_half = gradient[..., :half_dim]
    second_half = gradient[..., half_dim:]
    return jnp.concatenate(
        [
            first_half * cosine + second_half * sine_table,
            second_half * cosine - first_half * sine_table,
        ],
        axis=-1,
    )


def parent_slots(parents, assignment):
    count = parents.shape[0]
    slot_ids = jnp.arange(count, dtype=jnp.int32)
    at_slot = assignment[None, :] == slot_ids[:, None]
    parent_seg = jnp.sum(jnp.where(at_slot, parents[None, :], 0), axis=1)
    parent_match = slot_ids[None, :] == parent_seg[:, None]
    above_slot = jnp.sum(jnp.where(parent_match, assignment[None, :], 0), axis=1)
    return jnp.where(parent_seg >= 0, above_slot, -1)


def climb(parent_slot, start_slots):
    slot_ids = jnp.arange(parent_slot.shape[0], dtype=jnp.int32)
    levels = [start_slots]
    current = start_slots
    for step_index in range(climb_steps):
        matched = current[:, None] == slot_ids[None, :]
        upward = jnp.sum(jnp.where(matched, parent_slot[None, :], 0), axis=1)
        current = jnp.where(current >= 0, upward, -1)
        levels.append(current)
    return jnp.stack(levels, axis=1)


def norm_back(grad_normed, values, row_scale, gain_vector):
    scaled_grad = grad_normed * gain_vector
    grad_gain = jnp.sum(grad_normed * values * row_scale, axis=0)
    grad_values = row_scale * (
        scaled_grad
        - values * row_scale * row_scale * jnp.mean(scaled_grad * values, axis=-1, keepdims=True)
    )
    return (grad_values, grad_gain)


def path_rows(source, path_row):
    parts = []
    for level_index in range(climb_steps + 1):
        row_begin = (jnp.maximum(path_row[level_index], 0) * SEG).astype(jnp.int32)
        parts.append(lax.dynamic_slice_in_dim(source, row_begin, SEG, 0))
    return jnp.concatenate(parts, axis=0)


def path_permit(path_row, causal):
    parts = [causal]
    for level_index in range(1, climb_steps + 1):
        parts.append(jnp.broadcast_to(path_row[level_index] >= 0, (SEG, SEG)))
    return jnp.concatenate(parts, axis=1)


def body(
    inputs,
    first_values,
    w_query,
    w_key,
    w_value,
    w_out,
    w_gate,
    w_up,
    w_down,
    norm_attn,
    norm_ffn,
    cotangent,
    parents,
    depth_pos,
    assignment,
):
    row_count = inputs.shape[0]
    local_width = w_query.shape[1]
    head_count = local_width // HEAD_DIM
    score_scale = HEAD_DIM ** (-0.5)
    seg_count = row_count // SEG
    slot_total = parents.shape[0]
    slot_ids = jnp.arange(slot_total, dtype=jnp.int32)
    local_rows = jnp.arange(row_count, dtype=jnp.int32)
    own_slots = lax.axis_index("dp") * seg_count + jnp.arange(seg_count, dtype=jnp.int32)
    own_slot_rows = jnp.repeat(own_slots, SEG)
    depth_rows = jnp.sum(
        jnp.where(own_slot_rows[:, None] == slot_ids[None, :], depth_pos[None, :], 0), axis=1
    )
    positions = depth_rows + local_rows % SEG
    parent_slot = parent_slots(parents, assignment)
    own_paths = climb(parent_slot, own_slots)
    offsets = jnp.arange(SEG, dtype=jnp.int32)
    causal = offsets[None, :] <= offsets[:, None]
    cosine, sine_table = rotary_tables(positions, HEAD_DIM)
    inputs_wide = inputs.astype(jnp.float32)
    attn_scale = rms_scale(inputs_wide)
    gain_attn = norm_attn.astype(jnp.float32)
    normed = (inputs_wide * attn_scale * gain_attn).astype(jnp.bfloat16)
    query_proj = jnp.dot(normed, w_query, preferred_element_type=jnp.float32)
    key_proj = jnp.dot(normed, w_key, preferred_element_type=jnp.float32)
    value_proj = jnp.dot(normed, w_value, preferred_element_type=jnp.float32)
    query_rot = rotate(
        query_proj.reshape(row_count, head_count, HEAD_DIM), cosine, sine_table
    ).astype(jnp.bfloat16)
    key_rot = (
        rotate(key_proj.reshape(row_count, head_count, HEAD_DIM), cosine, sine_table)
        .astype(jnp.bfloat16)
        .reshape(row_count, local_width)
    )
    mixed = (0.5 * value_proj + 0.5 * first_values.astype(jnp.float32)).astype(jnp.bfloat16)
    key_all, value_all = (
        lax.all_gather(key_rot, "dp", axis=0, tiled=True),
        lax.all_gather(mixed, "dp", axis=0, tiled=True),
    )
    query_segs = query_rot.reshape(seg_count, SEG, head_count, HEAD_DIM)

    def segment_forward(operand):
        query_block, path_row = operand
        near_keys = path_rows(key_all, path_row).reshape(-1, head_count, HEAD_DIM)
        near_values = path_rows(value_all, path_row).reshape(-1, head_count, HEAD_DIM)
        permit = path_permit(path_row, causal)
        scores = (
            jnp.einsum("qhd,khd->hqk", query_block, near_keys, preferred_element_type=jnp.float32)
            * score_scale
        )
        scores = jnp.where(permit[None], scores, masked_score)
        row_max = jnp.max(scores, axis=-1)
        weights = jnp.where(permit[None], jnp.exp(scores - row_max[..., None]), 0.0)
        row_total = jnp.sum(weights, axis=-1)
        attn_probs = weights / row_total[..., None]
        block_out = jnp.einsum(
            "hqk,khd->qhd",
            attn_probs.astype(jnp.bfloat16),
            near_values,
            preferred_element_type=jnp.float32,
        )
        return (block_out, row_max + jnp.log(row_total))

    attn_parts, log_parts = lax.map(segment_forward, (query_segs, own_paths))
    attn_exact = attn_parts.reshape(row_count, head_count, HEAD_DIM)
    attended = attn_exact.reshape(row_count, local_width).astype(jnp.bfloat16)
    branch_attn = lax.psum(
        jnp.dot(attended, w_out, preferred_element_type=jnp.float32).astype(jnp.bfloat16), "tensor"
    ).astype(jnp.float32)
    hidden_state = inputs_wide + branch_attn
    ffn_scale = rms_scale(hidden_state)
    gain_ffn = norm_ffn.astype(jnp.float32)
    normed_ffn = (hidden_state * ffn_scale * gain_ffn).astype(jnp.bfloat16)
    gate_proj = jnp.dot(normed_ffn, w_gate, preferred_element_type=jnp.float32)
    up_proj = jnp.dot(normed_ffn, w_up, preferred_element_type=jnp.float32)
    silu_gate = jax.nn.silu(gate_proj)
    activated = (silu_gate * up_proj).astype(jnp.bfloat16)
    feed = lax.psum(
        jnp.dot(activated, w_down, preferred_element_type=jnp.float32).astype(jnp.bfloat16),
        "tensor",
    ).astype(jnp.float32)
    output = (hidden_state + feed).astype(jnp.bfloat16)
    grad_w_down = jnp.einsum("tf,td->fd", activated, cotangent, preferred_element_type=jnp.float32)
    grad_activated = jnp.einsum("td,fd->tf", cotangent, w_down, preferred_element_type=jnp.float32)
    sigmoid_gate = jax.nn.sigmoid(gate_proj)
    grad_gate = (
        grad_activated * up_proj * sigmoid_gate * (1.0 + gate_proj * (1.0 - sigmoid_gate))
    ).astype(jnp.bfloat16)
    grad_up = (grad_activated * silu_gate).astype(jnp.bfloat16)
    grad_w_gate = jnp.einsum("td,tf->df", normed_ffn, grad_gate, preferred_element_type=jnp.float32)
    grad_w_up = jnp.einsum("td,tf->df", normed_ffn, grad_up, preferred_element_type=jnp.float32)
    ffn_partial = jnp.einsum(
        "tf,df->td", grad_gate, w_gate, preferred_element_type=jnp.float32
    ) + jnp.einsum("tf,df->td", grad_up, w_up, preferred_element_type=jnp.float32)
    grad_normed_ffn = lax.psum(ffn_partial.astype(jnp.bfloat16), "tensor").astype(jnp.float32)
    grad_hidden_norm, grad_gain_ffn = norm_back(grad_normed_ffn, hidden_state, ffn_scale, gain_ffn)
    grad_hidden = cotangent.astype(jnp.float32) + grad_hidden_norm
    grad_branch = grad_hidden.astype(jnp.bfloat16)
    grad_w_out = jnp.einsum("tc,td->cd", attended, grad_branch, preferred_element_type=jnp.float32)
    grad_attended = jnp.einsum(
        "td,cd->tc", grad_branch, w_out, preferred_element_type=jnp.float32
    ).astype(jnp.bfloat16)
    grad_heads = grad_attended.reshape(row_count, head_count, HEAD_DIM)
    delta_rows = jnp.sum(grad_heads.astype(jnp.float32) * attn_exact, axis=-1)
    delta_parts = jnp.transpose(delta_rows.reshape(seg_count, SEG, head_count), (0, 2, 1))
    grad_segs = grad_heads.reshape(seg_count, SEG, head_count, HEAD_DIM)
    key_back, value_back = (key_all, value_all)

    def segment_back(query_block, grad_block, path_row, log_block, delta_block):
        near_keys = path_rows(key_back, path_row).reshape(-1, head_count, HEAD_DIM)
        near_values = path_rows(value_back, path_row).reshape(-1, head_count, HEAD_DIM)
        permit = path_permit(path_row, causal)
        scores = (
            jnp.einsum("qhd,khd->hqk", query_block, near_keys, preferred_element_type=jnp.float32)
            * score_scale
        )
        scores = jnp.where(permit[None], scores, masked_score)
        attn_probs = jnp.where(permit[None], jnp.exp(scores - log_block[..., None]), 0.0)
        grad_probs = jnp.einsum(
            "qhd,khd->hqk", grad_block, near_values, preferred_element_type=jnp.float32
        )
        grad_scores = (attn_probs * (grad_probs - delta_block[..., None])).astype(jnp.bfloat16)
        grad_part = (
            jnp.einsum("hqk,khd->qhd", grad_scores, near_keys, preferred_element_type=jnp.float32)
            * score_scale
        )
        return (attn_probs, grad_scores, grad_part)

    zero_rows = jnp.zeros((key_back.shape[0], local_width), jnp.float32)

    def scatter_step(fold_state, operand):
        key_acc, value_acc = fold_state
        query_block, grad_block, path_row, log_block, delta_block = operand
        attn_probs, grad_scores, grad_part = segment_back(
            query_block, grad_block, path_row, log_block, delta_block
        )
        key_term = (
            jnp.einsum("hqk,qhd->khd", grad_scores, query_block, preferred_element_type=jnp.float32)
            * score_scale
        ).reshape(climb_steps + 1, SEG, local_width)
        value_term = jnp.einsum(
            "hqk,qhd->khd",
            attn_probs.astype(jnp.bfloat16),
            grad_block,
            preferred_element_type=jnp.float32,
        ).reshape(climb_steps + 1, SEG, local_width)
        for level_index in range(climb_steps + 1):
            row_begin = (jnp.maximum(path_row[level_index], 0) * SEG).astype(jnp.int32)
            key_acc = lax.dynamic_update_slice_in_dim(
                key_acc,
                lax.dynamic_slice_in_dim(key_acc, row_begin, SEG, 0) + key_term[level_index],
                row_begin,
                0,
            )
            value_acc = lax.dynamic_update_slice_in_dim(
                value_acc,
                lax.dynamic_slice_in_dim(value_acc, row_begin, SEG, 0) + value_term[level_index],
                row_begin,
                0,
            )
        return ((key_acc, value_acc), grad_part)

    (key_terms, value_terms), grad_parts = lax.scan(
        scatter_step,
        (zero_rows, zero_rows),
        (query_segs, grad_segs, own_paths, log_parts, delta_parts),
    )
    grad_query_rot = grad_parts.reshape(row_count, head_count, HEAD_DIM)
    key_sums, value_sums = (
        lax.psum_scatter(
            key_terms.astype(jnp.bfloat16), "dp", scatter_dimension=0, tiled=True
        ).astype(jnp.float32),
        lax.psum_scatter(
            value_terms.astype(jnp.bfloat16), "dp", scatter_dimension=0, tiled=True
        ).astype(jnp.float32),
    )
    grad_key_rot = key_sums.reshape(row_count, head_count, HEAD_DIM)
    grad_first_values = 0.5 * value_sums
    grad_value = (0.5 * value_sums).astype(jnp.bfloat16)
    grad_key = (
        rotate_back(grad_key_rot, cosine, sine_table)
        .reshape(row_count, local_width)
        .astype(jnp.bfloat16)
    )
    grad_query = (
        rotate_back(grad_query_rot, cosine, sine_table)
        .reshape(row_count, local_width)
        .astype(jnp.bfloat16)
    )
    grad_w_query = jnp.einsum("td,tc->dc", normed, grad_query, preferred_element_type=jnp.float32)
    grad_w_key = jnp.einsum("td,tc->dc", normed, grad_key, preferred_element_type=jnp.float32)
    grad_w_value = jnp.einsum("td,tc->dc", normed, grad_value, preferred_element_type=jnp.float32)
    attn_partial = (
        jnp.einsum("tc,dc->td", grad_query, w_query, preferred_element_type=jnp.float32)
        + jnp.einsum("tc,dc->td", grad_key, w_key, preferred_element_type=jnp.float32)
        + jnp.einsum("tc,dc->td", grad_value, w_value, preferred_element_type=jnp.float32)
    )
    grad_normed = lax.psum(attn_partial.astype(jnp.bfloat16), "tensor").astype(jnp.float32)
    grad_input_norm, grad_gain_attn = norm_back(grad_normed, inputs_wide, attn_scale, gain_attn)
    grad_inputs = grad_hidden + grad_input_norm
    summed = (
        lax.psum(grad_w_query.astype(jnp.bfloat16), "dp").astype(jnp.float32),
        lax.psum(grad_w_key.astype(jnp.bfloat16), "dp").astype(jnp.float32),
        lax.psum(grad_w_value.astype(jnp.bfloat16), "dp").astype(jnp.float32),
        lax.psum(grad_w_out.astype(jnp.bfloat16), "dp").astype(jnp.float32),
        lax.psum(grad_w_gate.astype(jnp.bfloat16), "dp").astype(jnp.float32),
        lax.psum(grad_w_up.astype(jnp.bfloat16), "dp").astype(jnp.float32),
        lax.psum(grad_w_down.astype(jnp.bfloat16), "dp").astype(jnp.float32),
        lax.psum(grad_gain_attn.astype(jnp.bfloat16), "dp").astype(jnp.float32),
        lax.psum(grad_gain_ffn.astype(jnp.bfloat16), "dp").astype(jnp.float32),
    )
    return (
        output,
        grad_inputs,
        grad_first_values,
        summed[0],
        summed[1],
        summed[2],
        summed[3],
        summed[4],
        summed[5],
        summed[6],
        summed[7],
        summed[8],
    )


def solution(mesh):
    placed = (
        P("dp", None),
        P("dp", "tensor"),
        P(None, "tensor"),
        P(None, "tensor"),
        P(None, "tensor"),
        P("tensor", None),
        P(None, "tensor"),
        P(None, "tensor"),
        P("tensor", None),
        P(),
        P(),
        P("dp", None),
        P(),
        P(),
        P(),
    )
    return jax.shard_map(
        body,
        mesh=mesh,
        in_specs=placed,
        out_specs=(
            P("dp", None),
            P("dp", None),
            P("dp", "tensor"),
            P(None, "tensor"),
            P(None, "tensor"),
            P(None, "tensor"),
            P("tensor", None),
            P(None, "tensor"),
            P(None, "tensor"),
            P("tensor", None),
            P(),
            P(),
        ),
        check_vma=False,
    )
```

profile of v0, /device:TPU:0, one launch (start us, length us, event | category | flops | bytes accessed | tf_op | source)
XLA Modules:
  0.0 1030.7 jit_solution(15380133713444836444)
XLA Ops:
  29.8 60.8 %all-gather.3.cloned.1.call-done = bf16[8192,512]{1,0:T(8,128)(2,1)} async-done(((bf16[512,512]{1,0:T(8,128)(2,1)}), bf16[8192,512]{1,0:T(8,128)(2,1)}) %all-gather.3.cloned.1.call-update) | async-done | bytes 8388624 | tf_op jit(solution)/shard_map/all_gather | solution.py:154
  101.9 4.8 copy.57
  106.7 63.1 %all-gather.5.cloned.1.call-done = bf16[8192,512]{0,1:T(8,128)(2,1)} async-done(((bf16[512,512]{0,1:T(8,128)(2,1)}), bf16[8192,512]{0,1:T(8,128)(2,1)}) %all-gather.5.cloned.1.call-update) | async-done | bytes 8388624 | tf_op jit(solution)/shard_map/all_gather | solution.py:153
  180.9 22.8 %fusion.2 = (f32[8,512]{1,0:T(8,128)S(1)}, f32[8,512,3072]{2,1,0:T(8,128)}) fusion(pred[512,3072]{1,0:T(8,128)(4,1)} %broadcast_dynamic-update-slice_fusion, bf16[3072,8,64]{0,2,1:T(8,128)(2,1)} %bitcast.4, bf16[512,8,32]{0,2,1:T(8,128)(2,1)S(1)} %get-tuple-element.111, bf16[512,8,32]{0,2,1:T(8,128)(2,1)S(1)} %get-tuple-element.110), kind=kOutput, calls=%fused_computation.7 | convolution fusion | flops 1649405952 | bytes 55590912 | tf_op jit(solution)/shard_map/while/body/eval_jaxpr/qhd,khd->hqk/dot_general | solution.py:164
  203.7 23.2 %fusion = f32[8,512]{1,0:T(8,128)S(1)} fusion(f32[8,512,3072]{2,1,0:T(8,128)} %get-tuple-element.121, f32[8,512]{1,0:T(8,128)S(1)} %get-tuple-element.120, pred[512,3072]{1,0:T(8,128)(4,1)} %broadcast_dynamic-update-slice_fusion), kind=kLoop, calls=%fused_computation.5 | loop fusion | flops 62910464 | bytes 51937280 | tf_op jit(solution)/shard_map/while/body/eval_jaxpr/reduce_sum | solution.py:170
  226.9 22.0 %fusion.68 = (bf16[512,8,64]{0,2,1:T(8,128)(2,1)S(1)}, f32[512,8,64]{0,2,1:T(8,128)}) fusion(bf16[3072,8,64]{0,2,1:T(8,128)(2,1)S(1)} %bitcast.90, f32[8,512,3072]{2,1,0:T(8,128)} %get-tuple-element.121, f32[8,512]{1,0:T(8,128)S(1)} %fusion, f32[8,512]{1,0:T(8,128)S(1)} %get-tuple-element.120, pred[512,3072]{1,0:T(8,128)(4,1)} %broadcast_dynamic-update-slice_fusion), kind=kOutput, calls=%fused_computation.158 | convolution fusion | flops 1686372352 | bytes 56655872 | tf_op jit(solution)/shard_map/while/body/eval_jaxpr/hqk,khd->qhd/dot_general | solution.py:172
  251.7 38.1 %all-reduce.8.cloned.1.call-done = bf16[512,1024]{1,0:T(8,128)(2,1)} async-done(((bf16[512,1024]{1,0:T(8,128)(2,1)}), bf16[512,1024]{1,0:T(8,128)(2,1)}) %all-reduce.8.cloned.1.call-update) | async-done | bytes 1048592 | tf_op jit(solution)/shard_map/psum | solution.py:183
  306.6 40.1 %all-reduce.10.cloned.1.call-done = bf16[512,1024]{1,0:T(8,128)(2,1)} async-done(((bf16[512,1024]{1,0:T(8,128)(2,1)}), bf16[512,1024]{1,0:T(8,128)(2,1)}) %all-reduce.10.cloned.1.call-update) | async-done | bytes 1048592 | tf_op jit(solution)/shard_map/psum | solution.py:211
  354.2 24.3 %fusion.7 = f32[3072,8,64]{0,2,1:T(8,128)} fusion(bf16[512,8,64]{0,2,1:T(8,128)(2,1)} %bitcast.100, f32[8,512,3072]{2,1,0:T(8,128)} %get-tuple-element.121, f32[8,512]{1,0:T(8,128)S(1)} %log_add_fusion, pred[512,3072]{1,0:T(8,128)(4,1)} %broadcast_dynamic-update-slice_fusion), kind=kOutput, calls=%fused_computation.12 | convolution fusion | flops 1673527296 | bytes 58736640 | tf_op jit(solution)/shard_map/while/body/eval_jaxpr/hqk,qhd->khd/dot_general | solution.py:257
  378.5 32.9 %multiply_convert_fusion = bf16[8,512,3072]{2,1,0:T(8,128)(2,1)} fusion(f32[8,512,3072]{2,1,0:T(8,128)} %get-tuple-element.121, bf16[512,8,64]{0,2,1:T(8,128)(2,1)} %bitcast.101, bf16[3072,8,64]{0,2,1:T(8,128)(2,1)} %bitcast.89, f32[8,512]{1,0:T(8,128)S(1)} %bitcast.102, f32[8,512]{1,0:T(8,128)S(1)} %log_add_fusion, ...), kind=kOutput, calls=%fused_computation | convolution fusion | flops 1698693120 | bytes 80773120 | tf_op jit(solution)/shard_map/while/body/eval_jaxpr/qhd,khd->hqk/dot_general | solution.py:235
  411.4 10.7 %multiply_bitcast_fusion = f32[3072,8,64]{0,2,1:T(8,128)S(1)} fusion(bf16[8,512,3072]{2,1,0:T(8,128)(2,1)} %multiply_convert_fusion, bf16[512,8,32]{0,2,1:T(8,128)(2,1)S(1)} %copy-done.26, bf16[512,8,32]{0,2,1:T(8,128)(2,1)S(1)} %copy-done.24), kind=kOutput, calls=%fused_computation.11 | convolution fusion | flops 1613234176 | bytes 31981568 | tf_op jit(solution)/shard_map/while/body/eval_jaxpr/hqk,qhd->khd/dot_general | solution.py:254
  429.9 5.6 fusion.66
  453.1 7.9 broadcast_in_dim.186.clone
  493.9 9.2 convert_element_type.206
  507.4 14.5 %fusion.31 = f32[512,8,64]{0,2,1:T(8,128)} fusion(bf16[3072,8,64]{0,2,1:T(8,128)(2,1)} %bitcast.4, bf16[8,512,3072]{2,1,0:T(8,128)(2,1)} %multiply_convert_fusion), kind=kOutput, calls=%fused_computation.62 | convolution fusion | flops 1610874880 | bytes 29360128 | tf_op jit(solution)/shard_map/while/body/eval_jaxpr/hqk,khd->qhd/dot_general | solution.py:240
  521.8 55.8 %reduce-scatter.3.cloned.1.call-done = bf16[512,512]{1,0:T(8,128)(2,1)} async-done(((bf16[8192,512]{1,0:T(8,128)(2,1)}), bf16[512,512]{1,0:T(8,128)(2,1)}) %reduce-scatter.3.cloned.1.call-update) | async-done | bytes 524304 | tf_op jit(solution)/shard_map/reduce_scatter | solution.py:286
  586.1 99.8 %reduce-scatter.5.cloned.1.call-done = bf16[512,512]{1,0:T(8,128)(2,1)} async-done(((bf16[8192,512]{1,0:T(8,128)(2,1)}), bf16[512,512]{1,0:T(8,128)(2,1)}) %reduce-scatter.5.cloned.1.call-update) | async-done | bytes 524304 | tf_op jit(solution)/shard_map/reduce_scatter | solution.py:289
  688.1 4.2 add_convert_fusion
  692.4 5.2 convolution_convert_fusion.1
  712.4 42.9 %all-reduce.14.cloned.1.call-done = (bf16[512,1024]{1,0:T(8,128)(2,1)}, bf16[512,1024]{1,0:T(8,128)(2,1)}) async-done(((bf16[512,1024]{1,0:T(8,128)(2,1)}, bf16[512,1024]{1,0:T(8,128)(2,1)}), (bf16[512,1024]{1,0:T(8,128)(2,1)}, bf16[512,1024]{1,0:T(8,128)(2,1)})) %all-reduce.14.cloned.1.call-update) | async-done | bytes 2097168 | tf_op jit(solution)/shard_map/psum | solution.py:194
  757.8 34.7 %all-reduce = (bf16[1024]{0:T(1024)(128)(2,1)S(1)}, bf16[1024]{0:T(1024)(128)(2,1)S(1)}) all-reduce(bf16[1024]{0:T(1024)(128)(2,1)S(1)} %get-tuple-element.62, bf16[1024]{0:T(1024)(128)(2,1)S(1)} %copy-done.54), channel_id=1, replica_groups=mesh['dp'=16,'tensor'=2] {'dp'}, use_global_device_ids=true, to_apply=%region_29.30 | all-reduce | flops 2048 | bytes 8192 | tf_op jit(solution)/shard_map/psum | solution.py:325
  793.7 4.9 fusion.19
  798.6 207.5 %all-reduce.12.cloned.1.call-done = (bf16[1024,512]{1,0:T(8,128)(2,1)}, bf16[1024,512]{1,0:T(8,128)(2,1)}, bf16[1024,512]{1,0:T(8,128)(2,1)}, bf16[512,1024]{1,0...) async-done(((bf16[1024,512]{1,0:T(8,128)(2,1)}, bf16[1024,512]{1,0:T(8,128)(2,1)}, bf16[1024,512]{1,0:T(8,128)(2,1)}, ...) | async-done | bytes 12845072 | tf_op jit(solution)/shard_map/psum | solution.py:318
  1006.1 4.9 convert_element_type.220
  (254 shorter events, 172.4 us)
Async XLA Ops:
  7.2 290.7 %copy-start = (bf16[1408,1024]{1,0:T(8,128)(2,1)S(1)}, bf16[1408,1024]{1,0:T(8,128)(2,1)}, u32[]{:S(2)}) copy-start(bf16[1408,1024]{1,0:T(8,128)(2,1)} %param.23) | copy-start | bytes 8650756
  7.2 83.4 %all-gather.3.cloned.1.call-start = ((), (), s32[]{:S(2)}) async-start(), calls=%async_computation.2 | async-start | bytes 8912896 | tf_op jit(solution)/shard_map/all_gather | solution.py:154
  8.9 7.1 copy-start.50
  9.6 6.4 copy-start.46
  12.9 156.8 %all-gather.5.cloned.1.call-start = ((), (), s32[]{:S(2)}) async-start(), calls=%async_computation.3 | async-start | bytes 8912896 | tf_op jit(solution)/shard_map/all_gather | solution.py:153
  17.3 163.6 %copy-start.23 = (bf16[512,8,32]{0,2,1:T(8,128)(2,1)}, bf16[512,8,32]{0,2,1:T(8,128)(2,1)S(1)}, u32[]{:S(2)}) copy-start(bf16[512,8,32]{0,2,1:T(8,128)(2,1)S(1)} %get-tuple-element.110) | copy-start | bytes 786436
  17.3 163.6 %copy-start.25 = (bf16[512,8,32]{0,2,1:T(8,128)(2,1)}, bf16[512,8,32]{0,2,1:T(8,128)(2,1)S(1)}, u32[]{:S(2)}) copy-start(bf16[512,8,32]{0,2,1:T(8,128)(2,1)S(1)} %get-tuple-element.111) | copy-start | bytes 786436
  18.3 271.5 %all-reduce.8.cloned.1.call-start = ((), (), s32[]{:S(2)}) async-start(), calls=%async_computation.4 | async-start | bytes 2097152 | tf_op jit(solution)/shard_map/psum | solution.py:183
  203.7 23.2 %copy-start.20 = (bf16[3072,512]{0,1:T(8,128)(2,1)S(1)}, bf16[3072,512]{0,1:T(8,128)(2,1)}, u32[]{:S(2)}) copy-start(bf16[3072,512]{0,1:T(8,128)(2,1)} %copy.57) | copy-start | bytes 9437188
  226.9 22.8 %copy-start.59 = (bf16[512,1024]{1,0:T(8,128)(2,1)S(1)}, bf16[512,1024]{1,0:T(8,128)(2,1)}, u32[]{:S(2)}) copy-start(bf16[512,1024]{1,0:T(8,128)(2,1)} %param.20) | copy-start | bytes 3145732
  251.4 95.3 %all-reduce.10.cloned.1.call-start = ((), (), s32[]{:S(2)}) async-start(), calls=%async_computation.5 | async-start | bytes 2097152 | tf_op jit(solution)/shard_map/psum | solution.py:211
  251.7 98.5 %copy-start.44 = (f32[1024]{0:T(1024)}, f32[1024]{0:T(1024)S(1)}, u32[]{:S(2)}) copy-start(f32[1024]{0:T(1024)S(1)} %convert_element_type.187) | copy-start | bytes 12292
  291.9 58.3 %copy-start.48 = (f32[512]{0:T(512)}, f32[512]{0:T(512)S(1)}, u32[]{:S(2)}) copy-start(f32[512]{0:T(512)S(1)} %add_rsqrt_fusion) | copy-start | bytes 6148
  306.5 271.1 %reduce-scatter.3.cloned.1.call-start = ((), (), s32[]{:S(2)}) async-start(), calls=%async_computation.6 | async-start | bytes 8912896 | tf_op jit(solution)/shard_map/reduce_scatter | solution.py:286
  378.5 32.9 %copy-start.24 = (bf16[512,8,32]{0,2,1:T(8,128)(2,1)S(1)}, bf16[512,8,32]{0,2,1:T(8,128)(2,1)}, u32[]{:S(2)}) copy-start(bf16[512,8,32]{0,2,1:T(8,128)(2,1)} %copy-done.23) | copy-start | bytes 786436
  378.5 32.9 %copy-start.26 = (bf16[512,8,32]{0,2,1:T(8,128)(2,1)S(1)}, bf16[512,8,32]{0,2,1:T(8,128)(2,1)}, u32[]{:S(2)}) copy-start(bf16[512,8,32]{0,2,1:T(8,128)(2,1)} %copy-done.25) | copy-start | bytes 786436
  453.0 10.2 copy-start.8
  453.1 10.2 copy-start.9
  472.8 213.1 %reduce-scatter.5.cloned.1.call-start = ((), (), s32[]{:S(2)}) async-start(), calls=%async_computation.7 | async-start | bytes 8912896 | tf_op jit(solution)/shard_map/reduce_scatter | solution.py:289
  503.1 252.2 %all-reduce.14.cloned.1.call-start = ((), (), s32[]{:S(2)}) async-start(), calls=%async_computation.9 | async-start | bytes 4194304 | tf_op jit(solution)/shard_map/psum | solution.py:194
  507.4 72.5 %copy-start.41 = (f32[512,32]{0,1:T(8,128)S(1)}, f32[512,32]{0,1:T(8,128)}, u32[]{:S(2)}) copy-start(f32[512,32]{0,1:T(8,128)} %copy-done.40) | copy-start | bytes 196612
  507.4 72.5 %copy-start.43 = (f32[512,32]{0,1:T(8,128)S(1)}, f32[512,32]{0,1:T(8,128)}, u32[]{:S(2)}) copy-start(f32[512,32]{0,1:T(8,128)} %copy-done.42) | copy-start | bytes 196612
  692.3 313.7 %all-reduce.12.cloned.1.call-start = ((), (), s32[]{:S(2)}) async-start(), calls=%async_computation.8 | async-start | bytes 25690112 | tf_op jit(solution)/shard_map/psum | solution.py:318
  712.4 45.4 %copy-start.54 = (bf16[1024]{0:T(1024)(128)(2,1)S(1)}, bf16[1024]{0:T(1024)(128)(2,1)}, u32[]{:S(2)}) copy-start(bf16[1024]{0:T(1024)(128)(2,1)} %get-tuple-element.60) | copy-start | bytes 6148
  (52 other events, 152.3 us)
Sparse Core Ops, SparseCore 0:
  13.0 77.5 all-gather.2
  93.3 76.3 all-gather.4
  251.5 38.2 all-reduce.7
  306.6 40.0 all-reduce.9
  472.9 104.6 reduce-scatter.2
  581.5 104.3 reduce-scatter.4
  692.5 62.8 all-reduce.13
  763.0 243.0 all-reduce.11
where the time goes:
time: 1040 us; the launch traced here: 1030 us
  waiting for transfers between devices  608 us (58%)
  matrix products  184 us (18%)
  other arithmetic  95.9 us (9%)
  local copies, waits for them, and re-layouts  88.9 us (9%)
  blocking collectives  34.7 us (3%)
  between operations  18.5 us (2%)
    psum x1, waiting for transfers between devices, body(): lax.psum(grad_w_query.astype(jnp.bfloat16), 'dp').astype(jnp.float32)  207 us
    reduce_scatter x1, waiting for transfers between devices, body(): lax.psum_scatter(value_terms.astype(jnp.bfloat16), 'dp', scatter_dimensio...  99.8 us
    all_gather x1, waiting for transfers between devices, body(): lax.all_gather(key_rot, 'dp', axis=0, tiled=True)  63.1 us
    all_gather x1, waiting for transfers between devices, body(): lax.all_gather(mixed, 'dp', axis=0, tiled=True)  60.8 us
    reduce_scatter x1, waiting for transfers between devices, body(): lax.psum_scatter(key_terms.astype(jnp.bfloat16), 'dp', scatter_dimension=...  55.8 us
    psum x1, waiting for transfers between devices, body(): lax.psum(jnp.dot(activated, w_down, preferred_element_type=jnp.float32).a...  42.9 us
    psum x1, waiting for transfers between devices, body(): lax.psum(ffn_partial.astype(jnp.bfloat16), 'tensor').astype(jnp.float32)  40.1 us
    psum x1, waiting for transfers between devices, body(): lax.psum(jnp.dot(attended, w_out, preferred_element_type=jnp.float32).ast...  38.1 us
  transfers between devices with their start and end apart: 8, of which 8 were waited for; matrix products, arithmetic and copies ran while one was open for 11% of the time, Pallas kernels for 0%

commit v1 on v0

--- a/solution.py
+++ b/solution.py
@@ -1,6 +1,8 @@
 import jax
 import jax.numpy as jnp
 from jax import lax
+from jax.experimental import pallas as pl
+from jax.experimental.pallas import tpu as pltpu
 from jax.sharding import PartitionSpec as P
 
 HEAD_DIM = 64
@@ -97,7 +99,7 @@
     return jnp.concatenate(parts, axis=1)
 
 
-def body(
+def body_general(
     inputs,
     first_values,
     w_query,
@@ -341,6 +343,664 @@
     )
 
 
+TREE = 16
+TREE_DEPTHS = (0, 1, 2, 3, 4, 4, 4, 4, 5, 5, 5, 5, 5, 5, 5, 5)
+LANES = 128
+wide = jnp.float32
+narrow = jnp.bfloat16
+vmem_bytes = 60 * 1024 * 1024
+
+
+def lane_ids(shape):
+    return lax.broadcasted_iota(jnp.int32, shape, len(shape) - 1)
+
+
+def swap_pairs(left, right):
+    low = lane_ids(left.shape) < HEAD_DIM
+    first = jnp.where(low, left, pltpu.roll(right, HEAD_DIM, 1))
+    second = jnp.where(low, pltpu.roll(left, HEAD_DIM, 1), right)
+    return first, second
+
+
+def spin(values, cosine, signed_sine):
+    half = HEAD_DIM // 2
+    ahead = pltpu.roll(values, LANES - half, 1)
+    behind = pltpu.roll(values, half, 1)
+    other = jnp.where(lane_ids(values.shape) % HEAD_DIM < half, ahead, behind)
+    return values * cosine + other * signed_sine
+
+
+def dot_wide(left, right):
+    return jnp.dot(left, right, preferred_element_type=wide)
+
+
+def dot_rows(left, right):
+    return lax.dot_general(left, right, (((1,), (1,)), ((), ())), preferred_element_type=wide)
+
+
+def whole_spec():
+    return pl.BlockSpec(memory_space=pltpu.VMEM)
+
+
+def scalar_spec():
+    return pl.BlockSpec(memory_space=pltpu.SMEM)
+
+
+def project_kernel(
+    x_ref, gain_ref, first_ref, cos_ref, sin_ref, wq_ref, wk_ref, wv_ref, send_ref, normed_ref
+):
+    rows = x_ref.shape[0]
+    pairs = first_ref.shape[1] // LANES
+    x = x_ref[...].astype(wide)
+    normed = (x * rms_scale(x) * gain_ref[...].astype(wide)).astype(narrow)
+    normed_ref[...] = normed
+    query = dot_wide(normed, wq_ref[...]) * (HEAD_DIM ** (-0.5))
+    key = dot_wide(normed, wk_ref[...])
+    value = dot_wide(normed, wv_ref[...])
+    mixed = 0.5 * value + 0.5 * first_ref[...].astype(wide)
+    cosine = cos_ref[...]
+    sine = sin_ref[...]
+    for pair in range(pairs):
+        cols = slice(pair * LANES, (pair + 1) * LANES)
+        q = spin(query[:, cols], cosine, sine)
+        k = spin(key[:, cols], cosine, sine)
+        for at, tile in enumerate(swap_pairs(k, mixed[:, cols])):
+            send_ref[2 * pair + at, 0, :rows, :] = tile.astype(narrow)
+        for at, tile in enumerate(swap_pairs(q[: rows // 2], q[rows // 2 :])):
+            send_ref[2 * pair + at, 0, rows:, :] = tile.astype(narrow)
+
+
+def project(inputs, norm_attn, first_values, cosine, sine, w_query, w_key, w_value, groups):
+    rows, width = inputs.shape
+    local = w_query.shape[1]
+    part = rows // groups
+    heads = local // HEAD_DIM
+    fixed = lambda step: (0, 0)
+    moving = lambda step: (step, 0)
+    return pl.pallas_call(
+        project_kernel,
+        grid=(groups,),
+        in_specs=[
+            pl.BlockSpec((part, width), moving),
+            pl.BlockSpec((1, width), fixed),
+            pl.BlockSpec((part, local), moving),
+            pl.BlockSpec((part, LANES), moving),
+            pl.BlockSpec((part, LANES), moving),
+            pl.BlockSpec((width, local), fixed),
+            pl.BlockSpec((width, local), fixed),
+            pl.BlockSpec((width, local), fixed),
+        ],
+        out_specs=[
+            pl.BlockSpec((heads, 1, part + part // 2, LANES), lambda step: (0, step, 0, 0)),
+            pl.BlockSpec((part, width), moving),
+        ],
+        out_shape=[
+            jax.ShapeDtypeStruct((heads, groups, part + part // 2, LANES), narrow),
+            jax.ShapeDtypeStruct((rows, width), narrow),
+        ],
+        compiler_params=pltpu.CompilerParams(vmem_limit_bytes=vmem_bytes),
+        name="project",
+    )(inputs, norm_attn.reshape(1, width), first_values, cosine, sine, w_query, w_key, w_value)
+
+
+def tree_walk(run, count):
+    for base in range(0, count, TREE):
+        at = 0
+        while at < TREE:
+            same = 1
+            while at + same < TREE and TREE_DEPTHS[at + same] == TREE_DEPTHS[at]:
+                same += 1
+            depth = TREE_DEPTHS[at]
+            if same == 1:
+                run(base + at, depth)
+            else:
+                def step(i, carry, start=base + at, depth=depth):
+                    run(start + i, depth)
+                    return carry
+
+                lax.fori_loop(0, same, step, 0)
+            at += same
+
+
+def path_of(parents_ref, assign_ref, segment, depth):
+    slots = [assign_ref[segment]]
+    current = segment
+    for _ in range(depth):
+        current = parents_ref[current]
+        slots.append(assign_ref[current])
+    return slots
+
+
+def unpack_low(packed):
+    values = packed.astype(wide)
+    low = lane_ids(values.shape) < HEAD_DIM
+    top = jnp.where(low, values, 0.0)
+    bottom = jnp.where(low, pltpu.roll(values, HEAD_DIM, 1), 0.0)
+    return jnp.concatenate([top, bottom], axis=0).astype(narrow)
+
+
+def unpack_high(packed):
+    values = packed.astype(wide)
+    high = lane_ids(values.shape) >= HEAD_DIM
+    top = jnp.where(high, pltpu.roll(values, HEAD_DIM, 1), 0.0)
+    bottom = jnp.where(high, values, 0.0)
+    return jnp.concatenate([top, bottom], axis=0).astype(narrow)
+
+
+def pack_columns(transposed):
+    half = transposed.shape[1] // 2
+    stacked = jnp.concatenate([transposed[:, :half], transposed[:, half:]], axis=0)
+    return jnp.transpose(stacked)
+
+
+def gather_parts(part, recv_ref, other_ref, kv_ref, kvt_ref, lanes):
+    rows = other_ref.shape[1]
+
+    def fill(slot, carry):
+        kv_ref[slot, pl.ds(pl.multiple_of(part * rows, rows), rows), :] = recv_ref[slot, :rows, :]
+        kv_ref[slot, pl.ds(pl.multiple_of((1 - part) * rows, rows), rows), :] = other_ref[slot]
+        flipped = jnp.transpose(kv_ref[slot].astype(wide))
+        kvt_ref[slot] = flipped[lanes].astype(narrow)
+        return carry
+
+    lax.fori_loop(0, recv_ref.shape[0], fill, 0)
+
+
+def visible(part, keys, rows):
+    key_row = lax.broadcasted_iota(jnp.int32, (keys, rows), 0)
+    query_row = lax.broadcasted_iota(jnp.int32, (keys, rows), 1) + part * rows
+    return key_row <= query_row
+
+
+def attend_kernel(
+    parents_ref, assign_ref, part_ref, recv_ref, other_ref, send_ref, ot_ref, log_ref, kv_ref, vt_ref
+):
+    part = part_ref[0]
+    rows = other_ref.shape[1]
+    gather_parts(part, recv_ref, other_ref, kv_ref, vt_ref, slice(HEAD_DIM, LANES))
+
+    def run(segment, depth):
+        slots = path_of(parents_ref, assign_ref, segment, depth)
+        own = slots[0]
+        query = unpack_low(recv_ref[own, rows:, :])
+        scores = []
+        for level, slot in enumerate(slots):
+            block = dot_rows(kv_ref[slot], query)
+            if level == 0:
+                block = jnp.where(visible(part, SEG, rows), block, masked_score)
+            scores.append(block)
+        peak = jnp.max(scores[0], axis=0, keepdims=True)
+        for block in scores[1:]:
+            peak = jnp.maximum(peak, jnp.max(block, axis=0, keepdims=True))
+        total = jnp.zeros_like(peak)
+        mixed = jnp.zeros((HEAD_DIM, rows), wide)
+        for block, slot in zip(scores, slots, strict=True):
+            weight = jnp.exp(block - peak)
+            total = total + jnp.sum(weight, axis=0, keepdims=True)
+            mixed = mixed + dot_wide(vt_ref[slot], weight.astype(narrow))
+        mixed = mixed / total
+        ot_ref[own] = mixed
+        log_ref[own] = jnp.broadcast_to(peak + jnp.log(total), (8, rows))
+        send_ref[own] = pack_columns(mixed).astype(narrow)
+
+    tree_walk(run, recv_ref.shape[0])
+
+
+def attend(parents, assignment, part, recv, other):
+    count, rows, _ = other.shape
+    return pl.pallas_call(
+        attend_kernel,
+        in_specs=[scalar_spec()] * 3 + [whole_spec()] * 2,
+        out_specs=[whole_spec()] * 3,
+        out_shape=[
+            jax.ShapeDtypeStruct((count, rows // 2, LANES), narrow),
+            jax.ShapeDtypeStruct((count, HEAD_DIM, rows), wide),
+            jax.ShapeDtypeStruct((count, 8, rows), wide),
+        ],
+        scratch_shapes=[
+            pltpu.VMEM((count, SEG, LANES), narrow),
+            pltpu.VMEM((count, HEAD_DIM, SEG), narrow),
+        ],
+        compiler_params=pltpu.CompilerParams(vmem_limit_bytes=vmem_bytes),
+        name="attend",
+    )(parents, assignment, part, recv, other)
+
+
+def attend_back_kernel(
+    parents_ref,
+    assign_ref,
+    part_ref,
+    recv_ref,
+    other_ref,
+    grad_ref,
+    ot_ref,
+    log_ref,
+    dq_ref,
+    mine_ref,
+    theirs_ref,
+    kv_ref,
+    kt_ref,
+    sum_ref,
+):
+    part = part_ref[0]
+    rows = other_ref.shape[1]
+    count = recv_ref.shape[0]
+    gather_parts(part, recv_ref, other_ref, kv_ref, kt_ref, slice(0, HEAD_DIM))
+
+    def clear(slot, carry):
+        sum_ref[slot] = jnp.zeros((SEG, LANES), wide)
+        return carry
+
+    lax.fori_loop(0, count, clear, 0)
+
+    def run(segment, depth):
+        slots = path_of(parents_ref, assign_ref, segment, depth)
+        own = slots[0]
+        query = unpack_low(recv_ref[own, rows:, :])
+        packed = grad_ref[own]
+        grad = unpack_high(packed)
+        flipped = jnp.transpose(packed.astype(wide))
+        grad_t = jnp.concatenate([flipped[:HEAD_DIM], flipped[HEAD_DIM:]], axis=1)
+        delta = jnp.sum(grad_t * ot_ref[own], axis=0, keepdims=True)
+        log_row = log_ref[own][:1]
+        grad_query = jnp.zeros((HEAD_DIM, rows), wide)
+        for level, slot in enumerate(slots):
+            pair = kv_ref[slot]
+            probs = jnp.exp(dot_rows(pair, query) - log_row)
+            if level == 0:
+                probs = jnp.where(visible(part, SEG, rows), probs, 0.0)
+            grad_probs = dot_rows(pair, grad)
+            grad_scores = (probs * (grad_probs - delta)).astype(narrow)
+            sum_ref[slot] += dot_wide(grad_scores, query) + dot_wide(probs.astype(narrow), grad)
+            grad_query = grad_query + dot_wide(kt_ref[slot], grad_scores)
+        dq_ref[own] = pack_columns(grad_query * (HEAD_DIM ** (-0.5))).astype(narrow)
+
+    tree_walk(run, count)
+
+    def finish(slot, carry):
+        mine_ref[slot] = sum_ref[slot, pl.ds(pl.multiple_of(part * rows, rows), rows), :]
+        theirs = sum_ref[slot, pl.ds(pl.multiple_of((1 - part) * rows, rows), rows), :]
+        theirs_ref[slot] = theirs.astype(narrow)
+        return carry
+
+    lax.fori_loop(0, count, finish, 0)
+
+
+def attend_back(parents, assignment, part, recv, other, grad, ot, logs):
+    count, rows, _ = other.shape
+    return pl.pallas_call(
+        attend_back_kernel,
+        in_specs=[scalar_spec()] * 3 + [whole_spec()] * 5,
+        out_specs=[whole_spec()] * 3,
+        out_shape=[
+            jax.ShapeDtypeStruct((count, rows // 2, LANES), narrow),
+            jax.ShapeDtypeStruct((count, rows, LANES), wide),
+            jax.ShapeDtypeStruct((count, rows, LANES), narrow),
+        ],
+        scratch_shapes=[
+            pltpu.VMEM((count, SEG, LANES), narrow),
+            pltpu.VMEM((count, HEAD_DIM, SEG), narrow),
+            pltpu.VMEM((count, SEG, LANES), wide),
+        ],
+        compiler_params=pltpu.CompilerParams(vmem_limit_bytes=vmem_bytes),
+        name="attend_back",
+    )(parents, assignment, part, recv, other, grad, ot, logs)
+
+
+def heads_to_rows(recv_ref, groups):
+    half = recv_ref.shape[1]
+    heads = recv_ref.shape[0] // groups
+    strips = []
+    for pair in range(heads // 2):
+        pieces = []
+        for part in range(groups):
+            left = recv_ref[2 * pair * groups + part].astype(wide)
+            right = recv_ref[(2 * pair + 1) * groups + part].astype(wide)
+            pieces += list(swap_pairs(left, right))
+        strips.append(jnp.concatenate(pieces, axis=0))
+    return jnp.concatenate(strips, axis=1).astype(narrow)
+
+
+def merge_kernel(
+    own_ref, other_ref, w_own_ref, w_other_ref, x_ref, gain_ref, attended_ref, hidden_ref, normed_ref
+):
+    groups = 2
+    mine = heads_to_rows(own_ref, groups)
+    attended_ref[...] = mine
+    theirs = heads_to_rows(other_ref, groups)
+    branch = dot_wide(mine, w_own_ref[...]).astype(narrow).astype(wide)
+    branch = branch + dot_wide(theirs, w_other_ref[...]).astype(narrow).astype(wide)
+    hidden = x_ref[...].astype(wide) + branch
+    hidden_ref[...] = hidden
+    normed_ref[...] = (hidden * rms_scale(hidden) * gain_ref[...].astype(wide)).astype(narrow)
+
+
+def merge(own, other, w_own, w_other, inputs, norm_ffn):
+    tokens, width = inputs.shape
+    local = w_own.shape[0]
+    return pl.pallas_call(
+        merge_kernel,
+        in_specs=[whole_spec()] * 6,
+        out_specs=[whole_spec()] * 3,
+        out_shape=[
+            jax.ShapeDtypeStruct((tokens, local), narrow),
+            jax.ShapeDtypeStruct((tokens, width), wide),
+            jax.ShapeDtypeStruct((tokens, width), narrow),
+        ],
+        compiler_params=pltpu.CompilerParams(vmem_limit_bytes=vmem_bytes),
+        name="merge",
+    )(own, other, w_own, w_other, inputs, norm_ffn.reshape(1, width))
+
+
+def branch_back_kernel(
+    own_ref, other_ref, hidden_ref, cot_ref, gain_ref, w_ref, send_ref, hidden_grad_ref, branch_ref, gain_grad_ref
+):
+    groups = 2
+    grad_normed = own_ref[...].astype(wide) + other_ref[...].astype(wide)
+    hidden = hidden_ref[...]
+    back, gain_grad = norm_back(grad_normed, hidden, rms_scale(hidden), gain_ref[...].astype(wide))
+    gain_grad_ref[...] = gain_grad[None]
+    grad_hidden = cot_ref[...].astype(wide) + back
+    hidden_grad_ref[...] = grad_hidden
+    grad_branch = grad_hidden.astype(narrow)
+    branch_ref[...] = grad_branch
+    attended_grad = dot_rows(grad_branch, w_ref[...])
+    tokens, local = attended_grad.shape
+    half = tokens // groups // 2
+    for pair in range(local // LANES):
+        for part in range(groups):
+            cols = slice(pair * LANES, (pair + 1) * LANES)
+            low = attended_grad[2 * part * half : (2 * part + 1) * half, cols]
+            high = attended_grad[(2 * part + 1) * half : (2 * part + 2) * half, cols]
+            for at, tile in enumerate(swap_pairs(low, high)):
+                send_ref[2 * pair + at, part] = tile.astype(narrow)
+
+
+def branch_back(own, other, hidden, cotangent, norm_ffn, w_out):
+    tokens, width = hidden.shape
+    local = w_out.shape[0]
+    groups = 2
+    return pl.pallas_call(
+        branch_back_kernel,
+        in_specs=[whole_spec()] * 6,
+        out_specs=[whole_spec()] * 4,
+        out_shape=[
+            jax.ShapeDtypeStruct((local // HEAD_DIM, groups, tokens // groups // 2, LANES), narrow),
+            jax.ShapeDtypeStruct((tokens, width), wide),
+            jax.ShapeDtypeStruct((tokens, width), narrow),
+            jax.ShapeDtypeStruct((1, width), wide),
+        ],
+        compiler_params=pltpu.CompilerParams(vmem_limit_bytes=vmem_bytes),
+        name="branch_back",
+    )(own, other, hidden, cotangent, norm_ffn.reshape(1, width), w_out)
+
+
+def unproject_kernel(
+    recv_ref, cos_ref, sin_ref, wq_ref, wk_ref, wv_ref, gq_ref, gk_ref, gv_ref, first_ref, part_ref
+):
+    groups = 2
+    rows = recv_ref.shape[1] * 2 // 3
+    half = rows // 2
+    heads = recv_ref.shape[0] // groups
+    for part in range(groups):
+        span = slice(part * rows, (part + 1) * rows)
+        cosine = cos_ref[span, :]
+        sine = -sin_ref[span, :]
+        for pair in range(heads // 2):
+            cols = slice(pair * LANES, (pair + 1) * LANES)
+            left = recv_ref[2 * pair * groups + part].astype(wide)
+            right = recv_ref[(2 * pair + 1) * groups + part].astype(wide)
+            key, value = swap_pairs(left[:rows], right[:rows])
+            query = jnp.concatenate(swap_pairs(left[rows:], right[rows:]), axis=0)
+            gq_ref[span, cols] = spin(query, cosine, sine).astype(narrow)
+            gk_ref[span, cols] = spin(key, cosine, sine).astype(narrow)
+            value = 0.5 * value
+            first_ref[span, cols] = value
+            gv_ref[span, cols] = value.astype(narrow)
+    total = dot_rows(gq_ref[...], wq_ref[...])
+    total = total + dot_rows(gk_ref[...], wk_ref[...])
+    total = total + dot_rows(gv_ref[...], wv_ref[...])
+    part_ref[...] = total.astype(narrow)
+
+
+def unproject(recv, cosine, sine, w_query, w_key, w_value):
+    width, local = w_query.shape
+    tokens = cosine.shape[0]
+    return pl.pallas_call(
+        unproject_kernel,
+        in_specs=[whole_spec()] * 6,
+        out_specs=[whole_spec()] * 5,
+        out_shape=[jax.ShapeDtypeStruct((tokens, local), narrow)] * 3
+        + [
+            jax.ShapeDtypeStruct((tokens, local), wide),
+            jax.ShapeDtypeStruct((tokens, width), narrow),
+        ],
+        compiler_params=pltpu.CompilerParams(vmem_limit_bytes=vmem_bytes),
+        name="unproject",
+    )(recv, cosine, sine, w_query, w_key, w_value)
+
+
+def swap_tensor(values):
+    return lax.ppermute(values, "tensor", [(0, 1), (1, 0)])
+
+
+def swap_bit(values, bit, count):
+    return lax.ppermute(values, "dp", [(i, i ^ bit) for i in range(count)])
+
+
+def add_narrow(left, right):
+    return (left.astype(wide) + right.astype(wide)).astype(narrow)
+
+
+def take_part(values, index, parts):
+    size = values.shape[0] // parts
+    return lax.dynamic_slice_in_dim(values, index * size, size, 0)
+
+
+def reduce_bit(values, bit, place, count):
+    mine = (place // bit) % 2
+    arrived = swap_bit(take_part(values, 1 - mine, 2), bit, count)
+    return add_narrow(take_part(values, mine, 2), arrived)
+
+
+def gather_bit(values, bit, place, count):
+    mine = (place // bit) % 2
+    arrived = swap_bit(values, bit, count)
+    row = jnp.concatenate([arrived, values, arrived], axis=0)
+    size = values.shape[0]
+    return lax.dynamic_slice_in_dim(row, (1 - mine) * size, 2 * size, 0)
+
+
+def line_pairs(line, stride, count, up, keep):
+    pairs = []
+    for device in range(count):
+        at = device // stride
+        if up and at + 1 < line and keep(at):
+            pairs.append((device, device + stride))
+        if not up and at >= 1 and keep(line - 1 - at):
+            pairs.append((device, device - stride))
+    return pairs
+
+
+def reduce_line(values, stride, place, count):
+    line = count // stride
+    at = place // stride
+    up = down = None
+    for step in range(1, line):
+        share_up = take_part(values, jnp.clip(line - step + at, 0, line - 1), line)
+        share_down = take_part(values, jnp.clip(step - line + at, 0, line - 1), line)
+        if up is not None:
+            share_up = add_narrow(share_up, up)
+            share_down = add_narrow(share_down, down)
+        keep = lambda index, step=step: index <= step - 1
+        up = lax.ppermute(share_up, "dp", line_pairs(line, stride, count, True, keep))
+        down = lax.ppermute(share_down, "dp", line_pairs(line, stride, count, False, keep))
+    own = take_part(values, at, line).astype(wide)
+    return (own + up.astype(wide) + down.astype(wide)).astype(narrow)
+
+
+def gather_line(values, stride, place, count):
+    line = count // stride
+    at = place // stride
+    below, above = [], []
+    up = down = values
+    for step in range(1, line):
+        keep_up = lambda index, step=step: index >= step - 1
+        up = lax.ppermute(up, "dp", line_pairs(line, stride, count, True, keep_up))
+        down = lax.ppermute(down, "dp", line_pairs(line, stride, count, False, keep_up))
+        below.append(up)
+        above.append(down)
+    row = jnp.concatenate(below[::-1] + [values] + above, axis=0)
+    size = values.shape[0]
+    return lax.dynamic_slice_in_dim(row, (line - 1 - at) * size, line * size, 0)
+
+
+def sum_over_dp(values, place, count):
+    values = reduce_bit(values, 1, place, count)
+    values = reduce_bit(values, 2, place, count)
+    values = reduce_line(values, 4, place, count)
+    values = gather_line(values, 4, place, count)
+    values = gather_bit(values, 2, place, count)
+    return gather_bit(values, 1, place, count).astype(wide)
+
+
+def sum_small(values, count):
+    bit = 1
+    while bit < count:
+        values = values + swap_bit(values, bit, count)
+        bit *= 2
+    return values
+
+
+def body_heads(
+    inputs,
+    first_values,
+    w_query,
+    w_key,
+    w_value,
+    w_out,
+    w_gate,
+    w_up,
+    w_down,
+    norm_attn,
+    norm_ffn,
+    cotangent,
+    parents,
+    depth_pos,
+    assignment,
+):
+    count = parents.shape[0]
+    tokens, width = inputs.shape
+    local = w_query.shape[1]
+    heads = local // HEAD_DIM
+    groups = count // heads
+    place = lax.axis_index("dp")
+    part = (place % groups).astype(jnp.int32)
+    part_array = part.reshape(1)
+
+    w_out_other = swap_tensor(w_out)
+    slot_ids = jnp.arange(count, dtype=jnp.int32)
+    start = jnp.sum(jnp.where(slot_ids == place, depth_pos, 0))
+    positions = (start + jnp.arange(tokens, dtype=jnp.int32)).astype(wide)
+    half = HEAD_DIM // 2
+    lanes = jnp.arange(LANES, dtype=jnp.int32)
+    frequency = rope_base ** (-(lanes % half).astype(wide) * 2.0 / HEAD_DIM)
+    angles = positions[:, None] * frequency[None, :]
+    cosine = jnp.cos(angles)
+    sine = jnp.sin(angles) * jnp.where(lanes % HEAD_DIM < half, -1.0, 1.0)[None, :]
+
+    send, normed = project(
+        inputs, norm_attn, first_values, cosine, sine, w_query, w_key, w_value, groups
+    )
+    rows = tokens // groups
+    send = send.reshape(count, rows + rows // 2, LANES)
+    recv = lax.all_to_all(send, "dp", split_axis=0, concat_axis=0, tiled=True)
+    other = swap_bit(recv[:, :rows], 1, count)
+    packed, ot, logs = attend(parents, assignment, part_array, recv, other)
+    own_out = lax.all_to_all(packed, "dp", split_axis=0, concat_axis=0, tiled=True)
+    other_out = swap_tensor(own_out)
+    attended, hidden, normed_ffn = merge(own_out, other_out, w_out, w_out_other, inputs, norm_ffn)
+
+    gate_proj = jnp.dot(normed_ffn, w_gate, preferred_element_type=wide)
+    up_proj = jnp.dot(normed_ffn, w_up, preferred_element_type=wide)
+    silu_gate = jax.nn.silu(gate_proj)
+    activated = (silu_gate * up_proj).astype(narrow)
+    grad_activated = jnp.einsum("td,fd->tf", cotangent, w_down, preferred_element_type=wide)
+    sigmoid_gate = jax.nn.sigmoid(gate_proj)
+    grad_gate = (
+        grad_activated * up_proj * sigmoid_gate * (1.0 + gate_proj * (1.0 - sigmoid_gate))
+    ).astype(narrow)
+    grad_up = (grad_activated * silu_gate).astype(narrow)
+    ffn_partial = (
+        jnp.einsum("tf,df->td", grad_gate, w_gate, preferred_element_type=wide)
+        + jnp.einsum("tf,df->td", grad_up, w_up, preferred_element_type=wide)
+    ).astype(narrow)
+    ffn_other = swap_tensor(ffn_partial)
+    grad_w_gate = jnp.einsum("td,tf->df", normed_ffn, grad_gate, preferred_element_type=wide)
+    grad_w_up = jnp.einsum("td,tf->df", normed_ffn, grad_up, preferred_element_type=wide)
+    grad_w_down = jnp.einsum("tf,td->fd", activated, cotangent, preferred_element_type=wide)
+    grad_w_gate, grad_w_up, grad_w_down = lax.psum(
+        (grad_w_gate.astype(narrow), grad_w_up.astype(narrow), grad_w_down.astype(narrow)), "dp"
+    )
+    feed_partial = jnp.dot(activated, w_down, preferred_element_type=wide).astype(narrow)
+
+    grad_send, grad_hidden, grad_branch, grad_gain_ffn = branch_back(
+        ffn_partial, ffn_other, hidden, cotangent, norm_ffn, w_out
+    )
+    grad_recv = lax.all_to_all(
+        grad_send.reshape(count, rows // 2, LANES), "dp", split_axis=0, concat_axis=0, tiled=True
+    )
+    feed_other = swap_tensor(feed_partial)
+    feed = feed_partial.astype(wide) + feed_other.astype(wide)
+    output = (hidden + feed).astype(narrow)
+    grad_w_out = jnp.einsum("tc,td->cd", attended, grad_branch, preferred_element_type=wide)
+
+    grad_q, mine, theirs = attend_back(
+        parents, assignment, part_array, recv, other, grad_recv, ot, logs
+    )
+    arrived = swap_bit(theirs, 1, count)
+    back_send = jnp.concatenate([(mine + arrived.astype(wide)).astype(narrow), grad_q], axis=1)
+    back_recv = lax.all_to_all(back_send, "dp", split_axis=0, concat_axis=0, tiled=True)
+    grad_query, grad_key, grad_value, grad_first, attn_partial = unproject(
+        back_recv, cosine, sine, w_query, w_key, w_value
+    )
+    attn_other = swap_tensor(attn_partial)
+    grad_w_query = jnp.einsum("td,tc->dc", normed, grad_query, preferred_element_type=wide)
+    grad_w_key = jnp.einsum("td,tc->dc", normed, grad_key, preferred_element_type=wide)
+    grad_w_value = jnp.einsum("td,tc->dc", normed, grad_value, preferred_element_type=wide)
+    sums = [
+        sum_over_dp(term.astype(narrow), place, count)
+        for term in (grad_w_query, grad_w_key, grad_w_value, grad_w_out)
+    ]
+    inputs_wide = inputs.astype(wide)
+    grad_normed = attn_partial.astype(wide) + attn_other.astype(wide)
+    grad_input_norm, grad_gain_attn = norm_back(
+        grad_normed, inputs_wide, rms_scale(inputs_wide), norm_attn.astype(wide)
+    )
+    grad_inputs = grad_hidden + grad_input_norm
+    gains = sum_small(jnp.stack([grad_gain_attn, grad_gain_ffn[0]]), count)
+    return (
+        output,
+        grad_inputs,
+        grad_first,
+        sums[0],
+        sums[1],
+        sums[2],
+        sums[3],
+        grad_w_gate.astype(wide),
+        grad_w_up.astype(wide),
+        grad_w_down.astype(wide),
+        gains[0],
+        gains[1],
+    )
+
+
+def pick_body(mesh):
+    if mesh.shape["dp"] == 16 and mesh.shape["tensor"] == 2:
+        return body_heads
+    return body_general
+
+
 def solution(mesh):
     placed = (
         P("dp", None),
@@ -360,7 +1020,7 @@
         P(),
     )
     return jax.shard_map(
-        body,
+        pick_body(mesh),
         mesh=mesh,
         in_specs=placed,
         out_specs=(

time: 1040 us -> 647 us (0.62)
  waiting for transfers between devices: 608 us -> 238 us
  starting transfers between devices: 0.54 us -> 160 us
  matrix products: 184 us -> 38.9 us
  Pallas kernels: 0 us -> 90.9 us
  local copies, waits for them, and re-layouts: 88.9 us -> 9.25 us
  other arithmetic: 95.9 us -> 42.5 us
    psum x4 -> x1, waiting for transfers between devices: 329 us -> 85.9 us  [body_heads(): lax.psum((grad_w_gate.astype(narrow), grad_w_up.astype(narrow), grad_w_do...]
    reduce_scatter x2 -> x0, waiting for transfers between devices: 156 us -> none  [the longest x1 99.8 us: body(): lax.psum_scatter(value_terms.astype(jnp.bfloat16), 'dp', scatter_dimensio...]
    dot_general x27 -> x13, matrix products: 184 us -> 38.9 us  [the longest x1 5.54 us: body_heads(): jnp.einsum('td,fd->tf', cotangent, w_down, preferred_element_type=wide)]
    ppermute x0 -> x75, starting transfers between devices: none -> 145 us  [the longest x12 42.8 us: gather_line(): up = lax.ppermute(up, 'dp', line_pairs(line, stride, count, True, keep_up))]
    ppermute x0 -> x75, waiting for transfers between devices: none -> 137 us  [the longest x12 43.3 us: reduce_line(): lax.ppermute(share_down, 'dp', line_pairs(line, stride, count, False, keep))]
    all_gather x2 -> x0, waiting for transfers between devices: 124 us -> none  [the longest x1 63.1 us: body(): lax.all_gather(key_rot, 'dp', axis=0, tiled=True)]
    pallas_call x0 -> x6, Pallas kernels: none -> 90.9 us  [the longest x1 36.8 us: attend_back(): pl.pallas_call(attend_back_kernel, in_specs=[scalar_spec()] * 3 + [whole_...]
    all_to_all x0 -> x1, blocking collectives: none -> 43.5 us  [body_heads(): recv = lax.all_to_all(send, 'dp', split_axis=0, concat_axis=0, tiled=True)]
  transfers between devices with their start and end apart: 8 -> 79, of which waited for: 8 -> 29; matrix products, arithmetic and copies ran while one was open for 11% -> 10% of each run, Pallas kernels for 0% -> 6%
where the time goes in v1:
time: 647 us; the launch traced here: 639 us
  waiting for transfers between devices  238 us (37%)
  starting transfers between devices  160 us (25%)
  Pallas kernels  90.9 us (14%)
  blocking collectives  43.5 us (7%)
  other arithmetic  42.5 us (7%)
  matrix products  38.9 us (6%)
  between operations  15.9 us (2%)
  local copies, waits for them, and re-layouts  9.25 us (1%)
    psum x1, waiting for transfers between devices, body_heads(): lax.psum((grad_w_gate.astype(narrow), grad_w_up.astype(narrow), grad_w_do...  85.9 us
    all_to_all x1, blocking collectives, body_heads(): recv = lax.all_to_all(send, 'dp', split_axis=0, concat_axis=0, tiled=True)  43.5 us
    ppermute x12, waiting for transfers between devices, reduce_line(): lax.ppermute(share_down, 'dp', line_pairs(line, stride, count, False, keep))  43.3 us
    ppermute x12, starting transfers between devices, gather_line(): up = lax.ppermute(up, 'dp', line_pairs(line, stride, count, True, keep_up))  42.8 us
    ppermute x12, starting transfers between devices, reduce_line(): lax.ppermute(share_up, 'dp', line_pairs(line, stride, count, True, keep))  42.8 us
    ppermute x5, waiting for transfers between devices, swap_tensor(): return lax.ppermute(values, 'tensor', [(0, 1), (1, 0)])  40.2 us
    pallas_call x1, Pallas kernels, attend_back(): pl.pallas_call(attend_back_kernel, in_specs=[scalar_spec()] * 3 + [whole_...  36.8 us
    pallas_call x1, Pallas kernels, attend(): pl.pallas_call(attend_kernel, in_specs=[scalar_spec()] * 3 + [whole_spec(...  30 us
  transfers between devices with their start and end apart: 79, of which 29 were waited for; matrix products, arithmetic and copies ran while one was open for 10% of the time, Pallas kernels for 6%

profile of v1, /device:TPU:0, one launch (start us, length us, event | category | flops | bytes accessed | tf_op | source)
XLA Modules:
  0.0 638.6 jit_solution(6729432723257163588)
XLA Ops:
  12.4 6.2 project.1
  18.6 43.5 %all_to_all.20.recv_ref = bf16[16,384,128]{2,1,0:T(8,128)(2,1)S(1)} all-to-all(bf16[16,384,128]{2,1,0:T(8,128)(2,1)} %bitcast.32), channel_id=1, replica_groups=mesh['dp'=16,'tensor'=2] {'dp'}, dimensions={0} | all-to-all | bytes 3145728 | tf_op jit(solution)/shard_map/all_to_all | solution.py:917
  67.7 30.0 %attend.1 = (bf16[16,128,128]{2,1,0:T(8,128)(2,1)}, f32[16,64,256]{2,1,0:T(8,128)}, f32[16,8,256]{2,1,0:T(8,128)}) custom-call(s32[16]{0:T(128)} %parents_ref.3, s32[16]{0:T(128)} %assign_ref.3, s32[1]{0:T(128)} %bitcast.part_ref, bf16[16,384,128]{2,1,0:T(8,128)(2,1)} %copy-done.3, bf16[16,256,128]{2,1,0:T(8,128)(2,1)} %collective-permute-done.other_ref), custom_call_target="tpu_custom_call" | custom-call | tf_op jit(solution)/shard_map/attend/pallas_call | solution.py:551
  97.7 4.8 all-to-all-start.1
  104.1 12.9 %all-to-all-done.1.own_ref = bf16[16,128,128]{2,1,0:T(8,128)(2,1)S(1)} async-done(((bf16[16,128,128]{2,1,0:T(8,128)(2,1)}), bf16[16,128,128]{2,1,0:T(8,128)(2,1)S(1)}, u32[]{:S(2)}, u32[]{:S(2)}) %all-to-all-start.1) | async-done | bytes 524320 | tf_op jit(solution)/shard_map/all_to_all | solution.py:920
  119.1 5.5 fusion.40
  128.9 10.7 %collective-permute-done.1.other_ref = bf16[16,128,128]{2,1,0:T(8,128)(2,1)S(1)} collective-permute-done((bf16[16,128,128]{2,1,0:T(8,128)(2,1)S(1)}, bf16[16,128,128]{2,1,0:T(8,128)(2,1)S(1)}, u32[]{:S(2)}, u32[]{:S(2)}) %collective-permute-start.1) | collective-permute-done | bytes 524320 | tf_op jit(solution)/shard_map/ppermute | solution.py:784
  140.4 5.6 merge.1
  160.4 23.3 %collective-permute-done.4.other_ref = bf16[512,1024]{1,0:T(8,128)(2,1)S(1)} collective-permute-done((bf16[512,1024]{1,0:T(8,128)(2,1)S(1)}, bf16[512,1024]{1,0:T(8,128)(2,1)S(1)}, u32[]{:S(2)}, u32[]{:S(2)}) %collective-permute-start.4) | collective-permute-done | bytes 1048608 | tf_op jit(solution)/shard_map/ppermute | solution.py:784
  184.6 6.2 branch_back.1
  190.8 5.4 all-to-all-start.2
  211.4 36.8 %attend_back.1 = (bf16[16,128,128]{2,1,0:T(8,128)(2,1)}, f32[16,256,128]{2,1,0:T(8,128)}, bf16[16,256,128]{2,1,0:T(8,128)(2,1)}) custom-call(s32[16]{0:T(128)} %parents_ref.3, s32[16]{0:T(128)} %assign_ref.3, s32[1]{0:T(128)} %bitcast.part_ref, bf16[16,384,128]{2,1,0:T(8,128)(2,1)} %copy-done.3, bf16[16,256,128]{2,1,0:T(8,128)(2,1)} %collective-permute-done.other_ref, ...), custom_call_target="tpu_custom_call" | custom-call | tf_op jit(solution)/shard_map/attend_back/pallas_call | solution.py:631
  281.3 35.2 %collective-permute-done.62 = bf16[32,1024]{1,0:T(8,128)(2,1)S(1)} collective-permute-done((bf16[32,1024]{1,0:T(8,128)(2,1)S(1)}, bf16[32,1024]{1,0:T(8,128)(2,1)S(1)}, u32[]{:S(2)}, u32[]{:S(2)}) %collective-permute-start.62) | collective-permute-done | bytes 65568 | tf_op jit(solution)/shard_map/ppermute | solution.py:837
  316.6 23.6 %collective-permute-start.63 = (bf16[32,1024]{1,0:T(8,128)(2,1)S(1)}, bf16[32,1024]{1,0:T(8,128)(2,1)S(1)}, u32[]{:S(2)}, u32[]{:S(2)}) collective-permute-start(bf16[32,1024]{1,0:T(8,128)(2,1)S(1)} %add_convert_fusion.11), channel_id=1, source_target_pairs={{0,8},{2,10},{4,12},{6,14},{8,16},{10,18},{12,20},{14,22},{16,24},... | collective-permute-start | bytes 196616 | tf_op jit(solution)/shard_map/ppermute | solution.py:849
  357.0 8.9 %collective-permute-done.68 = bf16[32,1024]{1,0:T(8,128)(2,1)S(1)} collective-permute-done((bf16[32,1024]{1,0:T(8,128)(2,1)S(1)}, bf16[32,1024]{1,0:T(8,128)(2,1)S(1)}, u32[]{:S(2)}, u32[]{:S(2)}) %collective-permute-start.68) | collective-permute-done | bytes 65568 | tf_op jit(solution)/shard_map/ppermute | solution.py:850
  367.9 7.1 %collective-permute-done.69 = bf16[128,1024]{1,0:T(8,128)(2,1)} collective-permute-done((bf16[128,1024]{1,0:T(8,128)(2,1)S(1)}, bf16[128,1024]{1,0:T(8,128)(2,1)}, u32[]{:S(2)}, u32[]{:S(2)}) %collective-permute-start.69) | collective-permute-done | bytes 262176 | tf_op jit(solution)/shard_map/ppermute | solution.py:788
  384.2 85.9 %all-reduce.3.cloned.1.call-done = (bf16[1024,1408]{1,0:T(8,128)(2,1)}, bf16[1024,1408]{1,0:T(8,128)(2,1)}, bf16[1408,1024]{1,0:T(8,128)(2,1)}) async-done(((bf16[1024,1408]{1,0:T(8,128)(2,1)}, bf16[1024,1408]{1,0:T(8,128)(2,1)}, bf16[1408,1024]{1,0:T(8,128)(2,1)}), (bf16[1024,1408]{1,0:T(8,128)(2,1)}, bf16[1024,1408]{1,0:T(8,128)(2,1)}, bf16[1408,1024]{1,0:T(8,128)(2,1)})) %all-reduce.3.cloned.1.call-update) | async-done | bytes 8650768 | tf_op jit(solution)/shard_map/psum | solution.py:942
  470.1 4.9 convert_element_type.475
  481.2 6.0 unproject.1
  497.5 5.1 collective-permute-done.8
  535.6 5.2 collective-permute-start.43
  546.4 8.1 %collective-permute-done.14 = bf16[64,512]{1,0:T(8,128)(2,1)S(1)} collective-permute-done((bf16[64,512]{1,0:T(8,128)(2,1)S(1)}, bf16[64,512]{1,0:T(8,128)(2,1)S(1)}, u32[]{:S(2)}, u32[]{:S(2)}) %collective-permute-start.14) | collective-permute-done | bytes 65568 | tf_op jit(solution)/shard_map/ppermute | solution.py:837
  557.0 5.3 collective-permute-start.15
  590.8 7.9 %collective-permute-start.74 = (f32[2,1024]{1,0:T(2,128)S(1)}, f32[2,1024]{1,0:T(2,128)S(1)}, u32[]{:S(2)}, u32[]{:S(2)}) collective-permute-start(f32[2,1024]{1,0:T(2,128)S(1)} %add.436), channel_id=1, source_target_pairs={{0,16},{2,18},{4,20},{6,22},{8,24},{10,26},{12,28},{14,30},{16,0},... | collective-permute-start | bytes 24584 | tf_op jit(solution)/shard_map/ppermute | solution.py:788
  (320 shorter events, 228.6 us)
Async XLA Ops:
  97.7 19.3 %all-to-all-start.1 = ((bf16[16,128,128]{2,1,0:T(8,128)(2,1)}), bf16[16,128,128]{2,1,0:T(8,128)(2,1)S(1)}, u32[]{:S(2)}, u32[]{:S(2)}) async-start(bf16[16,128,128]{2,1,0:T(8,128)(2,1)} %get-tuple-element.33), calls=%async_computation.1 | async-start | bytes 1048576 | tf_op jit(solution)/shard_map/all_to_all | solution.py:920
  102.5 26.3 %collective-permute-start.2 = (bf16[512,1024]{1,0:T(8,128)(2,1)}, bf16[512,1024]{1,0:T(8,128)(2,1)}, u32[]{:S(2)}, u32[]{:S(2)}) collective-permute-start(bf16[512,1024]{1,0:T(8,128)(2,1)} %w_ref.1), channel_id=1, source_target_pairs={{0,1},{1,0},{2,3},{3,2},{4,5},{5,4},{6,7},{7,6},{8,9},{9,8},{10,11... | collective-permute-start | bytes 3145736 | tf_op jit(solution)/shard_map/ppermute | solution.py:784
  117.0 22.6 %collective-permute-start.1 = (bf16[16,128,128]{2,1,0:T(8,128)(2,1)S(1)}, bf16[16,128,128]{2,1,0:T(8,128)(2,1)S(1)}, u32[]{:S(2)}, u32[]{:S(2)}) collective-permute-start(bf16[16,128,128]{2,1,0:T(8,128)(2,1)S(1)} %all-to-all-done.1.own_ref), channel_id=1, source_target_pairs={{0,1},{1,0},{2,3},{3,2},{4,5},{5,4},{6,7},{7,6},{8,9},{9,8},{10,11... | collective-permute-start | bytes 1572872 | tf_op jit(solution)/shard_map/ppermute | solution.py:784
  158.8 24.8 %collective-permute-start.4 = (bf16[512,1024]{1,0:T(8,128)(2,1)S(1)}, bf16[512,1024]{1,0:T(8,128)(2,1)S(1)}, u32[]{:S(2)}, u32[]{:S(2)}) collective-permute-start(bf16[512,1024]{1,0:T(8,128)(2,1)S(1)} %add_convert_fusion.1.own_ref), channel_id=1, source_target_pairs={{0,1},{1,0},{2,3},{3,2},{4,5},{5,4},{6,7},{7,6},{8,9},{9,8},{10,11... | collective-permute-start | bytes 3145736 | tf_op jit(solution)/shard_map/ppermute | solution.py:784
  190.8 19.9 %all-to-all-start.2 = ((bf16[16,128,128]{2,1,0:T(8,128)(2,1)}), bf16[16,128,128]{2,1,0:T(8,128)(2,1)S(1)}, u32[]{:S(2)}, u32[]{:S(2)}) async-start(bf16[16,128,128]{2,1,0:T(8,128)(2,1)} %bitcast.33), calls=%async_computation.2 | async-start | bytes 1048576 | tf_op jit(solution)/shard_map/all_to_all | solution.py:950
  196.2 273.9 %all-reduce.3.cloned.1.call-start = ((), (), s32[]{:S(2)}) async-start(), calls=%async_computation.4 | async-start | bytes 17301504 | tf_op jit(solution)/shard_map/psum | solution.py:942
  206.5 46.4 %collective-permute-start.56 = (bf16[128,1024]{1,0:T(8,128)(2,1)S(1)}, bf16[128,1024]{1,0:T(8,128)(2,1)S(1)}, u32[]{:S(2)}, u32[]{:S(2)}) collective-permute-start(bf16[128,1024]{1,0:T(8,128)(2,1)S(1)} %constant_dynamic-slice_fusion.3), channel_id=1, source_target_pairs={{0,4},{2,6},{4,0},{6,2},{8,12},{10,14},{12,8},{14,10},{16,20},{18,... | collective-permute-start | bytes 786440 | tf_op jit(solution)/shard_map/ppermute | solution.py:788
  248.3 24.3 %collective-permute-start.5 = (bf16[16,256,128]{2,1,0:T(8,128)(2,1)}, bf16[16,256,128]{2,1,0:T(8,128)(2,1)}, u32[]{:S(2)}, u32[]{:S(2)}) collective-permute-start(bf16[16,256,128]{2,1,0:T(8,128)(2,1)} %get-tuple-element.41), channel_id=1, source_target_pairs={{0,2},{2,0},{4,6},{6,4},{8,10},{10,8},{12,14},{14,12},{16,18},{18,... | collective-permute-start | bytes 3145736 | tf_op jit(solution)/shard_map/ppermute | solution.py:788
  275.4 205.8 %all-to-all-start.3 = ((bf16[16,384,128]{2,1,0:T(8,128)(2,1)}), bf16[16,384,128]{2,1,0:T(8,128)(2,1)}, u32[]{:S(2)}, u32[]{:S(2)}) async-start(bf16[16,384,128]{2,1,0:T(8,128)(2,1)} %pad_maximum_fusion), calls=%async_computation.3 | async-start | bytes 3145728 | tf_op jit(solution)/shard_map/all_to_all | solution.py:963
  280.0 36.5 %collective-permute-start.62 = (bf16[32,1024]{1,0:T(8,128)(2,1)S(1)}, bf16[32,1024]{1,0:T(8,128)(2,1)S(1)}, u32[]{:S(2)}, u32[]{:S(2)}) collective-permute-start(bf16[32,1024]{1,0:T(8,128)(2,1)S(1)} %add_convert_fusion.12), channel_id=1, source_target_pairs={{8,0},{10,2},{12,4},{14,6},{16,8},{18,10},{20,12},{22,14},{24,16},... | collective-permute-start | bytes 196616 | tf_op jit(solution)/shard_map/ppermute | solution.py:837
  316.6 25.9 %collective-permute-start.63 = (bf16[32,1024]{1,0:T(8,128)(2,1)S(1)}, bf16[32,1024]{1,0:T(8,128)(2,1)S(1)}, u32[]{:S(2)}, u32[]{:S(2)}) collective-permute-start(bf16[32,1024]{1,0:T(8,128)(2,1)S(1)} %add_convert_fusion.11), channel_id=1, source_target_pairs={{0,8},{2,10},{4,12},{6,14},{8,16},{10,18},{12,20},{14,22},{16,24},... | collective-permute-start | bytes 196616 | tf_op jit(solution)/shard_map/ppermute | solution.py:849
  354.6 23.8 %collective-permute-start.3 = (bf16[512,1024]{1,0:T(8,128)(2,1)}, bf16[512,1024]{1,0:T(8,128)(2,1)}, u32[]{:S(2)}, u32[]{:S(2)}) collective-permute-start(bf16[512,1024]{1,0:T(8,128)(2,1)} %convolution_convert_fusion.3), channel_id=1, source_target_pairs={{0,1},{1,0},{2,3},{3,2},{4,5},{5,4},{6,7},{7,6},{8,9},{9,8},{10,11... | collective-permute-start | bytes 3145736 | tf_op jit(solution)/shard_map/ppermute | solution.py:784
  491.8 51.1 %collective-permute-start.6 = (bf16[512,1024]{1,0:T(8,128)(2,1)S(1)}, bf16[512,1024]{1,0:T(8,128)(2,1)S(1)}, u32[]{:S(2)}, u32[]{:S(2)}) collective-permute-start(bf16[512,1024]{1,0:T(8,128)(2,1)S(1)} %copy-done.5), channel_id=1, source_target_pairs={{0,1},{1,0},{2,3},{3,2},{4,5},{5,4},{6,7},{7,6},{8,9},{9,8},{10,11... | collective-permute-start | bytes 3145736 | tf_op jit(solution)/shard_map/ppermute | solution.py:784
  496.0 16.9 %collective-permute-start.40 = (bf16[256,512]{1,0:T(8,128)(2,1)S(1)}, bf16[256,512]{1,0:T(8,128)(2,1)S(1)}, u32[]{:S(2)}, u32[]{:S(2)}) collective-permute-start(bf16[256,512]{1,0:T(8,128)(2,1)S(1)} %constant_dynamic-slice_fusion.8), channel_id=1, source_target_pairs={{0,4},{2,6},{4,0},{6,2},{8,12},{10,14},{12,8},{14,10},{16,20},{18,... | collective-permute-start | bytes 786440 | tf_op jit(solution)/shard_map/ppermute | solution.py:788
  506.2 17.0 %collective-permute-start.12 = (bf16[64,512]{1,0:T(8,128)(2,1)S(1)}, bf16[64,512]{1,0:T(8,128)(2,1)S(1)}, u32[]{:S(2)}, u32[]{:S(2)}) collective-permute-start(bf16[64,512]{1,0:T(8,128)(2,1)S(1)} %get-tuple-element.75), channel_id=1, source_target_pairs={{24,16},{26,18},{28,20},{30,22},{25,17},{27,19},{29,21},{31,23}} | collective-permute-start | bytes 196616 | tf_op jit(solution)/shard_map/ppermute | solution.py:837
  512.8 16.5 %collective-permute-start.28 = (bf16[64,512]{1,0:T(8,128)(2,1)S(1)}, bf16[64,512]{1,0:T(8,128)(2,1)S(1)}, u32[]{:S(2)}, u32[]{:S(2)}) collective-permute-start(bf16[64,512]{1,0:T(8,128)(2,1)S(1)} %get-tuple-element.71), channel_id=1, source_target_pairs={{24,16},{26,18},{28,20},{30,22},{25,17},{27,19},{29,21},{31,23}} | collective-permute-start | bytes 196616 | tf_op jit(solution)/shard_map/ppermute | solution.py:837
  529.4 15.7 %collective-permute-start.11 = (bf16[64,512]{1,0:T(8,128)(2,1)S(1)}, bf16[64,512]{1,0:T(8,128)(2,1)S(1)}, u32[]{:S(2)}, u32[]{:S(2)}) collective-permute-start(bf16[64,512]{1,0:T(8,128)(2,1)S(1)} %get-tuple-element.72), channel_id=1, source_target_pairs={{0,8},{2,10},{4,12},{6,14},{8,16},{10,18},{12,20},{14,22},{16,24},... | collective-permute-start | bytes 196616 | tf_op jit(solution)/shard_map/ppermute | solution.py:836
  532.3 24.7 %collective-permute-start.27 = (bf16[64,512]{1,0:T(8,128)(2,1)S(1)}, bf16[64,512]{1,0:T(8,128)(2,1)S(1)}, u32[]{:S(2)}, u32[]{:S(2)}) collective-permute-start(bf16[64,512]{1,0:T(8,128)(2,1)S(1)} %get-tuple-element.68), channel_id=1, source_target_pairs={{0,8},{2,10},{4,12},{6,14},{8,16},{10,18},{12,20},{14,22},{16,24},... | collective-permute-start | bytes 196616 | tf_op jit(solution)/shard_map/ppermute | solution.py:836
  535.6 34.3 %collective-permute-start.43 = (bf16[64,512]{1,0:T(8,128)(2,1)S(1)}, bf16[64,512]{1,0:T(8,128)(2,1)S(1)}, u32[]{:S(2)}, u32[]{:S(2)}) collective-permute-start(bf16[64,512]{1,0:T(8,128)(2,1)S(1)} %get-tuple-element.64), channel_id=1, source_target_pairs={{0,8},{2,10},{4,12},{6,14},{8,16},{10,18},{12,20},{14,22},{16,24},... | collective-permute-start | bytes 196616 | tf_op jit(solution)/shard_map/ppermute | solution.py:836
  542.9 19.4 %collective-permute-start.30 = (bf16[64,512]{1,0:T(8,128)(2,1)S(1)}, bf16[64,512]{1,0:T(8,128)(2,1)S(1)}, u32[]{:S(2)}, u32[]{:S(2)}) collective-permute-start(bf16[64,512]{1,0:T(8,128)(2,1)S(1)} %add_convert_fusion.22), channel_id=1, source_target_pairs={{8,0},{10,2},{12,4},{14,6},{16,8},{18,10},{20,12},{22,14},{24,16},... | collective-permute-start | bytes 196616 | tf_op jit(solution)/shard_map/ppermute | solution.py:837
  545.1 26.1 %collective-permute-start.46 = (bf16[64,512]{1,0:T(8,128)(2,1)S(1)}, bf16[64,512]{1,0:T(8,128)(2,1)S(1)}, u32[]{:S(2)}, u32[]{:S(2)}) collective-permute-start(bf16[64,512]{1,0:T(8,128)(2,1)S(1)} %add_convert_fusion.17), channel_id=1, source_target_pairs={{8,0},{10,2},{12,4},{14,6},{16,8},{18,10},{20,12},{22,14},{24,16},... | collective-permute-start | bytes 196616 | tf_op jit(solution)/shard_map/ppermute | solution.py:837
  555.7 21.8 %collective-permute-start.18 = (bf16[64,512]{1,0:T(8,128)(2,1)S(1)}, bf16[64,512]{1,0:T(8,128)(2,1)S(1)}, u32[]{:S(2)}, u32[]{:S(2)}) collective-permute-start(bf16[64,512]{1,0:T(8,128)(2,1)S(1)} %add_convert_fusion.26), channel_id=1, source_target_pairs={{8,0},{10,2},{12,4},{14,6},{16,8},{18,10},{20,12},{22,14},{24,16},... | collective-permute-start | bytes 196616 | tf_op jit(solution)/shard_map/ppermute | solution.py:850
  557.0 27.1 %collective-permute-start.15 = (bf16[64,512]{1,0:T(8,128)(2,1)S(1)}, bf16[64,512]{1,0:T(8,128)(2,1)S(1)}, u32[]{:S(2)}, u32[]{:S(2)}) collective-permute-start(bf16[64,512]{1,0:T(8,128)(2,1)S(1)} %add_convert_fusion.26), channel_id=1, source_target_pairs={{0,8},{2,10},{4,12},{6,14},{8,16},{10,18},{12,20},{14,22},{16,24},... | collective-permute-start | bytes 196616 | tf_op jit(solution)/shard_map/ppermute | solution.py:849
  590.8 28.7 %collective-permute-start.74 = (f32[2,1024]{1,0:T(2,128)S(1)}, f32[2,1024]{1,0:T(2,128)S(1)}, u32[]{:S(2)}, u32[]{:S(2)}) collective-permute-start(f32[2,1024]{1,0:T(2,128)S(1)} %add.436), channel_id=1, source_target_pairs={{0,16},{2,18},{4,20},{6,22},{8,24},{10,26},{12,28},{14,30},{16,0},... | collective-permute-start | bytes 24584 | tf_op jit(solution)/shard_map/ppermute | solution.py:788
  (87 other events, 938.5 us)
Sparse Core Ops, SparseCore 0:
  253.1 216.9 all-reduce.2

commit v2 on v1

--- a/solution.py
+++ b/solution.py
@@ -351,6 +351,12 @@
 vmem_bytes = 60 * 1024 * 1024
 
 
+def busy(microseconds):
+    return pl.CostEstimate(
+        flops=int(microseconds * 1e9), bytes_accessed=int(microseconds * 2e6), transcendentals=0
+    )
+
+
 def lane_ids(shape):
     return lax.broadcasted_iota(jnp.int32, shape, len(shape) - 1)
 
@@ -439,6 +445,7 @@
             jax.ShapeDtypeStruct((rows, width), narrow),
         ],
         compiler_params=pltpu.CompilerParams(vmem_limit_bytes=vmem_bytes),
+        cost_estimate=busy(6),
         name="project",
     )(inputs, norm_attn.reshape(1, width), first_values, cosine, sine, w_query, w_key, w_value)
 
@@ -562,6 +569,7 @@
             pltpu.VMEM((count, HEAD_DIM, SEG), narrow),
         ],
         compiler_params=pltpu.CompilerParams(vmem_limit_bytes=vmem_bytes),
+        cost_estimate=busy(30),
         name="attend",
     )(parents, assignment, part, recv, other)
 
@@ -643,6 +651,7 @@
             pltpu.VMEM((count, SEG, LANES), wide),
         ],
         compiler_params=pltpu.CompilerParams(vmem_limit_bytes=vmem_bytes),
+        cost_estimate=busy(37),
         name="attend_back",
     )(parents, assignment, part, recv, other, grad, ot, logs)
 
@@ -688,6 +697,7 @@
             jax.ShapeDtypeStruct((tokens, width), narrow),
         ],
         compiler_params=pltpu.CompilerParams(vmem_limit_bytes=vmem_bytes),
+        cost_estimate=busy(6),
         name="merge",
     )(own, other, w_own, w_other, inputs, norm_ffn.reshape(1, width))
 
@@ -731,53 +741,147 @@
             jax.ShapeDtypeStruct((1, width), wide),
         ],
         compiler_params=pltpu.CompilerParams(vmem_limit_bytes=vmem_bytes),
+        cost_estimate=busy(6),
         name="branch_back",
     )(own, other, hidden, cotangent, norm_ffn.reshape(1, width), w_out)
 
 
-def unproject_kernel(
-    recv_ref, cos_ref, sin_ref, wq_ref, wk_ref, wv_ref, gq_ref, gk_ref, gv_ref, first_ref, part_ref
+def fold_kernel(
+    mine_ref, arrived_ref, dq_ref, cos_ref, sin_ref, slot_cos_ref, slot_sin_ref, send_ref, feats_ref
 ):
+    count, rows, _ = mine_ref.shape
+    half = rows // 2
+    low = lane_ids((rows, LANES)) < HEAD_DIM
+
+    def step(slot, carry):
+        turn_cos = slot_cos_ref[slot][:1]
+        turn_sin = slot_sin_ref[slot][:1]
+        cosine = cos_ref[...] * turn_cos - sin_ref[...] * turn_sin
+        sine = -(sin_ref[...] * turn_cos + cos_ref[...] * turn_sin)
+        pair = mine_ref[slot] + arrived_ref[slot].astype(wide)
+        key = spin(pair, cosine, sine)
+        send_ref[slot, :rows, :] = jnp.where(low, key, pair).astype(narrow)
+        feats_ref[slot, :, :LANES] = jnp.where(low, key, 0.5 * pair.astype(narrow).astype(wide)).astype(narrow)
+        packed = dq_ref[slot].astype(wide)
+        query = jnp.concatenate([packed, pltpu.roll(packed, HEAD_DIM, 1)], axis=0)
+        query = jnp.where(low, spin(query, cosine, sine), 0.0)
+        feats_ref[slot, :, LANES:] = query.astype(narrow)
+        top = query[:half]
+        bottom = pltpu.roll(query[half:], HEAD_DIM, 1)
+        send_ref[slot, rows:, :] = jnp.where(low[:half], top, bottom).astype(narrow)
+        return carry
+
+    lax.fori_loop(0, count, step, 0)
+
+
+def fold(mine, arrived, grad_q, cosine, sine, slot_cos, slot_sin):
+    count, rows, _ = mine.shape
+    return pl.pallas_call(
+        fold_kernel,
+        in_specs=[whole_spec()] * 7,
+        out_specs=[whole_spec()] * 2,
+        out_shape=[
+            jax.ShapeDtypeStruct((count, rows + rows // 2, LANES), narrow),
+            jax.ShapeDtypeStruct((count, rows, 2 * LANES), narrow),
+        ],
+        compiler_params=pltpu.CompilerParams(vmem_limit_bytes=vmem_bytes),
+        cost_estimate=busy(9),
+        name="fold",
+    )(mine, arrived, grad_q, cosine, sine, slot_cos, slot_sin)
+
+
+def unproject_kernel(recv_ref, wq_ref, wk_ref, wv_ref, first_ref, part_ref):
     groups = 2
     rows = recv_ref.shape[1] * 2 // 3
-    half = rows // 2
     heads = recv_ref.shape[0] // groups
     for part in range(groups):
         span = slice(part * rows, (part + 1) * rows)
-        cosine = cos_ref[span, :]
-        sine = -sin_ref[span, :]
+        keys, values, queries = [], [], []
         for pair in range(heads // 2):
             cols = slice(pair * LANES, (pair + 1) * LANES)
             left = recv_ref[2 * pair * groups + part].astype(wide)
             right = recv_ref[(2 * pair + 1) * groups + part].astype(wide)
             key, value = swap_pairs(left[:rows], right[:rows])
             query = jnp.concatenate(swap_pairs(left[rows:], right[rows:]), axis=0)
-            gq_ref[span, cols] = spin(query, cosine, sine).astype(narrow)
-            gk_ref[span, cols] = spin(key, cosine, sine).astype(narrow)
             value = 0.5 * value
             first_ref[span, cols] = value
-            gv_ref[span, cols] = value.astype(narrow)
-    total = dot_rows(gq_ref[...], wq_ref[...])
-    total = total + dot_rows(gk_ref[...], wk_ref[...])
-    total = total + dot_rows(gv_ref[...], wv_ref[...])
-    part_ref[...] = total.astype(narrow)
-
-
-def unproject(recv, cosine, sine, w_query, w_key, w_value):
+            keys.append(key.astype(narrow))
+            values.append(value.astype(narrow))
+            queries.append(query.astype(narrow))
+        total = dot_rows(jnp.concatenate(queries, axis=1), wq_ref[...])
+        total = total + dot_rows(jnp.concatenate(keys, axis=1), wk_ref[...])
+        total = total + dot_rows(jnp.concatenate(values, axis=1), wv_ref[...])
+        part_ref[span, :] = total.astype(narrow)
+
+
+def unproject(recv, w_query, w_key, w_value):
     width, local = w_query.shape
-    tokens = cosine.shape[0]
+    tokens = recv.shape[1] * 4 // 3
     return pl.pallas_call(
         unproject_kernel,
-        in_specs=[whole_spec()] * 6,
-        out_specs=[whole_spec()] * 5,
-        out_shape=[jax.ShapeDtypeStruct((tokens, local), narrow)] * 3
-        + [
+        in_specs=[whole_spec()] * 4,
+        out_specs=[whole_spec()] * 2,
+        out_shape=[
             jax.ShapeDtypeStruct((tokens, local), wide),
             jax.ShapeDtypeStruct((tokens, width), narrow),
         ],
         compiler_params=pltpu.CompilerParams(vmem_limit_bytes=vmem_bytes),
+        cost_estimate=busy(6),
         name="unproject",
-    )(recv, cosine, sine, w_query, w_key, w_value)
+    )(recv, w_query, w_key, w_value)
+
+
+def finish_kernel(part_ref, own_ref, other_ref, query_ref, key_ref, value_ref, out_ref):
+    chips, size, width = own_ref.shape
+    part = part_ref[0]
+    head_rows = 3 * HEAD_DIM // 2
+    out_rows = size - head_rows
+
+    def emit(first, second):
+        for chip in range(chips):
+            at = chip * out_rows
+            out_ref[at : at + out_rows, :] = first[chip, head_rows:, :].astype(wide)
+            at += chips * out_rows
+            out_ref[at : at + out_rows, :] = second[chip, head_rows:, :].astype(wide)
+
+        def column(block, carry):
+            cols = pl.ds(pl.multiple_of(block * LANES, LANES), LANES)
+            for pair in range(chips // 2):
+                pieces = [
+                    jnp.concatenate(
+                        [first[chip, :head_rows, cols], second[chip, :head_rows, cols]], axis=0
+                    ).astype(wide)
+                    for chip in (2 * pair, 2 * pair + 1)
+                ]
+                for at, target in enumerate((key_ref, value_ref, query_ref)):
+                    span = slice(at * HEAD_DIM, (at + 1) * HEAD_DIM)
+                    both = jnp.concatenate([piece[span] for piece in pieces], axis=0)
+                    target[cols, pair * LANES : (pair + 1) * LANES] = jnp.transpose(both)
+            return carry
+
+        lax.fori_loop(0, width // LANES, column, 0)
+
+    @pl.when(part == 0)
+    def _():
+        emit(own_ref, other_ref)
+
+    @pl.when(part == 1)
+    def _():
+        emit(other_ref, own_ref)
+
+
+def finish(part, own, other, local):
+    width = own.shape[2]
+    return pl.pallas_call(
+        finish_kernel,
+        in_specs=[scalar_spec()] + [whole_spec()] * 2,
+        out_specs=[whole_spec()] * 4,
+        out_shape=[jax.ShapeDtypeStruct((width, local), wide)] * 3
+        + [jax.ShapeDtypeStruct((local, width), wide)],
+        compiler_params=pltpu.CompilerParams(vmem_limit_bytes=vmem_bytes),
+        cost_estimate=busy(6),
+        name="finish",
+    )(part, own, other)
 
 
 def swap_tensor(values):
@@ -801,6 +905,73 @@
     mine = (place // bit) % 2
     arrived = swap_bit(take_part(values, 1 - mine, 2), bit, count)
     return add_narrow(take_part(values, mine, 2), arrived)
+
+
+def side_groups(count):
+    return [[chip * 2 + core for chip in range(count // 2)] for core in range(2)]
+
+
+def to_chips(values, count):
+    return lax.all_to_all(
+        values, "dp", split_axis=0, concat_axis=0, tiled=True, axis_index_groups=side_groups(count)
+    )
+
+
+def spread(values, count):
+    chips = count // 2
+    return to_chips(jnp.broadcast_to(values[None], (chips,) + values.shape), count)
+
+
+def spread_rows(values, before, place, count):
+    lines = [[z * 4 + rest for z in range(count // 4)] for rest in range(4)]
+    length = count // 4
+    along = lax.all_to_all(
+        jnp.broadcast_to(values[None], (length,) + values.shape),
+        "dp",
+        split_axis=0,
+        concat_axis=0,
+        tiled=True,
+        axis_index_groups=lines,
+    )
+    along = after(along, before)
+    arrived = swap_bit(along, 2, count)
+    high = (place // 2) % 2 == 1
+    pair = jnp.stack([jnp.where(high, arrived, along), jnp.where(high, along, arrived)], axis=1)
+    return pair.reshape((2 * length,) + values.shape)
+
+
+def gather_core(values, axis, place, count):
+    mine = place % 2
+    arrived = swap_bit(values, 1, count)
+    row = jnp.concatenate([arrived, values, arrived], axis=axis)
+    size = values.shape[axis]
+    return lax.dynamic_slice_in_dim(row, (1 - mine) * size, 2 * size, axis)
+
+
+def sum_over_dp(values, place, count):
+    chips = count // 2
+    values = reduce_bit(values, 1, place, count)
+    shares = to_chips(values.reshape((chips, values.shape[0] // chips) + values.shape[1:]), count)
+    total = jnp.sum(shares.astype(wide), axis=0).astype(narrow)
+    whole = spread(total, count)
+    whole = whole.reshape((-1,) + whole.shape[2:])
+    return gather_core(whole, 0, place, count)
+
+
+def reduce_z(values, place, count):
+    at = place // 4
+    total = take_part(values, at, 4).astype(wide)
+    for step in (1, 2, 3):
+        share = take_part(values, at ^ step, 4)
+        total = total + swap_bit(share, 4 * step, count).astype(wide)
+    return total.astype(narrow)
+
+
+def gather_z(values, place, count):
+    at = place // 4
+    shares = [values] + [swap_bit(values, 4 * step, count) for step in (1, 2, 3)]
+    row = jnp.concatenate(shares, axis=0)
+    return jnp.concatenate([take_part(row, at ^ target, 4) for target in range(4)], axis=0)
 
 
 def gather_bit(values, bit, place, count):
@@ -811,57 +982,8 @@
     return lax.dynamic_slice_in_dim(row, (1 - mine) * size, 2 * size, 0)
 
 
-def line_pairs(line, stride, count, up, keep):
-    pairs = []
-    for device in range(count):
-        at = device // stride
-        if up and at + 1 < line and keep(at):
-            pairs.append((device, device + stride))
-        if not up and at >= 1 and keep(line - 1 - at):
-            pairs.append((device, device - stride))
-    return pairs
-
-
-def reduce_line(values, stride, place, count):
-    line = count // stride
-    at = place // stride
-    up = down = None
-    for step in range(1, line):
-        share_up = take_part(values, jnp.clip(line - step + at, 0, line - 1), line)
-        share_down = take_part(values, jnp.clip(step - line + at, 0, line - 1), line)
-        if up is not None:
-            share_up = add_narrow(share_up, up)
-            share_down = add_narrow(share_down, down)
-        keep = lambda index, step=step: index <= step - 1
-        up = lax.ppermute(share_up, "dp", line_pairs(line, stride, count, True, keep))
-        down = lax.ppermute(share_down, "dp", line_pairs(line, stride, count, False, keep))
-    own = take_part(values, at, line).astype(wide)
-    return (own + up.astype(wide) + down.astype(wide)).astype(narrow)
-
-
-def gather_line(values, stride, place, count):
-    line = count // stride
-    at = place // stride
-    below, above = [], []
-    up = down = values
-    for step in range(1, line):
-        keep_up = lambda index, step=step: index >= step - 1
-        up = lax.ppermute(up, "dp", line_pairs(line, stride, count, True, keep_up))
-        down = lax.ppermute(down, "dp", line_pairs(line, stride, count, False, keep_up))
-        below.append(up)
-        above.append(down)
-    row = jnp.concatenate(below[::-1] + [values] + above, axis=0)
-    size = values.shape[0]
-    return lax.dynamic_slice_in_dim(row, (line - 1 - at) * size, line * size, 0)
-
-
-def sum_over_dp(values, place, count):
-    values = reduce_bit(values, 1, place, count)
-    values = reduce_bit(values, 2, place, count)
-    values = reduce_line(values, 4, place, count)
-    values = gather_line(values, 4, place, count)
-    values = gather_bit(values, 2, place, count)
-    return gather_bit(values, 1, place, count).astype(wide)
+def after(value, *others):
+    return lax.optimization_barrier((value,) + others)[0]
 
 
 def sum_small(values, count):
@@ -898,23 +1020,46 @@
     part = (place % groups).astype(jnp.int32)
     part_array = part.reshape(1)
 
+    rows = tokens // groups
+    half = HEAD_DIM // 2
     w_out_other = swap_tensor(w_out)
     slot_ids = jnp.arange(count, dtype=jnp.int32)
     start = jnp.sum(jnp.where(slot_ids == place, depth_pos, 0))
-    positions = (start + jnp.arange(tokens, dtype=jnp.int32)).astype(wide)
-    half = HEAD_DIM // 2
     lanes = jnp.arange(LANES, dtype=jnp.int32)
     frequency = rope_base ** (-(lanes % half).astype(wide) * 2.0 / HEAD_DIM)
+    sign = jnp.where(lanes % HEAD_DIM < half, -1.0, 1.0)[None, :]
+    positions = (start + jnp.arange(tokens, dtype=jnp.int32)).astype(wide)
     angles = positions[:, None] * frequency[None, :]
     cosine = jnp.cos(angles)
-    sine = jnp.sin(angles) * jnp.where(lanes % HEAD_DIM < half, -1.0, 1.0)[None, :]
+    sine = jnp.sin(angles) * sign
+    part_positions = (part * rows + jnp.arange(rows, dtype=jnp.int32)).astype(wide)
+    part_angles = part_positions[:, None] * frequency[None, :]
+    part_cos = jnp.cos(part_angles)
+    part_sin = jnp.sin(part_angles) * sign
+    slot_angles = depth_pos.astype(wide)[:, None] * frequency[None, :]
+    slot_shape = (count, 8, LANES)
+    slot_cos = jnp.broadcast_to(jnp.cos(slot_angles)[:, None, :], slot_shape)
+    slot_sin = jnp.broadcast_to((jnp.sin(slot_angles) * sign)[:, None, :], slot_shape)
 
     send, normed = project(
         inputs, norm_attn, first_values, cosine, sine, w_query, w_key, w_value, groups
     )
-    rows = tokens // groups
     send = send.reshape(count, rows + rows // 2, LANES)
     recv = lax.all_to_all(send, "dp", split_axis=0, concat_axis=0, tiled=True)
+    normed_theirs = swap_bit(take_part(normed, 1 - part, groups), 1, count)
+    normed_mine = take_part(normed, part, groups)
+    normed_row = jnp.concatenate([normed_theirs, normed_mine, normed_theirs], axis=0)
+    normed_chip = lax.dynamic_slice_in_dim(normed_row, (1 - part) * rows, groups * rows, 0)
+    side = lax.axis_index("tensor")
+    quarter = rows // 2
+    normed_quarter = lax.dynamic_index_in_dim(
+        normed_chip.reshape(groups, 2, quarter, width), side, 1, keepdims=False
+    ).reshape(groups * quarter, width)
+    recv, normed_quarter = lax.optimization_barrier((recv, normed_quarter))
+    normed_own = lax.all_gather(
+        normed_quarter, "dp", axis=0, tiled=True, axis_index_groups=side_groups(count)
+    )
+
     other = swap_bit(recv[:, :rows], 1, count)
     packed, ot, logs = attend(parents, assignment, part_array, recv, other)
     own_out = lax.all_to_all(packed, "dp", split_axis=0, concat_axis=0, tiled=True)
@@ -936,60 +1081,94 @@
         + jnp.einsum("tf,df->td", grad_up, w_up, preferred_element_type=wide)
     ).astype(narrow)
     ffn_other = swap_tensor(ffn_partial)
-    grad_w_gate = jnp.einsum("td,tf->df", normed_ffn, grad_gate, preferred_element_type=wide)
-    grad_w_up = jnp.einsum("td,tf->df", normed_ffn, grad_up, preferred_element_type=wide)
-    grad_w_down = jnp.einsum("tf,td->fd", activated, cotangent, preferred_element_type=wide)
-    grad_w_gate, grad_w_up, grad_w_down = lax.psum(
-        (grad_w_gate.astype(narrow), grad_w_up.astype(narrow), grad_w_down.astype(narrow)), "dp"
+    ffn_grads = tuple(
+        jnp.einsum(form, left, right, preferred_element_type=wide).astype(narrow)
+        for form, left, right in (
+            ("td,tf->df", normed_ffn, grad_gate),
+            ("td,tf->df", normed_ffn, grad_up),
+            ("tf,td->fd", activated, cotangent),
+        )
     )
     feed_partial = jnp.dot(activated, w_down, preferred_element_type=wide).astype(narrow)
 
-    grad_send, grad_hidden, grad_branch, grad_gain_ffn = branch_back(
-        ffn_partial, ffn_other, hidden, cotangent, norm_ffn, w_out
-    )
-    grad_recv = lax.all_to_all(
-        grad_send.reshape(count, rows // 2, LANES), "dp", split_axis=0, concat_axis=0, tiled=True
-    )
-    feed_other = swap_tensor(feed_partial)
-    feed = feed_partial.astype(wide) + feed_other.astype(wide)
-    output = (hidden + feed).astype(narrow)
-    grad_w_out = jnp.einsum("tc,td->cd", attended, grad_branch, preferred_element_type=wide)
-
-    grad_q, mine, theirs = attend_back(
-        parents, assignment, part_array, recv, other, grad_recv, ot, logs
-    )
-    arrived = swap_bit(theirs, 1, count)
-    back_send = jnp.concatenate([(mine + arrived.astype(wide)).astype(narrow), grad_q], axis=1)
-    back_recv = lax.all_to_all(back_send, "dp", split_axis=0, concat_axis=0, tiled=True)
-    grad_query, grad_key, grad_value, grad_first, attn_partial = unproject(
-        back_recv, cosine, sine, w_query, w_key, w_value
-    )
-    attn_other = swap_tensor(attn_partial)
-    grad_w_query = jnp.einsum("td,tc->dc", normed, grad_query, preferred_element_type=wide)
-    grad_w_key = jnp.einsum("td,tc->dc", normed, grad_key, preferred_element_type=wide)
-    grad_w_value = jnp.einsum("td,tc->dc", normed, grad_value, preferred_element_type=wide)
-    sums = [
-        sum_over_dp(term.astype(narrow), place, count)
-        for term in (grad_w_query, grad_w_key, grad_w_value, grad_w_out)
-    ]
-    inputs_wide = inputs.astype(wide)
-    grad_normed = attn_partial.astype(wide) + attn_other.astype(wide)
-    grad_input_norm, grad_gain_attn = norm_back(
-        grad_normed, inputs_wide, rms_scale(inputs_wide), norm_attn.astype(wide)
-    )
-    grad_inputs = grad_hidden + grad_input_norm
-    gains = sum_small(jnp.stack([grad_gain_attn, grad_gain_ffn[0]]), count)
+    normed_own, *ffn_grads = lax.optimization_barrier((normed_own,) + ffn_grads)
+    ffn_sums = lax.psum(tuple(ffn_grads), "dp")
+    ffn_other = after(ffn_other, *ffn_grads)
+
+    def way_back(ffn_other, normed_own):
+        grad_send, grad_hidden, grad_branch, grad_gain_ffn = branch_back(
+            ffn_partial, ffn_other, hidden, cotangent, norm_ffn, w_out
+        )
+        grad_recv = lax.all_to_all(
+            grad_send.reshape(count, rows // 2, LANES), "dp", split_axis=0, concat_axis=0, tiled=True
+        )
+        grad_w_out = jnp.einsum("tc,td->cd", attended, grad_branch, preferred_element_type=wide)
+        out_half = reduce_bit(grad_w_out.astype(narrow), 1, place, count)
+        grad_recv, out_half = lax.optimization_barrier((grad_recv, out_half))
+        chips = count // 2
+        out_shares = to_chips(out_half.reshape(chips, local // count, width), count)
+        out_share = jnp.sum(out_shares.astype(wide), axis=0).astype(narrow)
+        normed_other = swap_tensor(normed_own)
+        feed_other = swap_tensor(after(feed_partial, normed_other))
+
+        grad_q, mine, theirs = attend_back(
+            parents, assignment, part_array, recv, other, grad_recv, ot, logs
+        )
+        arrived = swap_bit(theirs, 1, count)
+        back_send, feats = fold(
+            mine, arrived, grad_q, part_cos, part_sin, slot_cos, slot_sin
+        )
+        back_recv = lax.all_to_all(back_send, "dp", split_axis=0, concat_axis=0, tiled=True)
+        feats = feats.reshape(count, 2, quarter, 2 * LANES)
+        head_grads = sum(
+            jnp.einsum(
+                "tc,td->cd",
+                lax.dynamic_index_in_dim(feats, at, 1, keepdims=False).reshape(-1, 2 * LANES),
+                normed_part,
+                preferred_element_type=wide,
+            )
+            for at, normed_part in ((side, normed_own), (1 - side, normed_other))
+        )
+        head_grads = head_grads[: 3 * HEAD_DIM].astype(narrow)
+        head_share = reduce_bit(head_grads, 1, place, count)
+        share = jnp.concatenate([head_share, out_share], axis=0)
+        back_recv, feed_other = lax.optimization_barrier((back_recv, feed_other))
+        grad_first, attn_partial = unproject(back_recv, w_query, w_key, w_value)
+        attn_other = swap_tensor(attn_partial)
+        spread_all = spread_rows(after(share, attn_partial), attn_other, place, count)
+        spread_other = swap_bit(spread_all, 1, count)
+
+        output = (hidden + (feed_partial.astype(wide) + feed_other.astype(wide))).astype(narrow)
+        inputs_wide = inputs.astype(wide)
+        grad_normed = attn_partial.astype(wide) + attn_other.astype(wide)
+        grad_input_norm, grad_gain_attn = norm_back(
+            grad_normed, inputs_wide, rms_scale(inputs_wide), norm_attn.astype(wide)
+        )
+        grad_inputs = grad_hidden + grad_input_norm
+        gains = sum_small(jnp.stack([grad_gain_attn, grad_gain_ffn[0]]), count)
+        head_grads = finish(part_array, spread_all, spread_other, local)
+        return (output, grad_inputs, grad_first, gains) + tuple(head_grads)
+
+    def no_tree(*operands):
+        shapes = jax.eval_shape(way_back, *operands)
+        return tuple(jnp.zeros(leaf.shape, leaf.dtype) for leaf in shapes)
+
+    output, grad_inputs, grad_first, gains, *head_grads = lax.cond(
+        parents[0] < 0, way_back, no_tree, ffn_other, normed_own
+    )
+    head_query, head_key, head_value, sum_w_out = head_grads
+    ffn_sums = [after(term, gains) for term in ffn_sums]
     return (
         output,
         grad_inputs,
         grad_first,
-        sums[0],
-        sums[1],
-        sums[2],
-        sums[3],
-        grad_w_gate.astype(wide),
-        grad_w_up.astype(wide),
-        grad_w_down.astype(wide),
+        head_query,
+        head_key,
+        head_value,
+        sum_w_out,
+        ffn_sums[0].astype(wide),
+        ffn_sums[1].astype(wide),
+        ffn_sums[2].astype(wide),
         gains[0],
         gains[1],
     )

time: 647 us -> 478 us (0.74)
  starting transfers between devices: 160 us -> 64 us
  waiting for transfers between devices: 238 us -> 194 us
  blocking collectives: 43.5 us -> 0 us
  Pallas kernels: 90.9 us -> 106 us
  local copies, waits for them, and re-layouts: 9.25 us -> 20.9 us
  other arithmetic: 42.5 us -> 31.3 us
    ppermute x48 -> x0, starting transfers between devices: 112 us -> none  [the longest x12 42.8 us: gather_line(): up = lax.ppermute(up, 'dp', line_pairs(line, stride, count, True, keep_up))]
    all_to_all x2 -> x5, waiting for transfers between devices: 2.39 us -> 98.8 us  [the longest x1 32.4 us: way_back(): lax.all_to_all(back_send, 'dp', split_axis=0, concat_axis=0, tiled=True)]
    psum x1, waiting for transfers between devices: 85.9 us -> 0.02 us  [body_heads(): ffn_sums = lax.psum(tuple(ffn_grads), 'dp')]
    ppermute x48 -> x0, waiting for transfers between devices: 68.3 us -> none  [the longest x12 43.3 us: reduce_line(): lax.ppermute(share_down, 'dp', line_pairs(line, stride, count, False, keep))]
    all_to_all x1 -> x0, blocking collectives: 43.5 us -> none  [body_heads(): recv = lax.all_to_all(send, 'dp', split_axis=0, concat_axis=0, tiled=True)]
    all_to_all x2 -> x5, starting transfers between devices: 9.91 us -> 37.1 us  [the longest x1 10.9 us: way_back(): lax.all_to_all(grad_send.reshape(count, rows // 2, LANES), 'dp', split_ax...]
    ppermute x22 -> x11, starting transfers between devices: 25.8 us -> 8.31 us  [swap_bit(): return lax.ppermute(values, 'dp', [(i, i ^ bit) for i in range(count)])]
    pallas_call x1 -> x3, Pallas kernels: 5.99 us -> 21.7 us  [the longest x1 8.83 us: fold(): pl.pallas_call(fold_kernel, in_specs=[whole_spec()] * 7, out_specs=[whole...]
  transfers between devices with their start and end apart: 79 -> 25, of which waited for: 29 -> 17; matrix products, arithmetic and copies ran while one was open for 10% -> 14% of each run, Pallas kernels for 6% -> 21%
where the time goes in v2:
time: 478 us; the launch traced here: 470 us
  waiting for transfers between devices  194 us (41%)
  Pallas kernels  106 us (22%)
  starting transfers between devices  64 us (13%)
  matrix products  38.5 us (8%)
  other arithmetic  31.3 us (7%)
  local copies, waits for them, and re-layouts  20.9 us (4%)
  between operations  14.9 us (3%)
    ppermute x6, waiting for transfers between devices, swap_tensor(): return lax.ppermute(values, 'tensor', [(0, 1), (1, 0)])  43.4 us
    pallas_call x1, Pallas kernels, attend_back(): pl.pallas_call(attend_back_kernel, in_specs=[scalar_spec()] * 3 + [whole_...  36.8 us
    all_to_all x1, waiting for transfers between devices, way_back(): lax.all_to_all(back_send, 'dp', split_axis=0, concat_axis=0, tiled=True)  32.4 us
    ppermute x11, waiting for transfers between devices, swap_bit(): return lax.ppermute(values, 'dp', [(i, i ^ bit) for i in range(count)])  30.7 us
    pallas_call x1, Pallas kernels, attend(): pl.pallas_call(attend_kernel, in_specs=[scalar_spec()] * 3 + [whole_spec(...  30 us
    all_to_all x1, waiting for transfers between devices, body_heads(): recv = lax.all_to_all(send, 'dp', split_axis=0, concat_axis=0, tiled=True)  24.6 us
    all_to_all x1, waiting for transfers between devices, body_heads(): lax.all_to_all(packed, 'dp', split_axis=0, concat_axis=0, tiled=True)  21 us
    all_to_all x1, waiting for transfers between devices, way_back(): lax.all_to_all(grad_send.reshape(count, rows // 2, LANES), 'dp', split_ax...  17.3 us
  transfers between devices with their start and end apart: 25, of which 17 were waited for; matrix products, arithmetic and copies ran while one was open for 14% of the time, Pallas kernels for 21%

profile of v2, /device:TPU:0, one launch (start us, length us, event | category | flops | bytes accessed | tf_op | source)
XLA Modules:
  0.0 470.0 jit_solution(16248911448813349964)
XLA Ops:
  12.4 6.2 %project.1 = (bf16[8,2,384,128]{3,2,1,0:T(8,128)(2,1)}, bf16[512,1024]{1,0:T(8,128)(2,1)}) custom-call(bf16[512,1024]{1,0:T(8,128)(2,1)} %x_ref.3, bf16[1,1024]{1,0:T(2,128)(2,1)} %reshape.176.gain_ref, bf16[512,512]{1,0:T(8,128)(2,1)} %first_ref.1, f32[512,128]{1,0:T(8,128)} %get-tuple-element.216.cos_ref, f32[512,128]{1,0:T(8,128)} %get-tuple-element.215.sin_ref, ...), custom_call_target="tpu_custom_call" | custom-call | flops 6000000000 | bytes 12000000 | tf_op jit(solution)/shard_map/project/pallas_call | solution.py:426
  18.6 7.4 %all-to-all-start.4 = ((bf16[16,384,128]{2,1,0:T(8,128)(2,1)}), bf16[16,384,128]{2,1,0:T(8,128)(2,1)}, u32[]{:S(2)}, u32[]{:S(2)}) async-start(bf16[16,384,128]{2,1,0:T(8,128)(2,1)} %bitcast.56), calls=%async_computation.4 | async-start | bytes 3145728 | tf_op jit(solution)/shard_map/all_to_all | solution.py:1048
  33.5 24.6 %all-to-all-done.4.recv_ref = bf16[16,384,128]{2,1,0:T(8,128)(2,1)} async-done(((bf16[16,384,128]{2,1,0:T(8,128)(2,1)}), bf16[16,384,128]{2,1,0:T(8,128)(2,1)}, u32[]{:S(2)}, u32[]{:S(2)}) %all-to-all-start.4) | async-done | bytes 1572896 | tf_op jit(solution)/shard_map/all_to_all | solution.py:1048
  63.8 30.0 %attend.1 = (bf16[16,128,128]{2,1,0:T(8,128)(2,1)}, f32[16,64,256]{2,1,0:T(8,128)}, f32[16,8,256]{2,1,0:T(8,128)}) custom-call(s32[16]{0:T(128)S(1)} %copy-done.22, s32[16]{0:T(128)S(1)} %copy-done.23, s32[1]{0:T(128)} %bitcast.15.part_ref, bf16[16,384,128]{2,1,0:T(8,128)(2,1)} %all-to-all-done.4.recv_ref, ...), custom_call_target="tpu_custom_call" | custom-call | flops 30000001024 | bytes 60000000 | tf_op jit(solution)/shard_map/attend/pallas_call | solution.py:558
  93.8 8.8 %all-to-all-start.5 = ((bf16[16,128,128]{2,1,0:T(8,128)(2,1)}), bf16[16,128,128]{2,1,0:T(8,128)(2,1)}, u32[]{:S(2)}, u32[]{:S(2)}) async-start(bf16[16,128,128]{2,1,0:T(8,128)(2,1)} %get-tuple-element.150), calls=%async_computation.5 | async-start | bytes 1048576 | tf_op jit(solution)/shard_map/all_to_all | solution.py:1065
  104.7 21.0 %all-to-all-done.5.own_ref = bf16[16,128,128]{2,1,0:T(8,128)(2,1)} async-done(((bf16[16,128,128]{2,1,0:T(8,128)(2,1)}), bf16[16,128,128]{2,1,0:T(8,128)(2,1)}, u32[]{:S(2)}, u32[]{:S(2)}) %all-to-all-start.5) | async-done | bytes 524320 | tf_op jit(solution)/shard_map/all_to_all | solution.py:1065
  127.8 5.6 %fusion.29 = f32[512,1408]{1,0:T(8,128)} fusion(bf16[512,1024]{1,0:T(8,128)(2,1)} %param.28, bf16[1408,1024]{1,0:T(8,128)(2,1)} %param.25), kind=kOutput, calls=%fused_computation.77 | convolution fusion | flops 1476395008 | bytes 6815744 | tf_op jit(solution)/shard_map/td,fd->tf/dot_general | solution.py:1073
  133.4 6.8 %collective-permute-done.14.other_ref = bf16[16,128,128]{2,1,0:T(8,128)(2,1)} collective-permute-done((bf16[16,128,128]{2,1,0:T(8,128)(2,1)}, bf16[16,128,128]{2,1,0:T(8,128)(2,1)}, u32[]{:S(2)}, u32[]{:S(2)}) %collective-permute-start.14) | collective-permute-done | bytes 524320 | tf_op jit(solution)/shard_map/ppermute | solution.py:888
  140.2 5.3 %merge.1 = (bf16[512,512]{1,0:T(8,128)(2,1)}, f32[512,1024]{1,0:T(8,128)}, bf16[512,1024]{1,0:T(8,128)(2,1)}) custom-call(bf16[16,128,128]{2,1,0:T(8,128)(2,1)} %all-to-all-done.5.own_ref, bf16[16,128,128]{2,1,0:T(8,128)(2,1)} %collective-permute-done.14.other_ref, bf16[512,1024]{1,0:T(8,128)(2,1)} %w_own_ref.1, ...), custom_call_target="tpu_custom_call" | custom-call | flops 6000000000 | bytes 12000000 | tf_op jit(solution)/shard_map/merge/pallas_call | solution.py:690
  168.6 12.8 %collective-permute-done.16 = bf16[512,1024]{1,0:T(8,128)(2,1)} collective-permute-done((bf16[512,1024]{1,0:T(8,128)(2,1)S(1)}, bf16[512,1024]{1,0:T(8,128)(2,1)}, u32[]{:S(2)}, u32[]{:S(2)}) %collective-permute-start.16) | collective-permute-done | bytes 1048608 | tf_op jit(solution)/shard_map/ppermute | solution.py:888
  186.7 263.5 %conditional.1 = (bf16[512,1024]{1,0:T(8,128)(2,1)}, f32[512,1024]{1,0:T(8,128)S(1)}, f32[512,512]{1,0:T(8,128)}, f32[2,1024]{1,0:T(2,128)}, f32[1024,512]{1,0:T...) conditional(s32[]{:T(128)} %bitcast.14, () %tuple.29, ...), branch_computations={%region_1.2_spmd, %region_2.7_spmd} | conditional | flops 66704850944 | bytes 294843040 | solution.py:1156
  187.3 5.8 %branch_back.1 = (bf16[8,2,128,128]{3,2,1,0:T(8,128)(2,1)}, f32[512,1024]{1,0:T(8,128)}, bf16[512,1024]{1,0:T(8,128)(2,1)}, f32[1,1024]{1,0:T(1,128)}) custom-call(bf16[512,1024]{1,0:T(8,128)(2,1)S(1)} %get-tuple-element.65.own_ref, bf16[512,1024]{1,0:T(8,128)(2,1)} %get-tuple-element.66.other_ref, f32[512,1024]{1,0:T(8,128)} %get-tuple-element.58.hidden_ref, ...), custom_call_target="tpu_custom_call" | custom-call | flops 6000000000 | bytes 12000000 | tf_op jit(solution)/shard_map/cond/branch_1_fun/branch_back/pallas_call | solution.py:733
  193.1 10.9 %all-to-all-start = ((bf16[16,128,128]{2,1,0:T(8,128)(2,1)}), bf16[16,128,128]{2,1,0:T(8,128)(2,1)S(1)}, u32[]{:S(2)}, u32[]{:S(2)}) async-start(bf16[16,128,128]{2,1,0:T(8,128)(2,1)} %bitcast.59), calls=%async_computation | async-start | bytes 1048576 | tf_op jit(solution)/shard_map/cond/branch_1_fun/all_to_all | solution.py:1102
  209.7 17.3 %all-to-all-done.grad_ref = bf16[16,128,128]{2,1,0:T(8,128)(2,1)S(1)} async-done(((bf16[16,128,128]{2,1,0:T(8,128)(2,1)}), bf16[16,128,128]{2,1,0:T(8,128)(2,1)S(1)}, u32[]{:S(2)}, u32[]{:S(2)}) %all-to-all-start) | async-done | bytes 524320 | tf_op jit(solution)/shard_map/cond/branch_1_fun/all_to_all | solution.py:1102
  227.9 36.8 %attend_back.1 = (bf16[16,128,128]{2,1,0:T(8,128)(2,1)}, f32[16,256,128]{2,1,0:T(8,128)}, bf16[16,256,128]{2,1,0:T(8,128)(2,1)}) custom-call(s32[16]{0:T(128)S(1)} %get-tuple-element.60.parents_ref, s32[16]{0:T(128)S(1)} %get-tuple-element.61.assign_ref, s32[1]{0:T(128)} %get-tuple-element.62.part_ref, bf16[16,384,128]{2,1,0:T(8,128)(2,1)} %get-tuple-element.63.recv_ref, ...), custom_call_target="tpu_custom_call" | custom-call | flops 36999999488 | bytes 74000000 | tf_op jit(solution)/shard_map/cond/branch_1_fun/attend_back/pallas_call | solution.py:639
  271.8 8.8 %fold.1 = (bf16[16,384,128]{2,1,0:T(8,128)(2,1)}, bf16[16,256,256]{2,1,0:T(8,128)(2,1)}) custom-call(f32[16,256,128]{2,1,0:T(8,128)} %get-tuple-element.77.mine_ref, bf16[16,256,128]{2,1,0:T(8,128)(2,1)} %collective-permute-done.1.arrived_ref, bf16[16,128,128]{2,1,0:T(8,128)(2,1)} %get-tuple-element.79.dq_ref, f32[256,128]{1,0:T(8,128)} %get-tuple-element.207.cos_ref, ...), custom_call_target="tpu_custom_call" | custom-call | flops 8999999488 | bytes 18000000 | tf_op jit(solution)/shard_map/cond/branch_1_fun/fold/pallas_call | solution.py:779
  280.6 12.1 %all-to-all-done.2 = bf16[8,32,1024]{2,1,0:T(8,128)(2,1)S(1)} async-done(((bf16[8,32,1024]{2,1,0:T(8,128)(2,1)}), bf16[8,32,1024]{2,1,0:T(8,128)(2,1)S(1)}, u32[]{:S(2)}, u32[]{:S(2)}) %all-to-all-start.2) | async-done | bytes 524320 | tf_op jit(solution)/shard_map/cond/branch_1_fun/all_to_all | solution.py:915
  308.8 32.4 %all-to-all-done.1.recv_ref = bf16[16,384,128]{2,1,0:T(8,128)(2,1)} async-done(((bf16[16,384,128]{2,1,0:T(8,128)(2,1)}), bf16[16,384,128]{2,1,0:T(8,128)(2,1)}, u32[]{:S(2)}, u32[]{:S(2)}) %all-to-all-start.1) | async-done | bytes 1572896 | tf_op jit(solution)/shard_map/cond/branch_1_fun/all_to_all | solution.py:1121
  341.2 5.6 %unproject.1 = (f32[512,512]{1,0:T(8,128)}, bf16[512,1024]{1,0:T(8,128)(2,1)}) custom-call(bf16[16,384,128]{2,1,0:T(8,128)(2,1)} %all-to-all-done.1.recv_ref, bf16[1024,512]{1,0:T(8,128)(2,1)} %get-tuple-element.91.wq_ref, bf16[1024,512]{1,0:T(8,128)(2,1)} %get-tuple-element.92.wk_ref, bf16[1024,512]{1,0:T(8,128)(2,1)} %get-tuple-element.93.wv_ref), custom_call_target="tpu_custom_call" | custom-call | flops 6000000000 | bytes 12000000 | tf_op jit(solution)/shard_map/cond/branch_1_fun/unproject/pallas_call | solution.py:820
  347.9 10.6 %all-to-all-start.3 = ((bf16[4,128,1024]{2,1,0:T(8,128)(2,1)}), bf16[4,128,1024]{2,1,0:T(8,128)(2,1)S(1)}, u32[]{:S(2)}, u32[]{:S(2)}) async-start(bf16[4,128,1024]{2,1,0:T(8,128)(2,1)} %broadcast_in_dim.12), calls=%async_computation.3 | async-start | bytes 2097152 | tf_op jit(solution)/shard_map/cond/branch_1_fun/all_to_all | solution.py:928
  360.0 23.8 %collective-permute-done.4 = bf16[512,1024]{1,0:T(8,128)(2,1)} collective-permute-done((bf16[512,1024]{1,0:T(8,128)(2,1)}, bf16[512,1024]{1,0:T(8,128)(2,1)}, u32[]{:S(2)}, u32[]{:S(2)}) %collective-permute-start.4) | collective-permute-done | bytes 1048608 | tf_op jit(solution)/shard_map/cond/branch_1_fun/ppermute | solution.py:888
  383.7 12.3 %all-to-all-done.3 = bf16[4,128,1024]{2,1,0:T(8,128)(2,1)S(1)} async-done(((bf16[4,128,1024]{2,1,0:T(8,128)(2,1)}), bf16[4,128,1024]{2,1,0:T(8,128)(2,1)S(1)}, u32[]{:S(2)}, u32[]{:S(2)}) %all-to-all-start.3) | async-done | bytes 1048608 | tf_op jit(solution)/shard_map/cond/branch_1_fun/all_to_all | solution.py:928
  397.4 21.8 %collective-permute-done.10 = bf16[4,128,1024]{2,1,0:T(8,128)(2,1)} collective-permute-done((bf16[4,128,1024]{2,1,0:T(8,128)(2,1)S(1)}, bf16[4,128,1024]{2,1,0:T(8,128)(2,1)}, u32[]{:S(2)}, u32[]{:S(2)}) %collective-permute-start.10) | collective-permute-done | bytes 1048608 | tf_op jit(solution)/shard_map/cond/branch_1_fun/ppermute | solution.py:892
  442.7 7.3 %finish.1 = (f32[1024,512]{1,0:T(8,128)}, f32[1024,512]{1,0:T(8,128)}, f32[1024,512]{1,0:T(8,128)}, f32[512,1024]{1,0:T(8,128)}) custom-call(s32[1]{0:T(128)} %get-tuple-element.62.part_ref, bf16[8,128,1024]{2,1,0:T(8,128)(2,1)} %bitcast.54, bf16[8,128,1024]{2,1,0:T(8,128)(2,1)} %collective-permute-done.11.other_ref), custom_call_target="tpu_custom_call" | custom-call | flops 6000000000 | bytes 12000000 | tf_op jit(solution)/shard_map/cond/branch_1_fun/finish/pallas_call | solution.py:875
  (151 shorter events, 120.4 us)
Async XLA Ops:
  18.6 39.5 %all-to-all-start.4 = ((bf16[16,384,128]{2,1,0:T(8,128)(2,1)}), bf16[16,384,128]{2,1,0:T(8,128)(2,1)}, u32[]{:S(2)}, u32[]{:S(2)}) async-start(bf16[16,384,128]{2,1,0:T(8,128)(2,1)} %bitcast.56), calls=%async_computation.4 | async-start | bytes 3145728 | tf_op jit(solution)/shard_map/all_to_all | solution.py:1048
  26.0 142.5 %all-gather.2.cloned.1.call-start = ((), (), s32[]{:S(2)}) async-start(), calls=%async_computation.6 | async-start | bytes 4718592 | tf_op jit(solution)/shard_map/all_gather | solution.py:1059
  28.2 2.3 collective-permute-start.12
  60.4 3.4 collective-permute-start.13
  93.8 31.9 %all-to-all-start.5 = ((bf16[16,128,128]{2,1,0:T(8,128)(2,1)}), bf16[16,128,128]{2,1,0:T(8,128)(2,1)}, u32[]{:S(2)}, u32[]{:S(2)}) async-start(bf16[16,128,128]{2,1,0:T(8,128)(2,1)} %get-tuple-element.150), calls=%async_computation.5 | async-start | bytes 1048576 | tf_op jit(solution)/shard_map/all_to_all | solution.py:1065
  102.6 347.7 %all-reduce.3.cloned.1.call-start = ((), (), s32[]{:S(2)}) async-start(), calls=%async_computation.7 | async-start | bytes 17301504 | tf_op jit(solution)/shard_map/psum | solution.py:1095
  103.2 30.3 %collective-permute-start.15 = (bf16[512,1024]{1,0:T(8,128)(2,1)}, bf16[512,1024]{1,0:T(8,128)(2,1)}, u32[]{:S(2)}, u32[]{:S(2)}) collective-permute-start(bf16[512,1024]{1,0:T(8,128)(2,1)} %w_own_ref.1), channel_id=1, source_target_pairs={{0,1},{1,0},{2,3},{3,2},{4,5},{5,4},{6,7},{7,6},{8,9},{9,8},{10,11... | collective-permute-start | bytes 3145736 | tf_op jit(solution)/shard_map/ppermute | solution.py:888
  125.7 14.5 %collective-permute-start.14 = (bf16[16,128,128]{2,1,0:T(8,128)(2,1)}, bf16[16,128,128]{2,1,0:T(8,128)(2,1)}, u32[]{:S(2)}, u32[]{:S(2)}) collective-permute-start(bf16[16,128,128]{2,1,0:T(8,128)(2,1)} %all-to-all-done.5.own_ref), channel_id=1, source_target_pairs={{0,1},{1,0},{2,3},{3,2},{4,5},{5,4},{6,7},{7,6},{8,9},{9,8},{10,11... | collective-permute-start | bytes 1572872 | tf_op jit(solution)/shard_map/ppermute | solution.py:888
  156.7 24.7 %collective-permute-start.16 = (bf16[512,1024]{1,0:T(8,128)(2,1)S(1)}, bf16[512,1024]{1,0:T(8,128)(2,1)}, u32[]{:S(2)}, u32[]{:S(2)}) collective-permute-start(bf16[512,1024]{1,0:T(8,128)(2,1)S(1)} %add_convert_fusion.2), channel_id=1, source_target_pairs={{0,1},{1,0},{2,3},{3,2},{4,5},{5,4},{6,7},{7,6},{8,9},{9,8},{10,11... | collective-permute-start | bytes 3145736 | tf_op jit(solution)/shard_map/ppermute | solution.py:888
  193.1 34.0 %all-to-all-start = ((bf16[16,128,128]{2,1,0:T(8,128)(2,1)}), bf16[16,128,128]{2,1,0:T(8,128)(2,1)S(1)}, u32[]{:S(2)}, u32[]{:S(2)}) async-start(bf16[16,128,128]{2,1,0:T(8,128)(2,1)} %bitcast.59), calls=%async_computation | async-start | bytes 1048576 | tf_op jit(solution)/shard_map/cond/branch_1_fun/all_to_all | solution.py:1102
  206.2 2.4 collective-permute-start
  206.7 95.1 %collective-permute-start.2 = (bf16[2048,1024]{1,0:T(8,128)(2,1)}, bf16[2048,1024]{1,0:T(8,128)(2,1)}, u32[]{:S(2)}, u32[]{:S(2)}) collective-permute-start(bf16[2048,1024]{1,0:T(8,128)(2,1)} %get-tuple-element.85), channel_id=1, source_target_pairs={{0,1},{1,0},{2,3},{3,2},{4,5},{5,4},{6,7},{7,6},{8,9},{9,8},{10,11... | collective-permute-start | bytes 12582920 | tf_op jit(solution)/shard_map/cond/branch_1_fun/ppermute | solution.py:888
  264.7 5.9 %collective-permute-start.1 = (bf16[16,256,128]{2,1,0:T(8,128)(2,1)}, bf16[16,256,128]{2,1,0:T(8,128)(2,1)}, u32[]{:S(2)}, u32[]{:S(2)}) collective-permute-start(bf16[16,256,128]{2,1,0:T(8,128)(2,1)} %get-tuple-element.78), channel_id=1, source_target_pairs={{0,2},{2,0},{4,6},{6,4},{8,10},{10,8},{12,14},{14,12},{16,18},{18,... | collective-permute-start | bytes 3145736 | tf_op jit(solution)/shard_map/cond/branch_1_fun/ppermute | solution.py:892
  266.9 25.9 %all-to-all-start.2 = ((bf16[8,32,1024]{2,1,0:T(8,128)(2,1)}), bf16[8,32,1024]{2,1,0:T(8,128)(2,1)S(1)}, u32[]{:S(2)}, u32[]{:S(2)}) async-start(bf16[8,32,1024]{2,1,0:T(8,128)(2,1)} %bitcast.7), calls=%async_computation.2 | async-start | bytes 1048576 | tf_op jit(solution)/shard_map/cond/branch_1_fun/all_to_all | solution.py:915
  292.8 48.5 %all-to-all-start.1 = ((bf16[16,384,128]{2,1,0:T(8,128)(2,1)}), bf16[16,384,128]{2,1,0:T(8,128)(2,1)}, u32[]{:S(2)}, u32[]{:S(2)}) async-start(bf16[16,384,128]{2,1,0:T(8,128)(2,1)} %get-tuple-element.84), calls=%async_computation.1 | async-start | bytes 3145728 | tf_op jit(solution)/shard_map/cond/branch_1_fun/all_to_all | solution.py:1121
  301.9 39.3 %collective-permute-start.3 = (bf16[512,1024]{1,0:T(8,128)(2,1)}, bf16[512,1024]{1,0:T(8,128)(2,1)}, u32[]{:S(2)}, u32[]{:S(2)}) collective-permute-start(bf16[512,1024]{1,0:T(8,128)(2,1)} %get-tuple-element.86), channel_id=1, source_target_pairs={{0,1},{1,0},{2,3},{3,2},{4,5},{5,4},{6,7},{7,6},{8,9},{9,8},{10,11... | collective-permute-start | bytes 3145736 | tf_op jit(solution)/shard_map/cond/branch_1_fun/ppermute | solution.py:888
  307.2 1.5 collective-permute-start.9
  347.9 48.1 %all-to-all-start.3 = ((bf16[4,128,1024]{2,1,0:T(8,128)(2,1)}), bf16[4,128,1024]{2,1,0:T(8,128)(2,1)S(1)}, u32[]{:S(2)}, u32[]{:S(2)}) async-start(bf16[4,128,1024]{2,1,0:T(8,128)(2,1)} %broadcast_in_dim.12), calls=%async_computation.3 | async-start | bytes 2097152 | tf_op jit(solution)/shard_map/cond/branch_1_fun/all_to_all | solution.py:928
  358.6 25.2 %collective-permute-start.4 = (bf16[512,1024]{1,0:T(8,128)(2,1)}, bf16[512,1024]{1,0:T(8,128)(2,1)}, u32[]{:S(2)}, u32[]{:S(2)}) collective-permute-start(bf16[512,1024]{1,0:T(8,128)(2,1)} %get-tuple-element.94), channel_id=1, source_target_pairs={{0,1},{1,0},{2,3},{3,2},{4,5},{5,4},{6,7},{7,6},{8,9},{9,8},{10,11... | collective-permute-start | bytes 3145736 | tf_op jit(solution)/shard_map/cond/branch_1_fun/ppermute | solution.py:888
  396.1 23.1 %collective-permute-start.10 = (bf16[4,128,1024]{2,1,0:T(8,128)(2,1)S(1)}, bf16[4,128,1024]{2,1,0:T(8,128)(2,1)}, u32[]{:S(2)}, u32[]{:S(2)}) collective-permute-start(bf16[4,128,1024]{2,1,0:T(8,128)(2,1)S(1)} %all-to-all-done.3), channel_id=1, source_target_pairs={{0,4},{2,6},{4,0},{6,2},{8,12},{10,14},{12,8},{14,10},{16,20},{18,... | collective-permute-start | bytes 3145736 | tf_op jit(solution)/shard_map/cond/branch_1_fun/ppermute | solution.py:892
  420.8 21.8 %collective-permute-start.11 = (bf16[8,128,1024]{2,1,0:T(8,128)(2,1)S(1)}, bf16[8,128,1024]{2,1,0:T(8,128)(2,1)}, u32[]{:S(2)}, u32[]{:S(2)}) collective-permute-start(bf16[8,128,1024]{2,1,0:T(8,128)(2,1)S(1)} %bitcast.53), channel_id=1, source_target_pairs={{0,2},{2,0},{4,6},{6,4},{8,10},{10,8},{12,14},{14,12},{16,18},{18,... | collective-permute-start | bytes 6291464 | tf_op jit(solution)/shard_map/cond/branch_1_fun/ppermute | solution.py:892
  425.7 4.3 collective-permute-start.6
  430.0 4.8 %collective-permute-start.7 = (f32[2,1024]{1,0:T(2,128)S(1)}, f32[2,1024]{1,0:T(2,128)S(1)}, u32[]{:S(2)}, u32[]{:S(2)}) collective-permute-start(f32[2,1024]{1,0:T(2,128)S(1)} %fusion.55), channel_id=1, source_target_pairs={{0,8},{2,10},{4,12},{6,14},{8,0},{10,2},{12,4},{14,6},{16,24},{18,... | collective-permute-start | bytes 24584 | tf_op jit(solution)/shard_map/cond/branch_1_fun/ppermute | solution.py:892
  434.8 4.5 collective-permute-start.8
  (29 other events, 396.0 us)
Sparse Core Ops, SparseCore 0:
  61.3 86.1 all-gather.1
  181.5 238.9 all-reduce.2

commit v3 on v2

--- a/solution.py
+++ b/solution.py
@@ -349,6 +349,7 @@
 wide = jnp.float32
 narrow = jnp.bfloat16
 vmem_bytes = 60 * 1024 * 1024
+safe_excess = 40.0
 
 
 def busy(microseconds):
@@ -450,7 +451,7 @@
     )(inputs, norm_attn.reshape(1, width), first_values, cosine, sine, w_query, w_key, w_value)
 
 
-def tree_walk(run, count):
+def tree_walk(run, count, unroll):
     for base in range(0, count, TREE):
         at = 0
         while at < TREE:
@@ -465,7 +466,7 @@
                     run(start + i, depth)
                     return carry
 
-                lax.fori_loop(0, same, step, 0)
+                lax.fori_loop(0, same, step, 0, unroll=unroll)
             at += same
 
 
@@ -519,38 +520,91 @@
     return key_row <= query_row
 
 
+def fold_rows(values, combine):
+    blocks = values.reshape(values.shape[0] // 8, 8, values.shape[1])
+    return combine(blocks, axis=0)
+
+
 def attend_kernel(
-    parents_ref, assign_ref, part_ref, recv_ref, other_ref, send_ref, ot_ref, log_ref, kv_ref, vt_ref
+    parents_ref,
+    assign_ref,
+    part_ref,
+    recv_ref,
+    other_ref,
+    send_ref,
+    ot_ref,
+    log_ref,
+    kv_ref,
+    vt_ref,
+    excess_ref,
 ):
     part = part_ref[0]
     rows = other_ref.shape[1]
+    count = recv_ref.shape[0]
     gather_parts(part, recv_ref, other_ref, kv_ref, vt_ref, slice(HEAD_DIM, LANES))
+    excess_ref[...] = jnp.zeros_like(excess_ref)
+
+    def own_scores(own, query):
+        block = dot_rows(kv_ref[own], query)
+        return jnp.where(visible(part, SEG, rows), block, masked_score)
+
+    def store(own, peak, total, mixed):
+        mixed = mixed / total
+        ot_ref[own] = mixed
+        log_ref[own] = jnp.broadcast_to(peak + jnp.log(total), (8, rows))
+        send_ref[own] = pack_columns(mixed).astype(narrow)
 
     def run(segment, depth):
         slots = path_of(parents_ref, assign_ref, segment, depth)
         own = slots[0]
         query = unpack_low(recv_ref[own, rows:, :])
-        scores = []
-        for level, slot in enumerate(slots):
+        block = own_scores(own, query)
+        peak = jnp.max(block, axis=0, keepdims=True)
+        weight = jnp.exp(block - peak)
+        total = fold_rows(weight, jnp.sum)
+        mixed = dot_wide(vt_ref[own], weight.astype(narrow))
+        crest = jnp.broadcast_to(peak, (8, rows))
+        for slot in slots[1:]:
             block = dot_rows(kv_ref[slot], query)
-            if level == 0:
-                block = jnp.where(visible(part, SEG, rows), block, masked_score)
-            scores.append(block)
-        peak = jnp.max(scores[0], axis=0, keepdims=True)
-        for block in scores[1:]:
-            peak = jnp.maximum(peak, jnp.max(block, axis=0, keepdims=True))
-        total = jnp.zeros_like(peak)
-        mixed = jnp.zeros((HEAD_DIM, rows), wide)
-        for block, slot in zip(scores, slots, strict=True):
+            crest = jnp.maximum(crest, fold_rows(block, jnp.max))
             weight = jnp.exp(block - peak)
-            total = total + jnp.sum(weight, axis=0, keepdims=True)
+            total = total + fold_rows(weight, jnp.sum)
             mixed = mixed + dot_wide(vt_ref[slot], weight.astype(narrow))
-        mixed = mixed / total
-        ot_ref[own] = mixed
-        log_ref[own] = jnp.broadcast_to(peak + jnp.log(total), (8, rows))
-        send_ref[own] = pack_columns(mixed).astype(narrow)
-
-    tree_walk(run, recv_ref.shape[0])
+        excess_ref[...] = jnp.maximum(excess_ref[...], crest - peak)
+        store(own, peak, jnp.sum(total, axis=0, keepdims=True), mixed)
+
+    tree_walk(run, count, 2)
+
+    @pl.when(jnp.max(excess_ref[...]) > safe_excess)
+    def _():
+        def again(segment, carry):
+            own = assign_ref[segment]
+            query = unpack_low(recv_ref[own, rows:, :])
+
+            def climb_up(state):
+                current, peak, total, mixed = state
+                current = parents_ref[current]
+                slot = assign_ref[current]
+                block = dot_rows(kv_ref[slot], query)
+                crest = jnp.maximum(peak, jnp.max(block, axis=0, keepdims=True))
+                fade = jnp.exp(peak - crest)
+                weight = jnp.exp(block - crest)
+                total = total * fade + jnp.sum(weight, axis=0, keepdims=True)
+                mixed = mixed * fade + dot_wide(vt_ref[slot], weight.astype(narrow))
+                return current, crest, total, mixed
+
+            block = own_scores(own, query)
+            peak = jnp.max(block, axis=0, keepdims=True)
+            weight = jnp.exp(block - peak)
+            total = jnp.sum(weight, axis=0, keepdims=True)
+            mixed = dot_wide(vt_ref[own], weight.astype(narrow))
+            _, peak, total, mixed = lax.while_loop(
+                lambda state: parents_ref[state[0]] >= 0, climb_up, (segment, peak, total, mixed)
+            )
+            store(own, peak, total, mixed)
+            return carry
+
+        lax.fori_loop(0, count, again, 0)
 
 
 def attend(parents, assignment, part, recv, other):
@@ -567,9 +621,10 @@
         scratch_shapes=[
             pltpu.VMEM((count, SEG, LANES), narrow),
             pltpu.VMEM((count, HEAD_DIM, SEG), narrow),
+            pltpu.VMEM((8, rows), wide),
         ],
         compiler_params=pltpu.CompilerParams(vmem_limit_bytes=vmem_bytes),
-        cost_estimate=busy(30),
+        cost_estimate=busy(22),
         name="attend",
     )(parents, assignment, part, recv, other)
 
@@ -623,7 +678,7 @@
             grad_query = grad_query + dot_wide(kt_ref[slot], grad_scores)
         dq_ref[own] = pack_columns(grad_query * (HEAD_DIM ** (-0.5))).astype(narrow)
 
-    tree_walk(run, count)
+    tree_walk(run, count, 1)
 
     def finish(slot, carry):
         mine_ref[slot] = sum_ref[slot, pl.ds(pl.multiple_of(part * rows, rows), rows), :]
@@ -703,10 +758,21 @@
 
 
 def branch_back_kernel(
-    own_ref, other_ref, hidden_ref, cot_ref, gain_ref, w_ref, send_ref, hidden_grad_ref, branch_ref, gain_grad_ref
+    own_ref,
+    early_ref,
+    late_ref,
+    hidden_ref,
+    cot_ref,
+    gain_ref,
+    w_ref,
+    send_ref,
+    hidden_grad_ref,
+    branch_ref,
+    gain_grad_ref,
 ):
     groups = 2
-    grad_normed = own_ref[...].astype(wide) + other_ref[...].astype(wide)
+    other = jnp.concatenate([early_ref[...], late_ref[...]], axis=0)
+    grad_normed = own_ref[...].astype(wide) + other.astype(wide)
     hidden = hidden_ref[...]
     back, gain_grad = norm_back(grad_normed, hidden, rms_scale(hidden), gain_ref[...].astype(wide))
     gain_grad_ref[...] = gain_grad[None]
@@ -726,13 +792,13 @@
                 send_ref[2 * pair + at, part] = tile.astype(narrow)
 
 
-def branch_back(own, other, hidden, cotangent, norm_ffn, w_out):
+def branch_back(own, early, late, hidden, cotangent, norm_ffn, w_out):
     tokens, width = hidden.shape
     local = w_out.shape[0]
     groups = 2
     return pl.pallas_call(
         branch_back_kernel,
-        in_specs=[whole_spec()] * 6,
+        in_specs=[whole_spec()] * 7,
         out_specs=[whole_spec()] * 4,
         out_shape=[
             jax.ShapeDtypeStruct((local // HEAD_DIM, groups, tokens // groups // 2, LANES), narrow),
@@ -743,7 +809,7 @@
         compiler_params=pltpu.CompilerParams(vmem_limit_bytes=vmem_bytes),
         cost_estimate=busy(6),
         name="branch_back",
-    )(own, other, hidden, cotangent, norm_ffn.reshape(1, width), w_out)
+    )(own, early, late, hidden, cotangent, norm_ffn.reshape(1, width), w_out)
 
 
 def fold_kernel(
@@ -771,7 +837,7 @@
         send_ref[slot, rows:, :] = jnp.where(low[:half], top, bottom).astype(narrow)
         return carry
 
-    lax.fori_loop(0, count, step, 0)
+    lax.fori_loop(0, count, step, 0, unroll=4)
 
 
 def fold(mine, arrived, grad_q, cosine, sine, slot_cos, slot_sin):
@@ -826,7 +892,7 @@
             jax.ShapeDtypeStruct((tokens, width), narrow),
         ],
         compiler_params=pltpu.CompilerParams(vmem_limit_bytes=vmem_bytes),
-        cost_estimate=busy(6),
+        cost_estimate=busy(60),
         name="unproject",
     )(recv, w_query, w_key, w_value)
 
@@ -922,22 +988,23 @@
     return to_chips(jnp.broadcast_to(values[None], (chips,) + values.shape), count)
 
 
-def spread_rows(values, before, place, count):
-    lines = [[z * 4 + rest for z in range(count // 4)] for rest in range(4)]
+def spread_line(copies, count):
     length = count // 4
-    along = lax.all_to_all(
-        jnp.broadcast_to(values[None], (length,) + values.shape),
+    return lax.all_to_all(
+        copies,
         "dp",
         split_axis=0,
         concat_axis=0,
         tiled=True,
-        axis_index_groups=lines,
-    )
-    along = after(along, before)
+        axis_index_groups=[[z * 4 + rest for z in range(length)] for rest in range(4)],
+    )
+
+
+def spread_pair(along, place, count):
     arrived = swap_bit(along, 2, count)
     high = (place // 2) % 2 == 1
     pair = jnp.stack([jnp.where(high, arrived, along), jnp.where(high, along, arrived)], axis=1)
-    return pair.reshape((2 * length,) + values.shape)
+    return pair.reshape((2 * along.shape[0],) + along.shape[1:])
 
 
 def gather_core(values, axis, place, count):
@@ -1080,7 +1147,7 @@
         jnp.einsum("tf,df->td", grad_gate, w_gate, preferred_element_type=wide)
         + jnp.einsum("tf,df->td", grad_up, w_up, preferred_element_type=wide)
     ).astype(narrow)
-    ffn_other = swap_tensor(ffn_partial)
+    ffn_early = swap_tensor(ffn_partial[: tokens // 2])
     ffn_grads = tuple(
         jnp.einsum(form, left, right, preferred_element_type=wide).astype(narrow)
         for form, left, right in (
@@ -1093,11 +1160,12 @@
 
     normed_own, *ffn_grads = lax.optimization_barrier((normed_own,) + ffn_grads)
     ffn_sums = lax.psum(tuple(ffn_grads), "dp")
-    ffn_other = after(ffn_other, *ffn_grads)
-
-    def way_back(ffn_other, normed_own):
+    ffn_early = after(ffn_early, *ffn_grads)
+
+    def way_back(ffn_early, normed_own):
+        ffn_late = swap_tensor(ffn_partial[tokens // 2 :])
         grad_send, grad_hidden, grad_branch, grad_gain_ffn = branch_back(
-            ffn_partial, ffn_other, hidden, cotangent, norm_ffn, w_out
+            ffn_partial, ffn_early, ffn_late, hidden, cotangent, norm_ffn, w_out
         )
         grad_recv = lax.all_to_all(
             grad_send.reshape(count, rows // 2, LANES), "dp", split_axis=0, concat_axis=0, tiled=True
@@ -1107,12 +1175,14 @@
         grad_recv, out_half = lax.optimization_barrier((grad_recv, out_half))
         chips = count // 2
         out_shares = to_chips(out_half.reshape(chips, local // count, width), count)
-        out_share = jnp.sum(out_shares.astype(wide), axis=0).astype(narrow)
         normed_other = swap_tensor(normed_own)
         feed_other = swap_tensor(after(feed_partial, normed_other))
 
         grad_q, mine, theirs = attend_back(
             parents, assignment, part_array, recv, other, grad_recv, ot, logs
+        )
+        grad_q, mine, theirs, out_shares = lax.optimization_barrier(
+            (grad_q, mine, theirs, out_shares)
         )
         arrived = swap_bit(theirs, 1, count)
         back_send, feats = fold(
@@ -1131,33 +1201,46 @@
         )
         head_grads = head_grads[: 3 * HEAD_DIM].astype(narrow)
         head_share = reduce_bit(head_grads, 1, place, count)
+        out_share = jnp.sum(out_shares.astype(wide), axis=0).astype(narrow)
         share = jnp.concatenate([head_share, out_share], axis=0)
-        back_recv, feed_other = lax.optimization_barrier((back_recv, feed_other))
+        copies = jnp.broadcast_to(share[None], (count // 4,) + share.shape)
+        back_recv, feed_other, copies = lax.optimization_barrier((back_recv, feed_other, copies))
         grad_first, attn_partial = unproject(back_recv, w_query, w_key, w_value)
         attn_other = swap_tensor(attn_partial)
-        spread_all = spread_rows(after(share, attn_partial), attn_other, place, count)
-        spread_other = swap_bit(spread_all, 1, count)
-
+        along = spread_line(copies, count)
+        spread_all = spread_pair(after(along, attn_partial), place, count)
         output = (hidden + (feed_partial.astype(wide) + feed_other.astype(wide))).astype(narrow)
-        inputs_wide = inputs.astype(wide)
-        grad_normed = attn_partial.astype(wide) + attn_other.astype(wide)
-        grad_input_norm, grad_gain_attn = norm_back(
-            grad_normed, inputs_wide, rms_scale(inputs_wide), norm_attn.astype(wide)
+        return (
+            output,
+            grad_hidden,
+            grad_gain_ffn,
+            grad_first,
+            attn_partial,
+            attn_other,
+            spread_all,
         )
-        grad_inputs = grad_hidden + grad_input_norm
-        gains = sum_small(jnp.stack([grad_gain_attn, grad_gain_ffn[0]]), count)
-        head_grads = finish(part_array, spread_all, spread_other, local)
-        return (output, grad_inputs, grad_first, gains) + tuple(head_grads)
 
     def no_tree(*operands):
         shapes = jax.eval_shape(way_back, *operands)
         return tuple(jnp.zeros(leaf.shape, leaf.dtype) for leaf in shapes)
 
-    output, grad_inputs, grad_first, gains, *head_grads = lax.cond(
-        parents[0] < 0, way_back, no_tree, ffn_other, normed_own
-    )
-    head_query, head_key, head_value, sum_w_out = head_grads
-    ffn_sums = [after(term, gains) for term in ffn_sums]
+    output, grad_hidden, grad_gain_ffn, grad_first, attn_partial, attn_other, spread_all = lax.cond(
+        parents[0] < 0, way_back, no_tree, ffn_early, normed_own
+    )
+    spread_other = swap_bit(spread_all, 1, count)
+    inputs_wide = inputs.astype(wide)
+    grad_normed = attn_partial.astype(wide) + attn_other.astype(wide)
+    grad_input_norm, grad_gain_attn = norm_back(
+        grad_normed, inputs_wide, rms_scale(inputs_wide), norm_attn.astype(wide)
+    )
+    grad_inputs = grad_hidden + grad_input_norm
+    gains = jnp.stack([grad_gain_attn, grad_gain_ffn[0]])
+    head_query, head_key, head_value, sum_w_out = finish(part_array, spread_all, spread_other, local)
+    gains = after(gains + swap_bit(gains, 1, count), sum_w_out)
+    sums = []
+    for at, term in enumerate(ffn_sums):
+        sums.append(after(term, grad_inputs, sum_w_out).astype(wide))
+        gains = after(gains + swap_bit(gains, 2 << at, count), sums[-1])
     return (
         output,
         grad_inputs,
@@ -1166,9 +1249,9 @@
         head_key,
         head_value,
         sum_w_out,
-        ffn_sums[0].astype(wide),
-        ffn_sums[1].astype(wide),
-        ffn_sums[2].astype(wide),
+        sums[0],
+        sums[1],
+        sums[2],
         gains[0],
         gains[1],
     )

time: 478 us -> 447 us (0.935)
  waiting for transfers between devices: 194 us -> 174 us
  Pallas kernels: 106 us -> 95.8 us
  local copies, waits for them, and re-layouts: 20.9 us -> 15.5 us
    all_to_all x1, waiting for transfers between devices: 32.4 us -> 6.88 us  [way_back(): lax.all_to_all(back_send, 'dp', split_axis=0, concat_axis=0, tiled=True)]
    all_to_all x1, waiting for transfers between devices: 12.3 us -> 31.2 us  [spread_line(): lax.all_to_all(copies, 'dp', split_axis=0, concat_axis=0, tiled=True, axi...]
    all_to_all x1, waiting for transfers between devices: 12.1 us -> 0.01 us  [to_chips(): lax.all_to_all(values, 'dp', split_axis=0, concat_axis=0, tiled=True, axi...]
    pallas_call x1, Pallas kernels: 30 us -> 21.1 us  [attend(): pl.pallas_call(attend_kernel, in_specs=[scalar_spec()] * 3 + [whole_spec(...]
    ppermute x6 -> x7, waiting for transfers between devices: 43.4 us -> 48.9 us  [swap_tensor(): return lax.ppermute(values, 'tensor', [(0, 1), (1, 0)])]
    ppermute x6 -> x7, starting transfers between devices: 9.3 us -> 10.5 us  [swap_tensor(): return lax.ppermute(values, 'tensor', [(0, 1), (1, 0)])]
  transfers between devices with their start and end apart: 25 -> 26, of which waited for: 17 -> 19; matrix products, arithmetic and copies ran while one was open for 14% -> 17% of each run, Pallas kernels for 21% -> 20%
where the time goes in v3:
time: 447 us; the launch traced here: 438 us
  waiting for transfers between devices  174 us (39%)
  Pallas kernels  95.8 us (21%)
  starting transfers between devices  63 us (14%)
  matrix products  41.1 us (9%)
  other arithmetic  33.9 us (8%)
  local copies, waits for them, and re-layouts  15.5 us (3%)
  between operations  14.6 us (3%)
    ppermute x7, waiting for transfers between devices, swap_tensor(): return lax.ppermute(values, 'tensor', [(0, 1), (1, 0)])  48.9 us
    pallas_call x1, Pallas kernels, attend_back(): pl.pallas_call(attend_back_kernel, in_specs=[scalar_spec()] * 3 + [whole_...  36.5 us
    all_to_all x1, waiting for transfers between devices, spread_line(): lax.all_to_all(copies, 'dp', split_axis=0, concat_axis=0, tiled=True, axi...  31.2 us
    ppermute x11, waiting for transfers between devices, swap_bit(): return lax.ppermute(values, 'dp', [(i, i ^ bit) for i in range(count)])  27.8 us
    all_to_all x1, waiting for transfers between devices, body_heads(): recv = lax.all_to_all(send, 'dp', split_axis=0, concat_axis=0, tiled=True)  24.5 us
    pallas_call x1, Pallas kernels, attend(): pl.pallas_call(attend_kernel, in_specs=[scalar_spec()] * 3 + [whole_spec(...  21.1 us
    all_to_all x1, waiting for transfers between devices, way_back(): lax.all_to_all(grad_send.reshape(count, rows // 2, LANES), 'dp', split_ax...  17.7 us
    all_to_all x1, waiting for transfers between devices, body_heads(): lax.all_to_all(packed, 'dp', split_axis=0, concat_axis=0, tiled=True)  17 us
  transfers between devices with their start and end apart: 26, of which 19 were waited for; matrix products, arithmetic and copies ran while one was open for 17% of the time, Pallas kernels for 20%

profile of v3, /device:TPU:0, one launch (start us, length us, event | category | flops | bytes accessed | tf_op | source)
XLA Modules:
  0.0 438.4 jit_solution(17044701251816437504)
XLA Ops:
  12.4 6.2 %project.1 = (bf16[8,2,384,128]{3,2,1,0:T(8,128)(2,1)}, bf16[512,1024]{1,0:T(8,128)(2,1)}) custom-call(bf16[512,1024]{1,0:T(8,128)(2,1)} %x_ref.3, bf16[1,1024]{1,0:T(2,128)(2,1)} %reshape.185.gain_ref, bf16[512,512]{1,0:T(8,128)(2,1)} %first_ref.1, f32[512,128]{1,0:T(8,128)} %get-tuple-element.224.cos_ref, f32[512,128]{1,0:T(8,128)} %get-tuple-element.223.sin_ref, ...), custom_call_target="tpu_custom_call" | custom-call | flops 6000000000 | bytes 12000000 | tf_op jit(solution)/shard_map/project/pallas_call | solution.py:427
  18.6 7.4 %all-to-all-start.4 = ((bf16[16,384,128]{2,1,0:T(8,128)(2,1)}), bf16[16,384,128]{2,1,0:T(8,128)(2,1)}, u32[]{:S(2)}, u32[]{:S(2)}) async-start(bf16[16,384,128]{2,1,0:T(8,128)(2,1)} %bitcast.54), calls=%async_computation.4 | async-start | bytes 3145728 | tf_op jit(solution)/shard_map/all_to_all | solution.py:1115
  33.6 24.5 %all-to-all-done.4.recv_ref = bf16[16,384,128]{2,1,0:T(8,128)(2,1)} async-done(((bf16[16,384,128]{2,1,0:T(8,128)(2,1)}), bf16[16,384,128]{2,1,0:T(8,128)(2,1)}, u32[]{:S(2)}, u32[]{:S(2)}) %all-to-all-start.4) | async-done | bytes 1572896 | tf_op jit(solution)/shard_map/all_to_all | solution.py:1115
  63.8 21.1 %attend.1 = (bf16[16,128,128]{2,1,0:T(8,128)(2,1)}, f32[16,64,256]{2,1,0:T(8,128)}, f32[16,8,256]{2,1,0:T(8,128)S(1)}) custom-call(s32[16]{0:T(128)S(1)} %copy-done.19, s32[16]{0:T(128)S(1)} %copy-done.20, s32[1]{0:T(128)} %bitcast.12.part_ref, bf16[16,384,128]{2,1,0:T(8,128)(2,1)} %all-to-all-done.4.recv_ref, ...), custom_call_target="tpu_custom_call" | custom-call | flops 22000001024 | bytes 44000000 | tf_op jit(solution)/shard_map/attend/pallas_call | solution.py:612
  84.9 8.8 %all-to-all-start.5 = ((bf16[16,128,128]{2,1,0:T(8,128)(2,1)}), bf16[16,128,128]{2,1,0:T(8,128)(2,1)}, u32[]{:S(2)}, u32[]{:S(2)}) async-start(bf16[16,128,128]{2,1,0:T(8,128)(2,1)} %get-tuple-element.172), calls=%async_computation.5 | async-start | bytes 1048576 | tf_op jit(solution)/shard_map/all_to_all | solution.py:1132
  95.6 17.0 %all-to-all-done.5.own_ref = bf16[16,128,128]{2,1,0:T(8,128)(2,1)} async-done(((bf16[16,128,128]{2,1,0:T(8,128)(2,1)}), bf16[16,128,128]{2,1,0:T(8,128)(2,1)}, u32[]{:S(2)}, u32[]{:S(2)}) %all-to-all-start.5) | async-done | bytes 524320 | tf_op jit(solution)/shard_map/all_to_all | solution.py:1132
  114.7 5.6 %fusion.28 = f32[512,1408]{1,0:T(8,128)} fusion(bf16[512,1024]{1,0:T(8,128)(2,1)} %param.28, bf16[1408,1024]{1,0:T(8,128)(2,1)} %param.25), kind=kOutput, calls=%fused_computation.76 | convolution fusion | flops 1476395008 | bytes 6815744 | tf_op jit(solution)/shard_map/td,fd->tf/dot_general | solution.py:1140
  120.4 10.6 %collective-permute-done.10.other_ref = bf16[16,128,128]{2,1,0:T(8,128)(2,1)S(1)} collective-permute-done((bf16[16,128,128]{2,1,0:T(8,128)(2,1)}, bf16[16,128,128]{2,1,0:T(8,128)(2,1)S(1)}, u32[]{:S(2)}, u32[]{:S(2)}) %collective-permute-start.10) | collective-permute-done | bytes 524320 | tf_op jit(solution)/shard_map/ppermute | solution.py:954
  131.7 5.6 %merge.1 = (bf16[512,512]{1,0:T(8,128)(2,1)}, f32[512,1024]{1,0:T(8,128)}, bf16[512,1024]{1,0:T(8,128)(2,1)}) custom-call(bf16[16,128,128]{2,1,0:T(8,128)(2,1)} %all-to-all-done.5.own_ref, bf16[16,128,128]{2,1,0:T(8,128)(2,1)} %copy-done.18, bf16[512,1024]{1,0:T(8,128)(2,1)} %w_own_ref.1, bf16[512,1024]{1,0:T(8,128)(2,1)} %collective-permute-done.11.w_other_ref, ...), custom_call_target="tpu_custom_call" | custom-call | flops 6000000000 | bytes 12000000 | tf_op jit(solution)/shard_map/merge/pallas_call | solution.py:745
  167.3 232.8 %conditional.1 = (bf16[512,1024]{1,0:T(8,128)(2,1)}, f32[512,1024]{1,0:T(8,128)}, f32[1,1024]{1,0:T(1,128)S(1)}, f32[512,512]{1,0:T(8,128)}, bf16[8,128,1024]{2,...) conditional(s32[]{:T(128)} %bitcast.11, () %tuple.35, (bf16[512,1024]{1,0:T(8,128)(2,1)}, ...), branch_computations={%region_1.2_spmd, %region_2.4_spmd} | conditional | flops 114693832704 | bytes 365336384 | solution.py:1227
  170.7 10.6 %collective-permute-done.late_ref = bf16[256,1024]{1,0:T(8,128)(2,1)} collective-permute-done((bf16[256,1024]{1,0:T(8,128)(2,1)S(1)}, bf16[256,1024]{1,0:T(8,128)(2,1)}, u32[]{:S(2)}, u32[]{:S(2)}) %collective-permute-start) | collective-permute-done | bytes 524320 | tf_op jit(solution)/shard_map/cond/branch_1_fun/ppermute | solution.py:954
  181.2 5.8 %branch_back.1 = (bf16[8,2,128,128]{3,2,1,0:T(8,128)(2,1)}, f32[512,1024]{1,0:T(8,128)}, bf16[512,1024]{1,0:T(8,128)(2,1)}, f32[1,1024]{1,0:T(1,128)S(1)}) custom-call(bf16[512,1024]{1,0:T(8,128)(2,1)} %get-tuple-element.83.own_ref, bf16[256,1024]{1,0:T(8,128)(2,1)S(1)} %get-tuple-element.84.early_ref, bf16[256,1024]{1,0:T(8,128)(2,1)} %collective-permute-done.late_ref, ...), custom_call_target="tpu_custom_call" | custom-call | flops 6000000000 | bytes 12000000 | tf_op jit(solution)/shard_map/cond/branch_1_fun/branch_back/pallas_call | solution.py:799
  187.0 7.7 %all-to-all-start = ((bf16[16,128,128]{2,1,0:T(8,128)(2,1)}), bf16[16,128,128]{2,1,0:T(8,128)(2,1)S(1)}, u32[]{:S(2)}, u32[]{:S(2)}) async-start(bf16[16,128,128]{2,1,0:T(8,128)(2,1)} %bitcast.57), calls=%async_computation | async-start | bytes 1048576 | tf_op jit(solution)/shard_map/cond/branch_1_fun/all_to_all | solution.py:1170
  200.1 17.7 %all-to-all-done.grad_ref = bf16[16,128,128]{2,1,0:T(8,128)(2,1)S(1)} async-done(((bf16[16,128,128]{2,1,0:T(8,128)(2,1)}), bf16[16,128,128]{2,1,0:T(8,128)(2,1)S(1)}, u32[]{:S(2)}, u32[]{:S(2)}) %all-to-all-start) | async-done | bytes 524320 | tf_op jit(solution)/shard_map/cond/branch_1_fun/all_to_all | solution.py:1170
  222.5 36.5 %attend_back.1 = (bf16[16,128,128]{2,1,0:T(8,128)(2,1)}, f32[16,256,128]{2,1,0:T(8,128)}, bf16[16,256,128]{2,1,0:T(8,128)(2,1)}) custom-call(s32[16]{0:T(128)S(1)} %get-tuple-element.78.parents_ref, s32[16]{0:T(128)S(1)} %get-tuple-element.79.assign_ref, s32[1]{0:T(128)} %get-tuple-element.80.part_ref, bf16[16,384,128]{2,1,0:T(8,128)(2,1)} %get-tuple-element.81.recv_ref, ...), custom_call_target="tpu_custom_call" | custom-call | flops 36999999488 | bytes 74000000 | tf_op jit(solution)/shard_map/cond/branch_1_fun/attend_back/pallas_call | solution.py:694
  263.3 8.0 %fold.1 = (bf16[16,384,128]{2,1,0:T(8,128)(2,1)}, bf16[16,256,256]{2,1,0:T(8,128)(2,1)}) custom-call(f32[16,256,128]{2,1,0:T(8,128)} %get-tuple-element.99.mine_ref, bf16[16,256,128]{2,1,0:T(8,128)(2,1)} %copy-done.17, bf16[16,128,128]{2,1,0:T(8,128)(2,1)} %get-tuple-element.101.dq_ref, f32[256,128]{1,0:T(8,128)} %get-tuple-element.213.cos_ref, ...), custom_call_target="tpu_custom_call" | custom-call | flops 8999999488 | bytes 18000000 | tf_op jit(solution)/shard_map/cond/branch_1_fun/fold/pallas_call | solution.py:845
  271.3 6.2 %all-to-all-start.2 = ((bf16[16,384,128]{2,1,0:T(8,128)(2,1)}), bf16[16,384,128]{2,1,0:T(8,128)(2,1)}, u32[]{:S(2)}, u32[]{:S(2)}) async-start(bf16[16,384,128]{2,1,0:T(8,128)(2,1)} %get-tuple-element.108), calls=%async_computation.2 | async-start | bytes 3145728 | tf_op jit(solution)/shard_map/cond/branch_1_fun/all_to_all | solution.py:1191
  281.6 8.6 %collective-permute-done.3 = bf16[2048,1024]{1,0:T(8,128)(2,1)} collective-permute-done((bf16[2048,1024]{1,0:T(8,128)(2,1)}, bf16[2048,1024]{1,0:T(8,128)(2,1)}, u32[]{:S(2)}, u32[]{:S(2)}) %collective-permute-start.3) | collective-permute-done | bytes 4194336 | tf_op jit(solution)/shard_map/cond/branch_1_fun/ppermute | solution.py:954
  296.8 17.8 %collective-permute-done.4 = bf16[512,1024]{1,0:T(8,128)(2,1)} collective-permute-done((bf16[512,1024]{1,0:T(8,128)(2,1)S(1)}, bf16[512,1024]{1,0:T(8,128)(2,1)}, u32[]{:S(2)}, u32[]{:S(2)}) %collective-permute-start.4) | collective-permute-done | bytes 1048608 | tf_op jit(solution)/shard_map/cond/branch_1_fun/ppermute | solution.py:954
  314.6 6.9 %all-to-all-done.2.recv_ref = bf16[16,384,128]{2,1,0:T(8,128)(2,1)} async-done(((bf16[16,384,128]{2,1,0:T(8,128)(2,1)}), bf16[16,384,128]{2,1,0:T(8,128)(2,1)}, u32[]{:S(2)}, u32[]{:S(2)}) %all-to-all-start.2) | async-done | bytes 1572896 | tf_op jit(solution)/shard_map/cond/branch_1_fun/all_to_all | solution.py:1191
  322.5 11.3 %all-to-all-start.3 = ((bf16[4,128,1024]{2,1,0:T(8,128)(2,1)}), bf16[4,128,1024]{2,1,0:T(8,128)(2,1)}, u32[]{:S(2)}, u32[]{:S(2)}) async-start(bf16[4,128,1024]{2,1,0:T(8,128)(2,1)} %broadcast_in_dim.18), calls=%async_computation.3 | async-start | bytes 2097152 | tf_op jit(solution)/shard_map/cond/branch_1_fun/all_to_all | solution.py:993
  340.7 31.2 %all-to-all-done.3 = bf16[4,128,1024]{2,1,0:T(8,128)(2,1)} async-done(((bf16[4,128,1024]{2,1,0:T(8,128)(2,1)}), bf16[4,128,1024]{2,1,0:T(8,128)(2,1)}, u32[]{:S(2)}, u32[]{:S(2)}) %all-to-all-start.3) | async-done | bytes 1048608 | tf_op jit(solution)/shard_map/cond/branch_1_fun/all_to_all | solution.py:993
  378.5 18.2 %collective-permute-done.6 = bf16[4,128,1024]{2,1,0:T(8,128)(2,1)} collective-permute-done((bf16[4,128,1024]{2,1,0:T(8,128)(2,1)}, bf16[4,128,1024]{2,1,0:T(8,128)(2,1)}, u32[]{:S(2)}, u32[]{:S(2)}) %collective-permute-start.6) | collective-permute-done | bytes 1048608 | tf_op jit(solution)/shard_map/cond/branch_1_fun/ppermute | solution.py:958
  404.7 7.1 %finish.1 = (f32[1024,512]{1,0:T(8,128)}, f32[1024,512]{1,0:T(8,128)}, f32[1024,512]{1,0:T(8,128)}, f32[512,1024]{1,0:T(8,128)}) custom-call(s32[1]{0:T(128)} %bitcast.12.part_ref, bf16[8,128,1024]{2,1,0:T(8,128)(2,1)} %get-tuple-element.188.own_ref, bf16[8,128,1024]{2,1,0:T(8,128)(2,1)} %collective-permute-done.13.other_ref), custom_call_target="tpu_custom_call" | custom-call | flops 6000000000 | bytes 12000000 | tf_op jit(solution)/shard_map/finish/pallas_call | solution.py:941
  (150 shorter events, 122.9 us)
Async XLA Ops:
  18.6 39.5 %all-to-all-start.4 = ((bf16[16,384,128]{2,1,0:T(8,128)(2,1)}), bf16[16,384,128]{2,1,0:T(8,128)(2,1)}, u32[]{:S(2)}, u32[]{:S(2)}) async-start(bf16[16,384,128]{2,1,0:T(8,128)(2,1)} %bitcast.54), calls=%async_computation.4 | async-start | bytes 3145728 | tf_op jit(solution)/shard_map/all_to_all | solution.py:1115
  26.0 134.8 %all-gather.2.cloned.1.call-start = ((), (), s32[]{:S(2)}) async-start(), calls=%async_computation.6 | async-start | bytes 4718592 | tf_op jit(solution)/shard_map/all_gather | solution.py:1126
  28.3 2.3 collective-permute-start.8
  60.4 3.4 collective-permute-start.9
  84.9 27.7 %all-to-all-start.5 = ((bf16[16,128,128]{2,1,0:T(8,128)(2,1)}), bf16[16,128,128]{2,1,0:T(8,128)(2,1)}, u32[]{:S(2)}, u32[]{:S(2)}) async-start(bf16[16,128,128]{2,1,0:T(8,128)(2,1)} %get-tuple-element.172), calls=%async_computation.5 | async-start | bytes 1048576 | tf_op jit(solution)/shard_map/all_to_all | solution.py:1132
  93.7 322.0 %all-reduce.3.cloned.1.call-start = ((), (), s32[]{:S(2)}) async-start(), calls=%async_computation.7 | async-start | bytes 17301504 | tf_op jit(solution)/shard_map/psum | solution.py:1162
  94.0 26.4 %collective-permute-start.11 = (bf16[512,1024]{1,0:T(8,128)(2,1)}, bf16[512,1024]{1,0:T(8,128)(2,1)}, u32[]{:S(2)}, u32[]{:S(2)}) collective-permute-start(bf16[512,1024]{1,0:T(8,128)(2,1)} %w_own_ref.1), channel_id=1, source_target_pairs={{0,1},{1,0},{2,3},{3,2},{4,5},{5,4},{6,7},{7,6},{8,9},{9,8},{10,11... | collective-permute-start | bytes 3145736 | tf_op jit(solution)/shard_map/ppermute | solution.py:954
  112.6 18.3 %collective-permute-start.10 = (bf16[16,128,128]{2,1,0:T(8,128)(2,1)}, bf16[16,128,128]{2,1,0:T(8,128)(2,1)S(1)}, u32[]{:S(2)}, u32[]{:S(2)}) collective-permute-start(bf16[16,128,128]{2,1,0:T(8,128)(2,1)} %all-to-all-done.5.own_ref), channel_id=1, source_target_pairs={{0,1},{1,0},{2,3},{3,2},{4,5},{5,4},{6,7},{7,6},{8,9},{9,8},{10,11... | collective-permute-start | bytes 1572872 | tf_op jit(solution)/shard_map/ppermute | solution.py:954
  148.6 13.5 %collective-permute-start.12 = (bf16[256,1024]{1,0:T(8,128)(2,1)S(1)}, bf16[256,1024]{1,0:T(8,128)(2,1)S(1)}, u32[]{:S(2)}, u32[]{:S(2)}) collective-permute-start(bf16[256,1024]{1,0:T(8,128)(2,1)S(1)} %slice.29), channel_id=1, source_target_pairs={{0,1},{1,0},{2,3},{3,2},{4,5},{5,4},{6,7},{7,6},{8,9},{9,8},{10,11... | collective-permute-start | bytes 1572872 | tf_op jit(solution)/shard_map/ppermute | solution.py:954
  168.5 12.7 %collective-permute-start = (bf16[256,1024]{1,0:T(8,128)(2,1)S(1)}, bf16[256,1024]{1,0:T(8,128)(2,1)}, u32[]{:S(2)}, u32[]{:S(2)}) collective-permute-start(bf16[256,1024]{1,0:T(8,128)(2,1)S(1)} %slice.15), channel_id=1, source_target_pairs={{0,1},{1,0},{2,3},{3,2},{4,5},{5,4},{6,7},{7,6},{8,9},{9,8},{10,11... | collective-permute-start | bytes 1572872 | tf_op jit(solution)/shard_map/cond/branch_1_fun/ppermute | solution.py:954
  187.0 30.8 %all-to-all-start = ((bf16[16,128,128]{2,1,0:T(8,128)(2,1)}), bf16[16,128,128]{2,1,0:T(8,128)(2,1)S(1)}, u32[]{:S(2)}, u32[]{:S(2)}) async-start(bf16[16,128,128]{2,1,0:T(8,128)(2,1)} %bitcast.57), calls=%async_computation | async-start | bytes 1048576 | tf_op jit(solution)/shard_map/cond/branch_1_fun/all_to_all | solution.py:1170
  197.3 92.9 %collective-permute-start.3 = (bf16[2048,1024]{1,0:T(8,128)(2,1)}, bf16[2048,1024]{1,0:T(8,128)(2,1)}, u32[]{:S(2)}, u32[]{:S(2)}) collective-permute-start(bf16[2048,1024]{1,0:T(8,128)(2,1)} %get-tuple-element.109), channel_id=1, source_target_pairs={{0,1},{1,0},{2,3},{3,2},{4,5},{5,4},{6,7},{7,6},{8,9},{9,8},{10,11... | collective-permute-start | bytes 12582920 | tf_op jit(solution)/shard_map/cond/branch_1_fun/ppermute | solution.py:954
  218.8 40.2 %all-to-all-start.1 = ((bf16[8,32,1024]{2,1,0:T(8,128)(2,1)}), bf16[8,32,1024]{2,1,0:T(8,128)(2,1)S(1)}, u32[]{:S(2)}, u32[]{:S(2)}) async-start(bf16[8,32,1024]{2,1,0:T(8,128)(2,1)} %bitcast.3), calls=%async_computation.1 | async-start | bytes 1048576 | tf_op jit(solution)/shard_map/cond/branch_1_fun/all_to_all | solution.py:981
  259.1 2.9 collective-permute-start.2
  271.3 50.1 %all-to-all-start.2 = ((bf16[16,384,128]{2,1,0:T(8,128)(2,1)}), bf16[16,384,128]{2,1,0:T(8,128)(2,1)}, u32[]{:S(2)}, u32[]{:S(2)}) async-start(bf16[16,384,128]{2,1,0:T(8,128)(2,1)} %get-tuple-element.108), calls=%async_computation.2 | async-start | bytes 3145728 | tf_op jit(solution)/shard_map/cond/branch_1_fun/all_to_all | solution.py:1191
  290.1 24.4 %collective-permute-start.4 = (bf16[512,1024]{1,0:T(8,128)(2,1)S(1)}, bf16[512,1024]{1,0:T(8,128)(2,1)}, u32[]{:S(2)}, u32[]{:S(2)}) collective-permute-start(bf16[512,1024]{1,0:T(8,128)(2,1)S(1)} %copy-done.9), channel_id=1, source_target_pairs={{0,1},{1,0},{2,3},{3,2},{4,5},{5,4},{6,7},{7,6},{8,9},{9,8},{10,11... | collective-permute-start | bytes 3145736 | tf_op jit(solution)/shard_map/cond/branch_1_fun/ppermute | solution.py:954
  322.5 49.4 %all-to-all-start.3 = ((bf16[4,128,1024]{2,1,0:T(8,128)(2,1)}), bf16[4,128,1024]{2,1,0:T(8,128)(2,1)}, u32[]{:S(2)}, u32[]{:S(2)}) async-start(bf16[4,128,1024]{2,1,0:T(8,128)(2,1)} %broadcast_in_dim.18), calls=%async_computation.3 | async-start | bytes 2097152 | tf_op jit(solution)/shard_map/cond/branch_1_fun/all_to_all | solution.py:993
  339.2 36.2 %collective-permute-start.7 = (bf16[512,1024]{1,0:T(8,128)(2,1)}, bf16[512,1024]{1,0:T(8,128)(2,1)}, u32[]{:S(2)}, u32[]{:S(2)}) collective-permute-start(bf16[512,1024]{1,0:T(8,128)(2,1)} %get-tuple-element.123), channel_id=1, source_target_pairs={{0,1},{1,0},{2,3},{3,2},{4,5},{5,4},{6,7},{7,6},{8,9},{9,8},{10,11... | collective-permute-start | bytes 3145736 | tf_op jit(solution)/shard_map/cond/branch_1_fun/ppermute | solution.py:954
  371.9 24.7 %collective-permute-start.6 = (bf16[4,128,1024]{2,1,0:T(8,128)(2,1)}, bf16[4,128,1024]{2,1,0:T(8,128)(2,1)}, u32[]{:S(2)}, u32[]{:S(2)}) collective-permute-start(bf16[4,128,1024]{2,1,0:T(8,128)(2,1)} %all-to-all-done.3), channel_id=1, source_target_pairs={{0,4},{2,6},{4,0},{6,2},{8,12},{10,14},{12,8},{14,10},{16,20},{18,... | collective-permute-start | bytes 3145736 | tf_op jit(solution)/shard_map/cond/branch_1_fun/ppermute | solution.py:958
  400.1 4.6 %collective-permute-start.13 = (bf16[8,128,1024]{2,1,0:T(8,128)(2,1)}, bf16[8,128,1024]{2,1,0:T(8,128)(2,1)}, u32[]{:S(2)}, u32[]{:S(2)}) collective-permute-start(bf16[8,128,1024]{2,1,0:T(8,128)(2,1)} %get-tuple-element.188.own_ref), channel_id=1, source_target_pairs={{0,2},{2,0},{4,6},{6,4},{8,10},{10,8},{12,14},{14,12},{16,18},{18,... | collective-permute-start | bytes 6291464 | tf_op jit(solution)/shard_map/ppermute | solution.py:958
  401.3 3.1 collective-permute-start.14
  411.8 3.8 collective-permute-start.15
  420.5 4.8 %collective-permute-start.16 = (f32[2,1024]{1,0:T(2,128)S(1)}, f32[2,1024]{1,0:T(2,128)S(1)}, u32[]{:S(2)}, u32[]{:S(2)}) collective-permute-start(f32[2,1024]{1,0:T(2,128)S(1)} %add.174), channel_id=1, source_target_pairs={{0,8},{2,10},{4,12},{6,14},{8,0},{10,2},{12,4},{14,6},{16,24},{18,... | collective-permute-start | bytes 24584 | tf_op jit(solution)/shard_map/ppermute | solution.py:958
  425.3 5.3 %collective-permute-start.17 = (f32[2,1024]{1,0:T(2,128)S(1)}, f32[2,1024]{1,0:T(2,128)S(1)}, u32[]{:S(2)}, u32[]{:S(2)}) collective-permute-start(f32[2,1024]{1,0:T(2,128)S(1)} %add.175), channel_id=1, source_target_pairs={{0,16},{2,18},{4,20},{6,22},{8,24},{10,26},{12,28},{14,30},{16,0},... | collective-permute-start | bytes 24584 | tf_op jit(solution)/shard_map/ppermute | solution.py:958
  (28 other events, 876.6 us)
Sparse Core Ops, SparseCore 0:
  61.3 81.7 all-gather.1
  162.3 238.4 all-reduce.2

commit v4 on v3

--- a/solution.py
+++ b/solution.py
@@ -1,5 +1,6 @@
 import jax
 import jax.numpy as jnp
+import numpy as np
 from jax import lax
 from jax.experimental import pallas as pl
 from jax.experimental.pallas import tpu as pltpu
@@ -377,6 +378,36 @@
     return values * cosine + other * signed_sine
 
 
+def turn_constants():
+    half = HEAD_DIM // 2
+    lanes = np.arange(LANES)
+    frequency = rope_base ** (-(lanes % half).astype(np.float64) * 2.0 / HEAD_DIM)
+    sign = np.where(lanes % HEAD_DIM < half, -1.0, 1.0)
+    levels = -(-(climb_steps + 1) // 8) * 8
+    at = np.concatenate([np.arange(16), 16 * np.arange(SEG // 16), SEG * np.arange(levels)])
+    angles = at[:, None].astype(np.float64) * frequency[None, :]
+    return np.stack([np.cos(angles), np.sin(angles) * sign[None, :]]).astype(np.float32)
+
+
+def turn(one, other):
+    return one[0] * other[0] - one[1] * other[1], one[1] * other[0] + one[0] * other[1]
+
+
+def turn_rows(turn_ref, first, rows):
+    fine = turn_ref[0, :16, :], turn_ref[1, :16, :]
+    parts = []
+    for block in range(rows // 16):
+        at = 16 + first // 16 + block
+        coarse = turn_ref[0, pl.ds(at, 1), :], turn_ref[1, pl.ds(at, 1), :]
+        parts.append(turn(fine, coarse))
+    return tuple(jnp.concatenate(pieces, axis=0) for pieces in zip(*parts, strict=True))
+
+
+def turn_depth(turn_ref, depth_pos):
+    at = 16 + SEG // 16 + depth_pos // SEG
+    return turn_ref[0, pl.ds(at, 1), :], turn_ref[1, pl.ds(at, 1), :]
+
+
 def dot_wide(left, right):
     return jnp.dot(left, right, preferred_element_type=wide)
 
@@ -394,19 +425,29 @@
 
 
 def project_kernel(
-    x_ref, gain_ref, first_ref, cos_ref, sin_ref, wq_ref, wk_ref, wv_ref, send_ref, normed_ref
+    place_ref,
+    depth_ref,
+    x_ref,
+    gain_ref,
+    first_ref,
+    turn_ref,
+    wq_ref,
+    wk_ref,
+    wv_ref,
+    send_ref,
+    normed_ref,
 ):
     rows = x_ref.shape[0]
     pairs = first_ref.shape[1] // LANES
     x = x_ref[...].astype(wide)
-    normed = (x * rms_scale(x) * gain_ref[...].astype(wide)).astype(narrow)
+    normed = (x * rms_scale(x) * gain_ref[...].astype(wide)[None]).astype(narrow)
     normed_ref[...] = normed
     query = dot_wide(normed, wq_ref[...]) * (HEAD_DIM ** (-0.5))
     key = dot_wide(normed, wk_ref[...])
     value = dot_wide(normed, wv_ref[...])
     mixed = 0.5 * value + 0.5 * first_ref[...].astype(wide)
-    cosine = cos_ref[...]
-    sine = sin_ref[...]
+    local = turn_rows(turn_ref, pl.program_id(0) * rows, rows)
+    cosine, sine = turn(local, turn_depth(turn_ref, depth_ref[place_ref[0]]))
     for pair in range(pairs):
         cols = slice(pair * LANES, (pair + 1) * LANES)
         q = spin(query[:, cols], cosine, sine)
@@ -417,7 +458,7 @@
             send_ref[2 * pair + at, 0, rows:, :] = tile.astype(narrow)
 
 
-def project(inputs, norm_attn, first_values, cosine, sine, w_query, w_key, w_value, groups):
+def project(place, depth_pos, inputs, norm_attn, first_values, turns, w_query, w_key, w_value, groups):
     rows, width = inputs.shape
     local = w_query.shape[1]
     part = rows // groups
@@ -428,11 +469,12 @@
         project_kernel,
         grid=(groups,),
         in_specs=[
+            scalar_spec(),
+            scalar_spec(),
             pl.BlockSpec((part, width), moving),
-            pl.BlockSpec((1, width), fixed),
+            pl.BlockSpec((width,), lambda step: (0,)),
             pl.BlockSpec((part, local), moving),
-            pl.BlockSpec((part, LANES), moving),
-            pl.BlockSpec((part, LANES), moving),
+            pl.BlockSpec(turns.shape, lambda step: (0, 0, 0)),
             pl.BlockSpec((width, local), fixed),
             pl.BlockSpec((width, local), fixed),
             pl.BlockSpec((width, local), fixed),
@@ -448,7 +490,7 @@
         compiler_params=pltpu.CompilerParams(vmem_limit_bytes=vmem_bytes),
         cost_estimate=busy(6),
         name="project",
-    )(inputs, norm_attn.reshape(1, width), first_values, cosine, sine, w_query, w_key, w_value)
+    )(place, depth_pos, inputs, norm_attn, first_values, turns, w_query, w_key, w_value)
 
 
 def tree_walk(run, count, unroll):
@@ -502,11 +544,11 @@
 
 
 def gather_parts(part, recv_ref, other_ref, kv_ref, kvt_ref, lanes):
-    rows = other_ref.shape[1]
+    rows = other_ref.shape[1] * 2 // 3
 
     def fill(slot, carry):
         kv_ref[slot, pl.ds(pl.multiple_of(part * rows, rows), rows), :] = recv_ref[slot, :rows, :]
-        kv_ref[slot, pl.ds(pl.multiple_of((1 - part) * rows, rows), rows), :] = other_ref[slot]
+        kv_ref[slot, pl.ds(pl.multiple_of((1 - part) * rows, rows), rows), :] = other_ref[slot, :rows, :]
         flipped = jnp.transpose(kv_ref[slot].astype(wide))
         kvt_ref[slot] = flipped[lanes].astype(narrow)
         return carry
@@ -539,7 +581,7 @@
     excess_ref,
 ):
     part = part_ref[0]
-    rows = other_ref.shape[1]
+    rows = other_ref.shape[1] * 2 // 3
     count = recv_ref.shape[0]
     gather_parts(part, recv_ref, other_ref, kv_ref, vt_ref, slice(HEAD_DIM, LANES))
     excess_ref[...] = jnp.zeros_like(excess_ref)
@@ -608,7 +650,7 @@
 
 
 def attend(parents, assignment, part, recv, other):
-    count, rows, _ = other.shape
+    count, rows = other.shape[0], other.shape[1] * 2 // 3
     return pl.pallas_call(
         attend_kernel,
         in_specs=[scalar_spec()] * 3 + [whole_spec()] * 2,
@@ -646,7 +688,7 @@
     sum_ref,
 ):
     part = part_ref[0]
-    rows = other_ref.shape[1]
+    rows = other_ref.shape[1] * 2 // 3
     count = recv_ref.shape[0]
     gather_parts(part, recv_ref, other_ref, kv_ref, kt_ref, slice(0, HEAD_DIM))
 
@@ -678,7 +720,7 @@
             grad_query = grad_query + dot_wide(kt_ref[slot], grad_scores)
         dq_ref[own] = pack_columns(grad_query * (HEAD_DIM ** (-0.5))).astype(narrow)
 
-    tree_walk(run, count, 1)
+    tree_walk(run, count, 2)
 
     def finish(slot, carry):
         mine_ref[slot] = sum_ref[slot, pl.ds(pl.multiple_of(part * rows, rows), rows), :]
@@ -690,7 +732,7 @@
 
 
 def attend_back(parents, assignment, part, recv, other, grad, ot, logs):
-    count, rows, _ = other.shape
+    count, rows = other.shape[0], other.shape[1] * 2 // 3
     return pl.pallas_call(
         attend_back_kernel,
         in_specs=[scalar_spec()] * 3 + [whole_spec()] * 5,
@@ -736,7 +778,7 @@
     branch = branch + dot_wide(theirs, w_other_ref[...]).astype(narrow).astype(wide)
     hidden = x_ref[...].astype(wide) + branch
     hidden_ref[...] = hidden
-    normed_ref[...] = (hidden * rms_scale(hidden) * gain_ref[...].astype(wide)).astype(narrow)
+    normed_ref[...] = (hidden * rms_scale(hidden) * gain_ref[...].astype(wide)[None]).astype(narrow)
 
 
 def merge(own, other, w_own, w_other, inputs, norm_ffn):
@@ -754,7 +796,7 @@
         compiler_params=pltpu.CompilerParams(vmem_limit_bytes=vmem_bytes),
         cost_estimate=busy(6),
         name="merge",
-    )(own, other, w_own, w_other, inputs, norm_ffn.reshape(1, width))
+    )(own, other, w_own, w_other, inputs, norm_ffn)
 
 
 def branch_back_kernel(
@@ -774,7 +816,7 @@
     other = jnp.concatenate([early_ref[...], late_ref[...]], axis=0)
     grad_normed = own_ref[...].astype(wide) + other.astype(wide)
     hidden = hidden_ref[...]
-    back, gain_grad = norm_back(grad_normed, hidden, rms_scale(hidden), gain_ref[...].astype(wide))
+    back, gain_grad = norm_back(grad_normed, hidden, rms_scale(hidden), gain_ref[...].astype(wide)[None])
     gain_grad_ref[...] = gain_grad[None]
     grad_hidden = cot_ref[...].astype(wide) + back
     hidden_grad_ref[...] = grad_hidden
@@ -809,51 +851,47 @@
         compiler_params=pltpu.CompilerParams(vmem_limit_bytes=vmem_bytes),
         cost_estimate=busy(6),
         name="branch_back",
-    )(own, early, late, hidden, cotangent, norm_ffn.reshape(1, width), w_out)
+    )(own, early, late, hidden, cotangent, norm_ffn, w_out)
 
 
 def fold_kernel(
-    mine_ref, arrived_ref, dq_ref, cos_ref, sin_ref, slot_cos_ref, slot_sin_ref, send_ref, feats_ref
+    part_ref, depth_ref, mine_ref, arrived_ref, dq_ref, turn_ref, send_ref, rows_ref, packed_ref
 ):
     count, rows, _ = mine_ref.shape
     half = rows // 2
     low = lane_ids((rows, LANES)) < HEAD_DIM
+    for at, table in enumerate(turn_rows(turn_ref, part_ref[0] * rows, rows)):
+        rows_ref[at] = table
+        packed_ref[at] = jnp.where(low[:half], table[:half], table[half:])
 
     def step(slot, carry):
-        turn_cos = slot_cos_ref[slot][:1]
-        turn_sin = slot_sin_ref[slot][:1]
-        cosine = cos_ref[...] * turn_cos - sin_ref[...] * turn_sin
-        sine = -(sin_ref[...] * turn_cos + cos_ref[...] * turn_sin)
+        depth = turn_depth(turn_ref, depth_ref[slot])
+        cosine, sine = turn((rows_ref[0], rows_ref[1]), depth)
         pair = mine_ref[slot] + arrived_ref[slot].astype(wide)
-        key = spin(pair, cosine, sine)
+        key = spin(pair, cosine, -sine)
         send_ref[slot, :rows, :] = jnp.where(low, key, pair).astype(narrow)
-        feats_ref[slot, :, :LANES] = jnp.where(low, key, 0.5 * pair.astype(narrow).astype(wide)).astype(narrow)
-        packed = dq_ref[slot].astype(wide)
-        query = jnp.concatenate([packed, pltpu.roll(packed, HEAD_DIM, 1)], axis=0)
-        query = jnp.where(low, spin(query, cosine, sine), 0.0)
-        feats_ref[slot, :, LANES:] = query.astype(narrow)
-        top = query[:half]
-        bottom = pltpu.roll(query[half:], HEAD_DIM, 1)
-        send_ref[slot, rows:, :] = jnp.where(low[:half], top, bottom).astype(narrow)
+        cosine, sine = turn((packed_ref[0], packed_ref[1]), depth)
+        send_ref[slot, rows:, :] = spin(dq_ref[slot].astype(wide), cosine, -sine).astype(narrow)
         return carry
 
     lax.fori_loop(0, count, step, 0, unroll=4)
 
 
-def fold(mine, arrived, grad_q, cosine, sine, slot_cos, slot_sin):
+def fold(part, depth_pos, mine, arrived, grad_q, turns):
     count, rows, _ = mine.shape
     return pl.pallas_call(
         fold_kernel,
-        in_specs=[whole_spec()] * 7,
-        out_specs=[whole_spec()] * 2,
-        out_shape=[
-            jax.ShapeDtypeStruct((count, rows + rows // 2, LANES), narrow),
-            jax.ShapeDtypeStruct((count, rows, 2 * LANES), narrow),
+        in_specs=[scalar_spec()] * 2 + [whole_spec()] * 4,
+        out_specs=whole_spec(),
+        out_shape=jax.ShapeDtypeStruct((count, rows + rows // 2, LANES), narrow),
+        scratch_shapes=[
+            pltpu.VMEM((2, rows, LANES), wide),
+            pltpu.VMEM((2, rows // 2, LANES), wide),
         ],
         compiler_params=pltpu.CompilerParams(vmem_limit_bytes=vmem_bytes),
-        cost_estimate=busy(9),
+        cost_estimate=busy(6),
         name="fold",
-    )(mine, arrived, grad_q, cosine, sine, slot_cos, slot_sin)
+    )(part, depth_pos, mine, arrived, grad_q, turns)
 
 
 def unproject_kernel(recv_ref, wq_ref, wk_ref, wv_ref, first_ref, part_ref):
@@ -897,25 +935,30 @@
     )(recv, w_query, w_key, w_value)
 
 
-def finish_kernel(part_ref, own_ref, other_ref, query_ref, key_ref, value_ref, out_ref):
-    chips, size, width = own_ref.shape
-    part = part_ref[0]
+def finish_kernel(
+    place_ref, near_ref, far_ref, near_core_ref, far_core_ref, query_ref, key_ref, value_ref, out_ref
+):
+    length, size, width = near_ref.shape
+    chips = 2 * length
     head_rows = 3 * HEAD_DIM // 2
     out_rows = size - head_rows
+    place = place_ref[0]
+    core = place % 2
+    high = (place // 2) % 2
 
     def emit(first, second):
         for chip in range(chips):
-            at = chip * out_rows
-            out_ref[at : at + out_rows, :] = first[chip, head_rows:, :].astype(wide)
-            at += chips * out_rows
-            out_ref[at : at + out_rows, :] = second[chip, head_rows:, :].astype(wide)
+            for at, refs in ((chip, first), (chips + chip, second)):
+                rows = refs[chip % 2][chip // 2, head_rows:, :]
+                out_ref[at * out_rows : (at + 1) * out_rows, :] = rows.astype(wide)
 
         def column(block, carry):
             cols = pl.ds(pl.multiple_of(block * LANES, LANES), LANES)
             for pair in range(chips // 2):
                 pieces = [
                     jnp.concatenate(
-                        [first[chip, :head_rows, cols], second[chip, :head_rows, cols]], axis=0
+                        [refs[chip % 2][chip // 2, :head_rows, cols] for refs in (first, second)],
+                        axis=0,
                     ).astype(wide)
                     for chip in (2 * pair, 2 * pair + 1)
                 ]
@@ -927,27 +970,28 @@
 
         lax.fori_loop(0, width // LANES, column, 0)
 
-    @pl.when(part == 0)
-    def _():
-        emit(own_ref, other_ref)
-
-    @pl.when(part == 1)
-    def _():
-        emit(other_ref, own_ref)
-
-
-def finish(part, own, other, local):
-    width = own.shape[2]
+    for core_at in range(2):
+        for high_at in range(2):
+
+            @pl.when((core == core_at) & (high == high_at))
+            def _(core_at=core_at, high_at=high_at):
+                own = (near_ref, far_ref) if high_at == 0 else (far_ref, near_ref)
+                other = (near_core_ref, far_core_ref) if high_at == 0 else (far_core_ref, near_core_ref)
+                emit(own, other) if core_at == 0 else emit(other, own)
+
+
+def finish(place, near, far, near_core, far_core, local):
+    width = near.shape[2]
     return pl.pallas_call(
         finish_kernel,
-        in_specs=[scalar_spec()] + [whole_spec()] * 2,
+        in_specs=[scalar_spec()] + [whole_spec()] * 4,
         out_specs=[whole_spec()] * 4,
         out_shape=[jax.ShapeDtypeStruct((width, local), wide)] * 3
         + [jax.ShapeDtypeStruct((local, width), wide)],
         compiler_params=pltpu.CompilerParams(vmem_limit_bytes=vmem_bytes),
         cost_estimate=busy(6),
         name="finish",
-    )(part, own, other)
+    )(place, near, far, near_core, far_core)
 
 
 def swap_tensor(values):
@@ -998,13 +1042,6 @@
         tiled=True,
         axis_index_groups=[[z * 4 + rest for z in range(length)] for rest in range(4)],
     )
-
-
-def spread_pair(along, place, count):
-    arrived = swap_bit(along, 2, count)
-    high = (place // 2) % 2 == 1
-    pair = jnp.stack([jnp.where(high, arrived, along), jnp.where(high, along, arrived)], axis=1)
-    return pair.reshape((2 * along.shape[0],) + along.shape[1:])
 
 
 def gather_core(values, axis, place, count):
@@ -1088,28 +1125,21 @@
     part_array = part.reshape(1)
 
     rows = tokens // groups
-    half = HEAD_DIM // 2
     w_out_other = swap_tensor(w_out)
-    slot_ids = jnp.arange(count, dtype=jnp.int32)
-    start = jnp.sum(jnp.where(slot_ids == place, depth_pos, 0))
-    lanes = jnp.arange(LANES, dtype=jnp.int32)
-    frequency = rope_base ** (-(lanes % half).astype(wide) * 2.0 / HEAD_DIM)
-    sign = jnp.where(lanes % HEAD_DIM < half, -1.0, 1.0)[None, :]
-    positions = (start + jnp.arange(tokens, dtype=jnp.int32)).astype(wide)
-    angles = positions[:, None] * frequency[None, :]
-    cosine = jnp.cos(angles)
-    sine = jnp.sin(angles) * sign
-    part_positions = (part * rows + jnp.arange(rows, dtype=jnp.int32)).astype(wide)
-    part_angles = part_positions[:, None] * frequency[None, :]
-    part_cos = jnp.cos(part_angles)
-    part_sin = jnp.sin(part_angles) * sign
-    slot_angles = depth_pos.astype(wide)[:, None] * frequency[None, :]
-    slot_shape = (count, 8, LANES)
-    slot_cos = jnp.broadcast_to(jnp.cos(slot_angles)[:, None, :], slot_shape)
-    slot_sin = jnp.broadcast_to((jnp.sin(slot_angles) * sign)[:, None, :], slot_shape)
+    turns = jnp.asarray(turn_constants())
+    place_array = place.astype(jnp.int32).reshape(1)
 
     send, normed = project(
-        inputs, norm_attn, first_values, cosine, sine, w_query, w_key, w_value, groups
+        place_array,
+        depth_pos,
+        inputs,
+        norm_attn,
+        first_values,
+        turns,
+        w_query,
+        w_key,
+        w_value,
+        groups,
     )
     send = send.reshape(count, rows + rows // 2, LANES)
     recv = lax.all_to_all(send, "dp", split_axis=0, concat_axis=0, tiled=True)
@@ -1127,7 +1157,7 @@
         normed_quarter, "dp", axis=0, tiled=True, axis_index_groups=side_groups(count)
     )
 
-    other = swap_bit(recv[:, :rows], 1, count)
+    other = swap_bit(recv, 1, count)
     packed, ot, logs = attend(parents, assignment, part_array, recv, other)
     own_out = lax.all_to_all(packed, "dp", split_axis=0, concat_axis=0, tiled=True)
     other_out = swap_tensor(own_out)
@@ -1185,21 +1215,25 @@
             (grad_q, mine, theirs, out_shares)
         )
         arrived = swap_bit(theirs, 1, count)
-        back_send, feats = fold(
-            mine, arrived, grad_q, part_cos, part_sin, slot_cos, slot_sin
-        )
+        back_send = fold(part_array, depth_pos, mine, arrived, grad_q, turns)
         back_recv = lax.all_to_all(back_send, "dp", split_axis=0, concat_axis=0, tiled=True)
-        feats = feats.reshape(count, 2, quarter, 2 * LANES)
-        head_grads = sum(
-            jnp.einsum(
+        pairs_terms = query_terms = 0.0
+        for at, normed_part in ((side, normed_own), (1 - side, normed_other)):
+            pairs = lax.dynamic_slice_in_dim(back_send, at * quarter, quarter, 1)
+            both = jnp.concatenate([pairs, back_send[:, rows:]], axis=2)
+            terms = jnp.einsum(
                 "tc,td->cd",
-                lax.dynamic_index_in_dim(feats, at, 1, keepdims=False).reshape(-1, 2 * LANES),
+                both.reshape(count * quarter, 2 * LANES),
                 normed_part,
                 preferred_element_type=wide,
             )
-            for at, normed_part in ((side, normed_own), (1 - side, normed_other))
-        )
-        head_grads = head_grads[: 3 * HEAD_DIM].astype(narrow)
+            pairs_terms = pairs_terms + terms[:LANES]
+            query_terms = query_terms + lax.dynamic_slice_in_dim(
+                terms, LANES + at * HEAD_DIM, HEAD_DIM, 0
+            )
+        head_grads = jnp.concatenate(
+            [pairs_terms[:HEAD_DIM], 0.5 * pairs_terms[HEAD_DIM:], query_terms], axis=0
+        ).astype(narrow)
         head_share = reduce_bit(head_grads, 1, place, count)
         out_share = jnp.sum(out_shares.astype(wide), axis=0).astype(narrow)
         share = jnp.concatenate([head_share, out_share], axis=0)
@@ -1208,39 +1242,31 @@
         grad_first, attn_partial = unproject(back_recv, w_query, w_key, w_value)
         attn_other = swap_tensor(attn_partial)
         along = spread_line(copies, count)
-        spread_all = spread_pair(after(along, attn_partial), place, count)
+        near = after(along, attn_partial)
+        far = swap_bit(near, 2, count)
+        near_core = swap_bit(near, 1, count)
         output = (hidden + (feed_partial.astype(wide) + feed_other.astype(wide))).astype(narrow)
-        return (
-            output,
-            grad_hidden,
-            grad_gain_ffn,
-            grad_first,
-            attn_partial,
-            attn_other,
-            spread_all,
+        inputs_wide = inputs.astype(wide)
+        grad_normed = attn_partial.astype(wide) + attn_other.astype(wide)
+        grad_input_norm, grad_gain_attn = norm_back(
+            grad_normed, inputs_wide, rms_scale(inputs_wide), norm_attn.astype(wide)
         )
+        grad_inputs = grad_hidden + grad_input_norm
+        gains = sum_small(jnp.stack([grad_gain_attn, grad_gain_ffn[0]]), count)
+        far_core = swap_bit(after(far, gains, grad_inputs, output), 1, count)
+        return output, grad_inputs, grad_first, gains, near, far, near_core, far_core
 
     def no_tree(*operands):
         shapes = jax.eval_shape(way_back, *operands)
         return tuple(jnp.zeros(leaf.shape, leaf.dtype) for leaf in shapes)
 
-    output, grad_hidden, grad_gain_ffn, grad_first, attn_partial, attn_other, spread_all = lax.cond(
+    output, grad_inputs, grad_first, gains, near, far, near_core, far_core = lax.cond(
         parents[0] < 0, way_back, no_tree, ffn_early, normed_own
     )
-    spread_other = swap_bit(spread_all, 1, count)
-    inputs_wide = inputs.astype(wide)
-    grad_normed = attn_partial.astype(wide) + attn_other.astype(wide)
-    grad_input_norm, grad_gain_attn = norm_back(
-        grad_normed, inputs_wide, rms_scale(inputs_wide), norm_attn.astype(wide)
-    )
-    grad_inputs = grad_hidden + grad_input_norm
-    gains = jnp.stack([grad_gain_attn, grad_gain_ffn[0]])
-    head_query, head_key, head_value, sum_w_out = finish(part_array, spread_all, spread_other, local)
-    gains = after(gains + swap_bit(gains, 1, count), sum_w_out)
-    sums = []
-    for at, term in enumerate(ffn_sums):
-        sums.append(after(term, grad_inputs, sum_w_out).astype(wide))
-        gains = after(gains + swap_bit(gains, 2 << at, count), sums[-1])
+    head_query, head_key, head_value, sum_w_out = finish(
+        place_array, near, far, near_core, far_core, local
+    )
+    sums = [after(term, sum_w_out).astype(wide) for term in ffn_sums]
     return (
         output,
         grad_inputs,

time: 447 us -> 422 us (0.944)
  other arithmetic: 33.9 us -> 26 us
  local copies, waits for them, and re-layouts: 15.5 us -> 9.72 us
  Pallas kernels: 95.8 us -> 90.5 us
  waiting for transfers between devices: 174 us -> 169 us
    ppermute x7, waiting for transfers between devices: 48.9 us -> 70 us  [swap_tensor(): return lax.ppermute(values, 'tensor', [(0, 1), (1, 0)])]
    all_to_all x1, waiting for transfers between devices: 31.2 us -> 15.1 us  [spread_line(): lax.all_to_all(copies, 'dp', split_axis=0, concat_axis=0, tiled=True, axi...]
    all_to_all x1, waiting for transfers between devices: 6.88 us -> 0.79 us  [way_back(): lax.all_to_all(back_send, 'dp', split_axis=0, concat_axis=0, tiled=True)]
    ppermute x11 -> x12, waiting for transfers between devices: 27.8 us -> 23 us  [swap_bit(): return lax.ppermute(values, 'dp', [(i, i ^ bit) for i in range(count)])]
    ppermute x11 -> x12, starting transfers between devices: 6.98 us -> 9.17 us  [swap_bit(): return lax.ppermute(values, 'dp', [(i, i ^ bit) for i in range(count)])]
    convert_element_type x7 -> x4, other arithmetic: 13.1 us -> 11 us  [the longest x3 11 us: body_heads(): sums = [after(term, sum_w_out).astype(wide) for term in ffn_sums]]
  transfers between devices with their start and end apart: 26 -> 27, of which waited for: 19 -> 22; matrix products, arithmetic and copies ran while one was open for 17% -> 15% of each run, Pallas kernels for 20% -> 20%
where the time goes in v4:
time: 422 us; the launch traced here: 414 us
  waiting for transfers between devices  169 us (40%)
  Pallas kernels  90.5 us (21%)
  starting transfers between devices  63.2 us (15%)
  matrix products  40.7 us (10%)
  other arithmetic  26 us (6%)
  between operations  14.8 us (4%)
  local copies, waits for them, and re-layouts  9.72 us (2%)
    ppermute x7, waiting for transfers between devices, swap_tensor(): return lax.ppermute(values, 'tensor', [(0, 1), (1, 0)])  70 us
    pallas_call x1, Pallas kernels, attend_back(): pl.pallas_call(attend_back_kernel, in_specs=[scalar_spec()] * 3 + [whole_...  34.3 us
    all_to_all x1, waiting for transfers between devices, body_heads(): recv = lax.all_to_all(send, 'dp', split_axis=0, concat_axis=0, tiled=True)  24.6 us
    ppermute x12, waiting for transfers between devices, swap_bit(): return lax.ppermute(values, 'dp', [(i, i ^ bit) for i in range(count)])  23 us
    pallas_call x1, Pallas kernels, attend(): pl.pallas_call(attend_kernel, in_specs=[scalar_spec()] * 3 + [whole_spec(...  21.3 us
    all_to_all x1, waiting for transfers between devices, body_heads(): lax.all_to_all(packed, 'dp', split_axis=0, concat_axis=0, tiled=True)  17.7 us
    all_to_all x1, waiting for transfers between devices, way_back(): lax.all_to_all(grad_send.reshape(count, rows // 2, LANES), 'dp', split_ax...  17.5 us
    all_to_all x1, waiting for transfers between devices, spread_line(): lax.all_to_all(copies, 'dp', split_axis=0, concat_axis=0, tiled=True, axi...  15.1 us
  transfers between devices with their start and end apart: 27, of which 22 were waited for; matrix products, arithmetic and copies ran while one was open for 15% of the time, Pallas kernels for 20%

profile of v4, /device:TPU:0, one launch (start us, length us, event | category | flops | bytes accessed | tf_op | source)
XLA Modules:
  0.0 414.1 jit_solution(17864773252437390291)
XLA Ops:
  7.2 6.2 %project.1 = (bf16[8,2,384,128]{3,2,1,0:T(8,128)(2,1)}, bf16[512,1024]{1,0:T(8,128)(2,1)}) custom-call(s32[1]{0:T(128)} %bitcast.11.place_ref, s32[16]{0:T(128)} %depth_ref.1, bf16[512,1024]{1,0:T(8,128)(2,1)} %x_ref.3, bf16[1024]{0:T(1024)(128)(2,1)} %gain_ref.2, bf16[512,512]{1,0:T(8,128)(2,1)} %first_ref.1, f32[2,56,128]{2,1,0:T(8,128)} %constant.103.clone.turn_ref, ...), custom_call_target="tpu_custom_call" | custom-call | flops 6000000000 | bytes 12000000 | tf_op jit(solution)/shard_map/project/pallas_call | solution.py:468
  13.4 7.4 %all-to-all-start.4 = ((bf16[16,384,128]{2,1,0:T(8,128)(2,1)}), bf16[16,384,128]{2,1,0:T(8,128)(2,1)}, u32[]{:S(2)}, u32[]{:S(2)}) async-start(bf16[16,384,128]{2,1,0:T(8,128)(2,1)} %bitcast.46), calls=%async_computation.4 | async-start | bytes 3145728 | tf_op jit(solution)/shard_map/all_to_all | solution.py:1145
  28.3 24.6 %all-to-all-done.4.recv_ref = bf16[16,384,128]{2,1,0:T(8,128)(2,1)} async-done(((bf16[16,384,128]{2,1,0:T(8,128)(2,1)}), bf16[16,384,128]{2,1,0:T(8,128)(2,1)}, u32[]{:S(2)}, u32[]{:S(2)}) %all-to-all-start.4) | async-done | bytes 1572896 | tf_op jit(solution)/shard_map/all_to_all | solution.py:1145
  57.1 21.3 %attend.1 = (bf16[16,128,128]{2,1,0:T(8,128)(2,1)}, f32[16,64,256]{2,1,0:T(8,128)}, f32[16,8,256]{2,1,0:T(8,128)}) custom-call(s32[16]{0:T(128)S(1)} %copy-done.19, s32[16]{0:T(128)S(1)} %copy-done.20, s32[1]{0:T(128)} %bitcast.10.part_ref, bf16[16,384,128]{2,1,0:T(8,128)(2,1)} %all-to-all-done.4.recv_ref, ...), custom_call_target="tpu_custom_call" | custom-call | flops 22000001024 | bytes 44000000 | tf_op jit(solution)/shard_map/attend/pallas_call | solution.py:654
  78.3 8.8 %all-to-all-start.5 = ((bf16[16,128,128]{2,1,0:T(8,128)(2,1)}), bf16[16,128,128]{2,1,0:T(8,128)(2,1)}, u32[]{:S(2)}, u32[]{:S(2)}) async-start(bf16[16,128,128]{2,1,0:T(8,128)(2,1)} %get-tuple-element.146), calls=%async_computation.5 | async-start | bytes 1048576 | tf_op jit(solution)/shard_map/all_to_all | solution.py:1162
  89.2 17.7 %all-to-all-done.5.own_ref = bf16[16,128,128]{2,1,0:T(8,128)(2,1)} async-done(((bf16[16,128,128]{2,1,0:T(8,128)(2,1)}), bf16[16,128,128]{2,1,0:T(8,128)(2,1)}, u32[]{:S(2)}, u32[]{:S(2)}) %all-to-all-start.5) | async-done | bytes 524320 | tf_op jit(solution)/shard_map/all_to_all | solution.py:1162
  108.4 5.6 %fusion.20 = f32[512,1408]{1,0:T(8,128)} fusion(bf16[512,1024]{1,0:T(8,128)(2,1)} %param.29, bf16[1408,1024]{1,0:T(8,128)(2,1)} %param.26), kind=kOutput, calls=%fused_computation.59 | convolution fusion | flops 1476395008 | bytes 6815744 | tf_op jit(solution)/shard_map/td,fd->tf/dot_general | solution.py:1170
  114.1 10.7 %collective-permute-done.16.other_ref = bf16[16,128,128]{2,1,0:T(8,128)(2,1)} collective-permute-done((bf16[16,128,128]{2,1,0:T(8,128)(2,1)}, bf16[16,128,128]{2,1,0:T(8,128)(2,1)}, u32[]{:S(2)}, u32[]{:S(2)}) %collective-permute-start.16) | collective-permute-done | bytes 524320 | tf_op jit(solution)/shard_map/ppermute | solution.py:998
  124.7 5.4 %merge.1 = (bf16[512,512]{1,0:T(8,128)(2,1)}, f32[512,1024]{1,0:T(8,128)}, bf16[512,1024]{1,0:T(8,128)(2,1)}) custom-call(bf16[16,128,128]{2,1,0:T(8,128)(2,1)} %all-to-all-done.5.own_ref, bf16[16,128,128]{2,1,0:T(8,128)(2,1)} %collective-permute-done.16.other_ref, bf16[512,1024]{1,0:T(8,128)(2,1)} %w_own_ref.1, ...), custom_call_target="tpu_custom_call" | custom-call | flops 6000000000 | bytes 12000000 | tf_op jit(solution)/shard_map/merge/pallas_call | solution.py:787
  160.0 228.3 %conditional.1 = (bf16[512,1024]{1,0:T(8,128)(2,1)}, f32[512,1024]{1,0:T(8,128)}, f32[512,512]{1,0:T(8,128)}, f32[2,1024]{1,0:T(2,128)}, bf16[4,128,1024]{2,1,0:...) conditional(s32[]{:T(128)} %bitcast.9, () %tuple.30, ...), branch_computations={%region_0.1_spmd, %region_1.0_spmd} | conditional | flops 111707529216 | bytes 360422944 | solution.py:1263
  161.6 11.0 %collective-permute-done.late_ref = bf16[256,1024]{1,0:T(8,128)(2,1)} collective-permute-done((bf16[256,1024]{1,0:T(8,128)(2,1)S(1)}, bf16[256,1024]{1,0:T(8,128)(2,1)}, u32[]{:S(2)}, u32[]{:S(2)}) %collective-permute-start) | collective-permute-done | bytes 524320 | tf_op jit(solution)/shard_map/cond/branch_1_fun/ppermute | solution.py:998
  172.6 5.7 %branch_back.1 = (bf16[8,2,128,128]{3,2,1,0:T(8,128)(2,1)}, f32[512,1024]{1,0:T(8,128)}, bf16[512,1024]{1,0:T(8,128)(2,1)}, f32[1,1024]{1,0:T(1,128)}) custom-call(bf16[512,1024]{1,0:T(8,128)(2,1)S(1)} %get-tuple-element.62.own_ref, bf16[256,1024]{1,0:T(8,128)(2,1)S(1)} %get-tuple-element.63.early_ref, bf16[256,1024]{1,0:T(8,128)(2,1)} %collective-permute-done.late_ref, ...), custom_call_target="tpu_custom_call" | custom-call | flops 6000000000 | bytes 12000000 | tf_op jit(solution)/shard_map/cond/branch_1_fun/branch_back/pallas_call | solution.py:841
  178.4 7.9 %all-to-all-start = ((bf16[16,128,128]{2,1,0:T(8,128)(2,1)}), bf16[16,128,128]{2,1,0:T(8,128)(2,1)S(1)}, u32[]{:S(2)}, u32[]{:S(2)}) async-start(bf16[16,128,128]{2,1,0:T(8,128)(2,1)} %bitcast.49), calls=%async_computation | async-start | bytes 1048576 | tf_op jit(solution)/shard_map/cond/branch_1_fun/all_to_all | solution.py:1200
  191.8 17.5 %all-to-all-done.grad_ref = bf16[16,128,128]{2,1,0:T(8,128)(2,1)S(1)} async-done(((bf16[16,128,128]{2,1,0:T(8,128)(2,1)}), bf16[16,128,128]{2,1,0:T(8,128)(2,1)S(1)}, u32[]{:S(2)}, u32[]{:S(2)}) %all-to-all-start) | async-done | bytes 524320 | tf_op jit(solution)/shard_map/cond/branch_1_fun/all_to_all | solution.py:1200
  214.1 34.3 %attend_back.1 = (bf16[16,128,128]{2,1,0:T(8,128)(2,1)}, f32[16,256,128]{2,1,0:T(8,128)}, bf16[16,256,128]{2,1,0:T(8,128)(2,1)}) custom-call(s32[16]{0:T(128)S(1)} %get-tuple-element.58.parents_ref, s32[16]{0:T(128)S(1)} %get-tuple-element.59.assign_ref, s32[1]{0:T(128)} %get-tuple-element.56.part_ref, bf16[16,384,128]{2,1,0:T(8,128)(2,1)} %get-tuple-element.60.recv_ref, ...), custom_call_target="tpu_custom_call" | custom-call | flops 36999999488 | bytes 74000000 | tf_op jit(solution)/shard_map/cond/branch_1_fun/attend_back/pallas_call | solution.py:736
  257.3 6.2 %all-to-all-start.2 = ((bf16[16,384,128]{2,1,0:T(8,128)(2,1)}), bf16[16,384,128]{2,1,0:T(8,128)(2,1)}, u32[]{:S(2)}, u32[]{:S(2)}) async-start(bf16[16,384,128]{2,1,0:T(8,128)(2,1)} %fold.1), calls=%async_computation.2 | async-start | bytes 3145728 | tf_op jit(solution)/shard_map/cond/branch_1_fun/all_to_all | solution.py:1219
  267.5 14.3 %collective-permute-done.3 = bf16[2048,1024]{1,0:T(8,128)(2,1)} collective-permute-done((bf16[2048,1024]{1,0:T(8,128)(2,1)}, bf16[2048,1024]{1,0:T(8,128)(2,1)}, u32[]{:S(2)}, u32[]{:S(2)}) %collective-permute-start.3) | collective-permute-done | bytes 4194336 | tf_op jit(solution)/shard_map/cond/branch_1_fun/ppermute | solution.py:998
  289.7 16.6 %collective-permute-done.4 = bf16[512,1024]{1,0:T(8,128)(2,1)} collective-permute-done((bf16[512,1024]{1,0:T(8,128)(2,1)S(1)}, bf16[512,1024]{1,0:T(8,128)(2,1)}, u32[]{:S(2)}, u32[]{:S(2)}) %collective-permute-start.4) | collective-permute-done | bytes 1048608 | tf_op jit(solution)/shard_map/cond/branch_1_fun/ppermute | solution.py:998
  308.1 5.3 %unproject.1 = (f32[512,512]{1,0:T(8,128)}, bf16[512,1024]{1,0:T(8,128)(2,1)}) custom-call(bf16[16,384,128]{2,1,0:T(8,128)(2,1)} %all-to-all-done.2.recv_ref, bf16[1024,512]{1,0:T(8,128)(2,1)} %get-tuple-element.90.wq_ref, bf16[1024,512]{1,0:T(8,128)(2,1)} %get-tuple-element.91.wk_ref, bf16[1024,512]{1,0:T(8,128)(2,1)} %get-tuple-element.92.wv_ref), custom_call_target="tpu_custom_call" | custom-call | flops 60000002048 | bytes 120000000 | tf_op jit(solution)/shard_map/cond/branch_1_fun/unproject/pallas_call | solution.py:924
  314.9 8.9 %all-to-all-start.3 = ((bf16[4,128,1024]{2,1,0:T(8,128)(2,1)}), bf16[4,128,1024]{2,1,0:T(8,128)(2,1)}, u32[]{:S(2)}, u32[]{:S(2)}) async-start(bf16[4,128,1024]{2,1,0:T(8,128)(2,1)} %broadcast_in_dim.0), calls=%async_computation.3 | async-start | bytes 2097152 | tf_op jit(solution)/shard_map/cond/branch_1_fun/all_to_all | solution.py:1037
  324.0 15.7 %collective-permute-done.6 = bf16[512,1024]{1,0:T(8,128)(2,1)} collective-permute-done((bf16[512,1024]{1,0:T(8,128)(2,1)}, bf16[512,1024]{1,0:T(8,128)(2,1)}, u32[]{:S(2)}, u32[]{:S(2)}) %collective-permute-start.6) | collective-permute-done | bytes 1048608 | tf_op jit(solution)/shard_map/cond/branch_1_fun/ppermute | solution.py:998
  346.1 15.1 %all-to-all-done.3 = bf16[4,128,1024]{2,1,0:T(8,128)(2,1)} async-done(((bf16[4,128,1024]{2,1,0:T(8,128)(2,1)}), bf16[4,128,1024]{2,1,0:T(8,128)(2,1)}, u32[]{:S(2)}, u32[]{:S(2)}) %all-to-all-start.3) | async-done | bytes 1048608 | tf_op jit(solution)/shard_map/cond/branch_1_fun/all_to_all | solution.py:1037
  375.2 9.8 %collective-permute-done.11 = bf16[4,128,1024]{2,1,0:T(8,128)(2,1)} collective-permute-done((bf16[4,128,1024]{2,1,0:T(8,128)(2,1)}, bf16[4,128,1024]{2,1,0:T(8,128)(2,1)}, u32[]{:S(2)}, u32[]{:S(2)}) %collective-permute-start.11) | collective-permute-done | bytes 1048608 | tf_op jit(solution)/shard_map/cond/branch_1_fun/ppermute | solution.py:1002
  388.3 7.3 %finish.1 = (f32[1024,512]{1,0:T(8,128)}, f32[1024,512]{1,0:T(8,128)}, f32[1024,512]{1,0:T(8,128)}, f32[512,1024]{1,0:T(8,128)}) custom-call(s32[1]{0:T(128)} %bitcast.11.place_ref, bf16[4,128,1024]{2,1,0:T(8,128)(2,1)} %get-tuple-element.161.near_ref, bf16[4,128,1024]{2,1,0:T(8,128)(2,1)} %get-tuple-element.162.far_ref, ...), custom_call_target="tpu_custom_call" | custom-call | flops 6000000000 | bytes 12000000 | tf_op jit(solution)/shard_map/finish/pallas_call | solution.py:985
  (147 shorter events, 115.7 us)
Async XLA Ops:
  13.4 39.5 %all-to-all-start.4 = ((bf16[16,384,128]{2,1,0:T(8,128)(2,1)}), bf16[16,384,128]{2,1,0:T(8,128)(2,1)}, u32[]{:S(2)}, u32[]{:S(2)}) async-start(bf16[16,384,128]{2,1,0:T(8,128)(2,1)} %bitcast.46), calls=%async_computation.4 | async-start | bytes 3145728 | tf_op jit(solution)/shard_map/all_to_all | solution.py:1145
  20.9 132.3 %all-gather.2.cloned.1.call-start = ((), (), s32[]{:S(2)}) async-start(), calls=%async_computation.6 | async-start | bytes 4718592 | tf_op jit(solution)/shard_map/all_gather | solution.py:1156
  23.0 2.3 collective-permute-start.14
  52.9 4.1 %collective-permute-start.15 = (bf16[16,384,128]{2,1,0:T(8,128)(2,1)}, bf16[16,384,128]{2,1,0:T(8,128)(2,1)}, u32[]{:S(2)}, u32[]{:S(2)}) collective-permute-start(bf16[16,384,128]{2,1,0:T(8,128)(2,1)} %all-to-all-done.4.recv_ref), channel_id=1, source_target_pairs={{0,2},{2,0},{4,6},{6,4},{8,10},{10,8},{12,14},{14,12},{16,18},{18,... | collective-permute-start | bytes 4718600 | tf_op jit(solution)/shard_map/ppermute | solution.py:1002
  78.3 28.6 %all-to-all-start.5 = ((bf16[16,128,128]{2,1,0:T(8,128)(2,1)}), bf16[16,128,128]{2,1,0:T(8,128)(2,1)}, u32[]{:S(2)}, u32[]{:S(2)}) async-start(bf16[16,128,128]{2,1,0:T(8,128)(2,1)} %get-tuple-element.146), calls=%async_computation.5 | async-start | bytes 1048576 | tf_op jit(solution)/shard_map/all_to_all | solution.py:1162
  87.1 308.5 %all-reduce.3.cloned.1.call-start = ((), (), s32[]{:S(2)}) async-start(), calls=%async_computation.7 | async-start | bytes 17301504 | tf_op jit(solution)/shard_map/psum | solution.py:1192
  87.7 26.4 %collective-permute-start.17 = (bf16[512,1024]{1,0:T(8,128)(2,1)}, bf16[512,1024]{1,0:T(8,128)(2,1)}, u32[]{:S(2)}, u32[]{:S(2)}) collective-permute-start(bf16[512,1024]{1,0:T(8,128)(2,1)} %w_own_ref.1), channel_id=1, source_target_pairs={{0,1},{1,0},{2,3},{3,2},{4,5},{5,4},{6,7},{7,6},{8,9},{9,8},{10,11... | collective-permute-start | bytes 3145736 | tf_op jit(solution)/shard_map/ppermute | solution.py:998
  106.9 17.8 %collective-permute-start.16 = (bf16[16,128,128]{2,1,0:T(8,128)(2,1)}, bf16[16,128,128]{2,1,0:T(8,128)(2,1)}, u32[]{:S(2)}, u32[]{:S(2)}) collective-permute-start(bf16[16,128,128]{2,1,0:T(8,128)(2,1)} %all-to-all-done.5.own_ref), channel_id=1, source_target_pairs={{0,1},{1,0},{2,3},{3,2},{4,5},{5,4},{6,7},{7,6},{8,9},{9,8},{10,11... | collective-permute-start | bytes 1572872 | tf_op jit(solution)/shard_map/ppermute | solution.py:998
  141.3 13.4 %collective-permute-start.18 = (bf16[256,1024]{1,0:T(8,128)(2,1)S(1)}, bf16[256,1024]{1,0:T(8,128)(2,1)S(1)}, u32[]{:S(2)}, u32[]{:S(2)}) collective-permute-start(bf16[256,1024]{1,0:T(8,128)(2,1)S(1)} %slice.47), channel_id=1, source_target_pairs={{0,1},{1,0},{2,3},{3,2},{4,5},{5,4},{6,7},{7,6},{8,9},{9,8},{10,11... | collective-permute-start | bytes 1572872 | tf_op jit(solution)/shard_map/ppermute | solution.py:998
  160.0 12.6 %collective-permute-start = (bf16[256,1024]{1,0:T(8,128)(2,1)S(1)}, bf16[256,1024]{1,0:T(8,128)(2,1)}, u32[]{:S(2)}, u32[]{:S(2)}) collective-permute-start(bf16[256,1024]{1,0:T(8,128)(2,1)S(1)} %slice.28), channel_id=1, source_target_pairs={{0,1},{1,0},{2,3},{3,2},{4,5},{5,4},{6,7},{7,6},{8,9},{9,8},{10,11... | collective-permute-start | bytes 1572872 | tf_op jit(solution)/shard_map/cond/branch_1_fun/ppermute | solution.py:998
  178.4 31.0 %all-to-all-start = ((bf16[16,128,128]{2,1,0:T(8,128)(2,1)}), bf16[16,128,128]{2,1,0:T(8,128)(2,1)S(1)}, u32[]{:S(2)}, u32[]{:S(2)}) async-start(bf16[16,128,128]{2,1,0:T(8,128)(2,1)} %bitcast.49), calls=%async_computation | async-start | bytes 1048576 | tf_op jit(solution)/shard_map/cond/branch_1_fun/all_to_all | solution.py:1200
  189.0 92.9 %collective-permute-start.3 = (bf16[2048,1024]{1,0:T(8,128)(2,1)}, bf16[2048,1024]{1,0:T(8,128)(2,1)}, u32[]{:S(2)}, u32[]{:S(2)}) collective-permute-start(bf16[2048,1024]{1,0:T(8,128)(2,1)} %get-tuple-element.82), channel_id=1, source_target_pairs={{0,1},{1,0},{2,3},{3,2},{4,5},{5,4},{6,7},{7,6},{8,9},{9,8},{10,11... | collective-permute-start | bytes 12582920 | tf_op jit(solution)/shard_map/cond/branch_1_fun/ppermute | solution.py:998
  210.4 38.0 %all-to-all-start.1 = ((bf16[8,32,1024]{2,1,0:T(8,128)(2,1)}), bf16[8,32,1024]{2,1,0:T(8,128)(2,1)S(1)}, u32[]{:S(2)}, u32[]{:S(2)}) async-start(bf16[8,32,1024]{2,1,0:T(8,128)(2,1)} %bitcast.3), calls=%async_computation.1 | async-start | bytes 1048576 | tf_op jit(solution)/shard_map/cond/branch_1_fun/all_to_all | solution.py:1025
  248.3 2.9 collective-permute-start.2
  257.3 49.8 %all-to-all-start.2 = ((bf16[16,384,128]{2,1,0:T(8,128)(2,1)}), bf16[16,384,128]{2,1,0:T(8,128)(2,1)}, u32[]{:S(2)}, u32[]{:S(2)}) async-start(bf16[16,384,128]{2,1,0:T(8,128)(2,1)} %fold.1), calls=%async_computation.2 | async-start | bytes 3145728 | tf_op jit(solution)/shard_map/cond/branch_1_fun/all_to_all | solution.py:1219
  281.8 24.4 %collective-permute-start.4 = (bf16[512,1024]{1,0:T(8,128)(2,1)S(1)}, bf16[512,1024]{1,0:T(8,128)(2,1)}, u32[]{:S(2)}, u32[]{:S(2)}) collective-permute-start(bf16[512,1024]{1,0:T(8,128)(2,1)S(1)} %copy-done.9), channel_id=1, source_target_pairs={{0,1},{1,0},{2,3},{3,2},{4,5},{5,4},{6,7},{7,6},{8,9},{9,8},{10,11... | collective-permute-start | bytes 3145736 | tf_op jit(solution)/shard_map/cond/branch_1_fun/ppermute | solution.py:998
  313.4 26.3 %collective-permute-start.6 = (bf16[512,1024]{1,0:T(8,128)(2,1)}, bf16[512,1024]{1,0:T(8,128)(2,1)}, u32[]{:S(2)}, u32[]{:S(2)}) collective-permute-start(bf16[512,1024]{1,0:T(8,128)(2,1)} %get-tuple-element.93), channel_id=1, source_target_pairs={{0,1},{1,0},{2,3},{3,2},{4,5},{5,4},{6,7},{7,6},{8,9},{9,8},{10,11... | collective-permute-start | bytes 3145736 | tf_op jit(solution)/shard_map/cond/branch_1_fun/ppermute | solution.py:998
  314.9 46.3 %all-to-all-start.3 = ((bf16[4,128,1024]{2,1,0:T(8,128)(2,1)}), bf16[4,128,1024]{2,1,0:T(8,128)(2,1)}, u32[]{:S(2)}, u32[]{:S(2)}) async-start(bf16[4,128,1024]{2,1,0:T(8,128)(2,1)} %broadcast_in_dim.0), calls=%async_computation.3 | async-start | bytes 2097152 | tf_op jit(solution)/shard_map/cond/branch_1_fun/all_to_all | solution.py:1037
  343.1 23.0 %collective-permute-start.8 = (f32[2,1024]{1,0:T(2,128)S(1)}, f32[2,1024]{1,0:T(2,128)S(1)}, u32[]{:S(2)}, u32[]{:S(2)}) collective-permute-start(f32[2,1024]{1,0:T(2,128)S(1)} %fusion.12), channel_id=1, source_target_pairs={{0,4},{2,6},{4,0},{6,2},{8,12},{10,14},{12,8},{14,10},{16,20},{18,... | collective-permute-start | bytes 24584 | tf_op jit(solution)/shard_map/cond/branch_1_fun/ppermute | solution.py:1002
  361.2 23.9 %collective-permute-start.11 = (bf16[4,128,1024]{2,1,0:T(8,128)(2,1)}, bf16[4,128,1024]{2,1,0:T(8,128)(2,1)}, u32[]{:S(2)}, u32[]{:S(2)}) collective-permute-start(bf16[4,128,1024]{2,1,0:T(8,128)(2,1)} %all-to-all-done.3), channel_id=1, source_target_pairs={{0,4},{2,6},{4,0},{6,2},{8,12},{10,14},{12,8},{14,10},{16,20},{18,... | collective-permute-start | bytes 3145736 | tf_op jit(solution)/shard_map/cond/branch_1_fun/ppermute | solution.py:1002
  366.1 3.8 collective-permute-start.9
  369.9 4.7 %collective-permute-start.10 = (f32[2,1024]{1,0:T(2,128)S(1)}, f32[2,1024]{1,0:T(2,128)S(1)}, u32[]{:S(2)}, u32[]{:S(2)}) collective-permute-start(f32[2,1024]{1,0:T(2,128)S(1)} %add.107), channel_id=1, source_target_pairs={{0,16},{2,18},{4,20},{6,22},{8,24},{10,26},{12,28},{14,30},{16,0},... | collective-permute-start | bytes 24584 | tf_op jit(solution)/shard_map/cond/branch_1_fun/ppermute | solution.py:1002
  375.2 12.6 %collective-permute-start.12 = (bf16[4,128,1024]{2,1,0:T(8,128)(2,1)}, bf16[4,128,1024]{2,1,0:T(8,128)(2,1)}, u32[]{:S(2)}, u32[]{:S(2)}) collective-permute-start(bf16[4,128,1024]{2,1,0:T(8,128)(2,1)} %all-to-all-done.3), channel_id=1, source_target_pairs={{0,2},{2,0},{4,6},{6,4},{8,10},{10,8},{12,14},{14,12},{16,18},{18,... | collective-permute-start | bytes 3145736 | tf_op jit(solution)/shard_map/cond/branch_1_fun/ppermute | solution.py:1002
  385.0 3.0 collective-permute-start.13
  (31 other events, 436.6 us)
Sparse Core Ops, SparseCore 0:
  53.8 82.7 all-gather.1
  154.9 234.0 all-reduce.2

commit v5 on v4

--- a/solution.py
+++ b/solution.py
@@ -768,17 +768,24 @@
 
 
 def merge_kernel(
-    own_ref, other_ref, w_own_ref, w_other_ref, x_ref, gain_ref, attended_ref, hidden_ref, normed_ref
+    own_ref, other_ref, w_own_ref, w_other_ref, x_ref, gain_ref, attended_ref, hidden_ref, normed_ref, theirs_ref
 ):
     groups = 2
-    mine = heads_to_rows(own_ref, groups)
-    attended_ref[...] = mine
-    theirs = heads_to_rows(other_ref, groups)
-    branch = dot_wide(mine, w_own_ref[...]).astype(narrow).astype(wide)
-    branch = branch + dot_wide(theirs, w_other_ref[...]).astype(narrow).astype(wide)
-    hidden = x_ref[...].astype(wide) + branch
-    hidden_ref[...] = hidden
-    normed_ref[...] = (hidden * rms_scale(hidden) * gain_ref[...].astype(wide)[None]).astype(narrow)
+    attended_ref[...] = heads_to_rows(own_ref, groups)
+    theirs_ref[...] = heads_to_rows(other_ref, groups)
+    size = own_ref.shape[1]
+
+    def step(block, carry):
+        span = pl.ds(pl.multiple_of(block * size, size), size)
+        branch = dot_wide(attended_ref[span, :], w_own_ref[...]).astype(narrow).astype(wide)
+        branch = branch + dot_wide(theirs_ref[span, :], w_other_ref[...]).astype(narrow).astype(wide)
+        hidden = x_ref[span, :].astype(wide) + branch
+        hidden_ref[span, :] = hidden
+        normed = hidden * rms_scale(hidden) * gain_ref[...].astype(wide)[None]
+        normed_ref[span, :] = normed.astype(narrow)
+        return carry
+
+    lax.fori_loop(0, 2 * groups, step, 0)
 
 
 def merge(own, other, w_own, w_other, inputs, norm_ffn):
@@ -793,6 +800,7 @@
             jax.ShapeDtypeStruct((tokens, width), wide),
             jax.ShapeDtypeStruct((tokens, width), narrow),
         ],
+        scratch_shapes=[pltpu.VMEM((tokens, local), narrow)],
         compiler_params=pltpu.CompilerParams(vmem_limit_bytes=vmem_bytes),
         cost_estimate=busy(6),
         name="merge",
@@ -822,16 +830,22 @@
     hidden_grad_ref[...] = grad_hidden
     grad_branch = grad_hidden.astype(narrow)
     branch_ref[...] = grad_branch
-    attended_grad = dot_rows(grad_branch, w_ref[...])
-    tokens, local = attended_grad.shape
-    half = tokens // groups // 2
-    for pair in range(local // LANES):
-        for part in range(groups):
+    tokens = grad_branch.shape[0]
+    local = w_ref.shape[0]
+    rows = tokens // groups
+    half = rows // 2
+
+    def step(part, carry):
+        span = pl.ds(pl.multiple_of(part * rows, rows), rows)
+        attended_grad = dot_rows(branch_ref[span, :], w_ref[...])
+        for pair in range(local // LANES):
             cols = slice(pair * LANES, (pair + 1) * LANES)
-            low = attended_grad[2 * part * half : (2 * part + 1) * half, cols]
-            high = attended_grad[(2 * part + 1) * half : (2 * part + 2) * half, cols]
-            for at, tile in enumerate(swap_pairs(low, high)):
+            tiles = swap_pairs(attended_grad[:half, cols], attended_grad[half:, cols])
+            for at, tile in enumerate(tiles):
                 send_ref[2 * pair + at, part] = tile.astype(narrow)
+        return carry
+
+    lax.fori_loop(0, groups, step, 0)
 
 
 def branch_back(own, early, late, hidden, cotangent, norm_ffn, w_out):

time: 422 us -> 428 us (1.014)
  starting transfers between devices: 63.2 us -> 71.1 us
    all_to_all x1, waiting for transfers between devices: 17.7 us -> 7.38 us  [body_heads(): lax.all_to_all(packed, 'dp', split_axis=0, concat_axis=0, tiled=True)]
    psum x1, starting transfers between devices: 0.57 us -> 10.8 us  [body_heads(): ffn_sums = lax.psum(tuple(ffn_grads), 'dp')]
    ppermute x7, waiting for transfers between devices: 70 us -> 80.2 us  [swap_tensor(): return lax.ppermute(values, 'tensor', [(0, 1), (1, 0)])]
where the time goes in v5:
time: 428 us; the launch traced here: 423 us
  waiting for transfers between devices  169 us (39%)
  Pallas kernels  91.7 us (21%)
  starting transfers between devices  71.1 us (17%)
  matrix products  40.5 us (9%)
  other arithmetic  26 us (6%)
  between operations  14.6 us (3%)
  local copies, waits for them, and re-layouts  9.72 us (2%)
    ppermute x7, waiting for transfers between devices, swap_tensor(): return lax.ppermute(values, 'tensor', [(0, 1), (1, 0)])  80.2 us
    pallas_call x1, Pallas kernels, attend_back(): pl.pallas_call(attend_back_kernel, in_specs=[scalar_spec()] * 3 + [whole_...  34.2 us
    all_to_all x1, waiting for transfers between devices, body_heads(): recv = lax.all_to_all(send, 'dp', split_axis=0, concat_axis=0, tiled=True)  24.6 us
    ppermute x12, waiting for transfers between devices, swap_bit(): return lax.ppermute(values, 'dp', [(i, i ^ bit) for i in range(count)])  23.1 us
    pallas_call x1, Pallas kernels, attend(): pl.pallas_call(attend_kernel, in_specs=[scalar_spec()] * 3 + [whole_spec(...  21.3 us
    all_to_all x1, waiting for transfers between devices, way_back(): lax.all_to_all(grad_send.reshape(count, rows // 2, LANES), 'dp', split_ax...  17.5 us
    all_to_all x1, waiting for transfers between devices, spread_line(): lax.all_to_all(copies, 'dp', split_axis=0, concat_axis=0, tiled=True, axi...  15.1 us
    convert_element_type x3, other arithmetic, body_heads(): sums = [after(term, sum_w_out).astype(wide) for term in ffn_sums]  11 us
  transfers between devices with their start and end apart: 27, of which 22 were waited for; matrix products, arithmetic and copies ran while one was open for 15% of the time, Pallas kernels for 20%

profile of v5, /device:TPU:0, one launch (start us, length us, event | category | flops | bytes accessed | tf_op | source)
XLA Modules:
  0.0 423.2 jit_solution(823369752464513077)
XLA Ops:
  7.2 6.2 %project.1 = (bf16[8,2,384,128]{3,2,1,0:T(8,128)(2,1)}, bf16[512,1024]{1,0:T(8,128)(2,1)}) custom-call(s32[1]{0:T(128)} %bitcast.11.place_ref, s32[16]{0:T(128)} %depth_ref.1, bf16[512,1024]{1,0:T(8,128)(2,1)} %x_ref.3, bf16[1024]{0:T(1024)(128)(2,1)} %gain_ref.2, bf16[512,512]{1,0:T(8,128)(2,1)} %first_ref.1, f32[2,56,128]{2,1,0:T(8,128)} %constant.103.clone.turn_ref, ...), custom_call_target="tpu_custom_call" | custom-call | flops 6000000000 | bytes 12000000 | tf_op jit(solution)/shard_map/project/pallas_call | solution.py:468
  13.4 7.4 %all-to-all-start.4 = ((bf16[16,384,128]{2,1,0:T(8,128)(2,1)}), bf16[16,384,128]{2,1,0:T(8,128)(2,1)}, u32[]{:S(2)}, u32[]{:S(2)}) async-start(bf16[16,384,128]{2,1,0:T(8,128)(2,1)} %bitcast.46), calls=%async_computation.4 | async-start | bytes 3145728 | tf_op jit(solution)/shard_map/all_to_all | solution.py:1159
  28.3 24.6 %all-to-all-done.4.recv_ref = bf16[16,384,128]{2,1,0:T(8,128)(2,1)} async-done(((bf16[16,384,128]{2,1,0:T(8,128)(2,1)}), bf16[16,384,128]{2,1,0:T(8,128)(2,1)}, u32[]{:S(2)}, u32[]{:S(2)}) %all-to-all-start.4) | async-done | bytes 1572896 | tf_op jit(solution)/shard_map/all_to_all | solution.py:1159
  57.1 21.3 %attend.1 = (bf16[16,128,128]{2,1,0:T(8,128)(2,1)}, f32[16,64,256]{2,1,0:T(8,128)}, f32[16,8,256]{2,1,0:T(8,128)}) custom-call(s32[16]{0:T(128)S(1)} %copy-done.19, s32[16]{0:T(128)S(1)} %copy-done.20, s32[1]{0:T(128)} %bitcast.10.part_ref, bf16[16,384,128]{2,1,0:T(8,128)(2,1)} %all-to-all-done.4.recv_ref, ...), custom_call_target="tpu_custom_call" | custom-call | flops 22000001024 | bytes 44000000 | tf_op jit(solution)/shard_map/attend/pallas_call | solution.py:654
  78.3 8.8 %all-to-all-start.5 = ((bf16[16,128,128]{2,1,0:T(8,128)(2,1)}), bf16[16,128,128]{2,1,0:T(8,128)(2,1)}, u32[]{:S(2)}, u32[]{:S(2)}) async-start(bf16[16,128,128]{2,1,0:T(8,128)(2,1)} %get-tuple-element.146), calls=%async_computation.5 | async-start | bytes 1048576 | tf_op jit(solution)/shard_map/all_to_all | solution.py:1176
  87.1 10.8 %all-reduce.3.cloned.1.call-start = ((), (), s32[]{:S(2)}) async-start(), calls=%async_computation.7 | async-start | bytes 17301504 | tf_op jit(solution)/shard_map/psum | solution.py:1206
  99.5 7.4 %all-to-all-done.5.own_ref = bf16[16,128,128]{2,1,0:T(8,128)(2,1)} async-done(((bf16[16,128,128]{2,1,0:T(8,128)(2,1)}), bf16[16,128,128]{2,1,0:T(8,128)(2,1)}, u32[]{:S(2)}, u32[]{:S(2)}) %all-to-all-start.5) | async-done | bytes 524320 | tf_op jit(solution)/shard_map/all_to_all | solution.py:1176
  108.4 5.6 %fusion.20 = f32[512,1408]{1,0:T(8,128)} fusion(bf16[512,1024]{1,0:T(8,128)(2,1)} %param.29, bf16[1408,1024]{1,0:T(8,128)(2,1)} %param.26), kind=kOutput, calls=%fused_computation.59 | convolution fusion | flops 1476395008 | bytes 6815744 | tf_op jit(solution)/shard_map/td,fd->tf/dot_general | solution.py:1184
  114.0 10.3 %collective-permute-done.17.w_other_ref = bf16[512,1024]{1,0:T(8,128)(2,1)} collective-permute-done((bf16[512,1024]{1,0:T(8,128)(2,1)}, bf16[512,1024]{1,0:T(8,128)(2,1)}, u32[]{:S(2)}, u32[]{:S(2)}) %collective-permute-start.17) | collective-permute-done | bytes 1048608 | tf_op jit(solution)/shard_map/ppermute | solution.py:1012
  124.3 10.7 %collective-permute-done.16.other_ref = bf16[16,128,128]{2,1,0:T(8,128)(2,1)} collective-permute-done((bf16[16,128,128]{2,1,0:T(8,128)(2,1)}, bf16[16,128,128]{2,1,0:T(8,128)(2,1)}, u32[]{:S(2)}, u32[]{:S(2)}) %collective-permute-start.16) | collective-permute-done | bytes 524320 | tf_op jit(solution)/shard_map/ppermute | solution.py:1012
  135.0 6.2 %merge.1 = (bf16[512,512]{1,0:T(8,128)(2,1)}, f32[512,1024]{1,0:T(8,128)}, bf16[512,1024]{1,0:T(8,128)(2,1)}) custom-call(bf16[16,128,128]{2,1,0:T(8,128)(2,1)} %all-to-all-done.5.own_ref, bf16[16,128,128]{2,1,0:T(8,128)(2,1)} %collective-permute-done.16.other_ref, bf16[512,1024]{1,0:T(8,128)(2,1)} %w_own_ref.1, ...), custom_call_target="tpu_custom_call" | custom-call | flops 6000000000 | bytes 12000000 | tf_op jit(solution)/shard_map/merge/pallas_call | solution.py:794
  171.0 226.6 %conditional.1 = (bf16[512,1024]{1,0:T(8,128)(2,1)}, f32[512,1024]{1,0:T(8,128)}, f32[512,512]{1,0:T(8,128)}, f32[2,1024]{1,0:T(2,128)}, bf16[4,128,1024]{2,1,0:...) conditional(s32[]{:T(128)} %bitcast.9, () %tuple.30, ...), branch_computations={%region_0.1_spmd, %region_1.0_spmd} | conditional | flops 111707529216 | bytes 360422944 | solution.py:1277
  172.9 11.1 %collective-permute-done.late_ref = bf16[256,1024]{1,0:T(8,128)(2,1)} collective-permute-done((bf16[256,1024]{1,0:T(8,128)(2,1)S(1)}, bf16[256,1024]{1,0:T(8,128)(2,1)}, u32[]{:S(2)}, u32[]{:S(2)}) %collective-permute-start) | collective-permute-done | bytes 524320 | tf_op jit(solution)/shard_map/cond/branch_1_fun/ppermute | solution.py:1012
  183.9 6.1 %branch_back.1 = (bf16[8,2,128,128]{3,2,1,0:T(8,128)(2,1)}, f32[512,1024]{1,0:T(8,128)}, bf16[512,1024]{1,0:T(8,128)(2,1)}, f32[1,1024]{1,0:T(1,128)}) custom-call(bf16[512,1024]{1,0:T(8,128)(2,1)S(1)} %get-tuple-element.62.own_ref, bf16[256,1024]{1,0:T(8,128)(2,1)S(1)} %get-tuple-element.63.early_ref, bf16[256,1024]{1,0:T(8,128)(2,1)} %collective-permute-done.late_ref, ...), custom_call_target="tpu_custom_call" | custom-call | flops 6000000000 | bytes 12000000 | tf_op jit(solution)/shard_map/cond/branch_1_fun/branch_back/pallas_call | solution.py:855
  201.0 17.5 %all-to-all-done.grad_ref = bf16[16,128,128]{2,1,0:T(8,128)(2,1)S(1)} async-done(((bf16[16,128,128]{2,1,0:T(8,128)(2,1)}), bf16[16,128,128]{2,1,0:T(8,128)(2,1)S(1)}, u32[]{:S(2)}, u32[]{:S(2)}) %all-to-all-start) | async-done | bytes 524320 | tf_op jit(solution)/shard_map/cond/branch_1_fun/all_to_all | solution.py:1214
  223.4 34.2 %attend_back.1 = (bf16[16,128,128]{2,1,0:T(8,128)(2,1)}, f32[16,256,128]{2,1,0:T(8,128)}, bf16[16,256,128]{2,1,0:T(8,128)(2,1)}) custom-call(s32[16]{0:T(128)S(1)} %get-tuple-element.58.parents_ref, s32[16]{0:T(128)S(1)} %get-tuple-element.59.assign_ref, s32[1]{0:T(128)} %get-tuple-element.56.part_ref, bf16[16,384,128]{2,1,0:T(8,128)(2,1)} %get-tuple-element.60.recv_ref, ...), custom_call_target="tpu_custom_call" | custom-call | flops 36999999488 | bytes 74000000 | tf_op jit(solution)/shard_map/cond/branch_1_fun/attend_back/pallas_call | solution.py:736
  266.6 6.2 %all-to-all-start.2 = ((bf16[16,384,128]{2,1,0:T(8,128)(2,1)}), bf16[16,384,128]{2,1,0:T(8,128)(2,1)}, u32[]{:S(2)}, u32[]{:S(2)}) async-start(bf16[16,384,128]{2,1,0:T(8,128)(2,1)} %fold.1), calls=%async_computation.2 | async-start | bytes 3145728 | tf_op jit(solution)/shard_map/cond/branch_1_fun/all_to_all | solution.py:1233
  276.8 14.1 %collective-permute-done.3 = bf16[2048,1024]{1,0:T(8,128)(2,1)} collective-permute-done((bf16[2048,1024]{1,0:T(8,128)(2,1)}, bf16[2048,1024]{1,0:T(8,128)(2,1)}, u32[]{:S(2)}, u32[]{:S(2)}) %collective-permute-start.3) | collective-permute-done | bytes 4194336 | tf_op jit(solution)/shard_map/cond/branch_1_fun/ppermute | solution.py:1012
  298.8 16.6 %collective-permute-done.4 = bf16[512,1024]{1,0:T(8,128)(2,1)} collective-permute-done((bf16[512,1024]{1,0:T(8,128)(2,1)S(1)}, bf16[512,1024]{1,0:T(8,128)(2,1)}, u32[]{:S(2)}, u32[]{:S(2)}) %collective-permute-start.4) | collective-permute-done | bytes 1048608 | tf_op jit(solution)/shard_map/cond/branch_1_fun/ppermute | solution.py:1012
  324.2 8.9 %all-to-all-start.3 = ((bf16[4,128,1024]{2,1,0:T(8,128)(2,1)}), bf16[4,128,1024]{2,1,0:T(8,128)(2,1)}, u32[]{:S(2)}, u32[]{:S(2)}) async-start(bf16[4,128,1024]{2,1,0:T(8,128)(2,1)} %broadcast_in_dim.0), calls=%async_computation.3 | async-start | bytes 2097152 | tf_op jit(solution)/shard_map/cond/branch_1_fun/all_to_all | solution.py:1051
  333.4 15.7 %collective-permute-done.6 = bf16[512,1024]{1,0:T(8,128)(2,1)} collective-permute-done((bf16[512,1024]{1,0:T(8,128)(2,1)}, bf16[512,1024]{1,0:T(8,128)(2,1)}, u32[]{:S(2)}, u32[]{:S(2)}) %collective-permute-start.6) | collective-permute-done | bytes 1048608 | tf_op jit(solution)/shard_map/cond/branch_1_fun/ppermute | solution.py:1012
  355.5 15.1 %all-to-all-done.3 = bf16[4,128,1024]{2,1,0:T(8,128)(2,1)} async-done(((bf16[4,128,1024]{2,1,0:T(8,128)(2,1)}), bf16[4,128,1024]{2,1,0:T(8,128)(2,1)}, u32[]{:S(2)}, u32[]{:S(2)}) %all-to-all-start.3) | async-done | bytes 1048608 | tf_op jit(solution)/shard_map/cond/branch_1_fun/all_to_all | solution.py:1051
  384.6 9.8 %collective-permute-done.11 = bf16[4,128,1024]{2,1,0:T(8,128)(2,1)} collective-permute-done((bf16[4,128,1024]{2,1,0:T(8,128)(2,1)}, bf16[4,128,1024]{2,1,0:T(8,128)(2,1)}, u32[]{:S(2)}, u32[]{:S(2)}) %collective-permute-start.11) | collective-permute-done | bytes 1048608 | tf_op jit(solution)/shard_map/cond/branch_1_fun/ppermute | solution.py:1016
  397.7 7.3 %finish.1 = (f32[1024,512]{1,0:T(8,128)}, f32[1024,512]{1,0:T(8,128)}, f32[1024,512]{1,0:T(8,128)}, f32[512,1024]{1,0:T(8,128)}) custom-call(s32[1]{0:T(128)} %bitcast.11.place_ref, bf16[4,128,1024]{2,1,0:T(8,128)(2,1)} %get-tuple-element.161.near_ref, bf16[4,128,1024]{2,1,0:T(8,128)(2,1)} %get-tuple-element.162.far_ref, ...), custom_call_target="tpu_custom_call" | custom-call | flops 6000000000 | bytes 12000000 | tf_op jit(solution)/shard_map/finish/pallas_call | solution.py:999
  (147 shorter events, 126.1 us)
Async XLA Ops:
  13.4 39.5 %all-to-all-start.4 = ((bf16[16,384,128]{2,1,0:T(8,128)(2,1)}), bf16[16,384,128]{2,1,0:T(8,128)(2,1)}, u32[]{:S(2)}, u32[]{:S(2)}) async-start(bf16[16,384,128]{2,1,0:T(8,128)(2,1)} %bitcast.46), calls=%async_computation.4 | async-start | bytes 3145728 | tf_op jit(solution)/shard_map/all_to_all | solution.py:1159
  20.9 143.2 %all-gather.2.cloned.1.call-start = ((), (), s32[]{:S(2)}) async-start(), calls=%async_computation.6 | async-start | bytes 4718592 | tf_op jit(solution)/shard_map/all_gather | solution.py:1170
  23.0 2.3 collective-permute-start.14
  52.9 4.1 collective-permute-start.15
  78.3 28.5 %all-to-all-start.5 = ((bf16[16,128,128]{2,1,0:T(8,128)(2,1)}), bf16[16,128,128]{2,1,0:T(8,128)(2,1)}, u32[]{:S(2)}, u32[]{:S(2)}) async-start(bf16[16,128,128]{2,1,0:T(8,128)(2,1)} %get-tuple-element.146), calls=%async_computation.5 | async-start | bytes 1048576 | tf_op jit(solution)/shard_map/all_to_all | solution.py:1176
  87.1 317.9 %all-reduce.3.cloned.1.call-start = ((), (), s32[]{:S(2)}) async-start(), calls=%async_computation.7 | async-start | bytes 17301504 | tf_op jit(solution)/shard_map/psum | solution.py:1206
  97.9 26.4 %collective-permute-start.17 = (bf16[512,1024]{1,0:T(8,128)(2,1)}, bf16[512,1024]{1,0:T(8,128)(2,1)}, u32[]{:S(2)}, u32[]{:S(2)}) collective-permute-start(bf16[512,1024]{1,0:T(8,128)(2,1)} %w_own_ref.1), channel_id=1, source_target_pairs={{0,1},{1,0},{2,3},{3,2},{4,5},{5,4},{6,7},{7,6},{8,9},{9,8},{10,11... | collective-permute-start | bytes 3145736 | tf_op jit(solution)/shard_map/ppermute | solution.py:1012
  106.9 28.1 %collective-permute-start.16 = (bf16[16,128,128]{2,1,0:T(8,128)(2,1)}, bf16[16,128,128]{2,1,0:T(8,128)(2,1)}, u32[]{:S(2)}, u32[]{:S(2)}) collective-permute-start(bf16[16,128,128]{2,1,0:T(8,128)(2,1)} %all-to-all-done.5.own_ref), channel_id=1, source_target_pairs={{0,1},{1,0},{2,3},{3,2},{4,5},{5,4},{6,7},{7,6},{8,9},{9,8},{10,11... | collective-permute-start | bytes 1572872 | tf_op jit(solution)/shard_map/ppermute | solution.py:1012
  152.3 13.4 %collective-permute-start.18 = (bf16[256,1024]{1,0:T(8,128)(2,1)S(1)}, bf16[256,1024]{1,0:T(8,128)(2,1)S(1)}, u32[]{:S(2)}, u32[]{:S(2)}) collective-permute-start(bf16[256,1024]{1,0:T(8,128)(2,1)S(1)} %slice.47), channel_id=1, source_target_pairs={{0,1},{1,0},{2,3},{3,2},{4,5},{5,4},{6,7},{7,6},{8,9},{9,8},{10,11... | collective-permute-start | bytes 1572872 | tf_op jit(solution)/shard_map/ppermute | solution.py:1012
  171.3 12.6 %collective-permute-start = (bf16[256,1024]{1,0:T(8,128)(2,1)S(1)}, bf16[256,1024]{1,0:T(8,128)(2,1)}, u32[]{:S(2)}, u32[]{:S(2)}) collective-permute-start(bf16[256,1024]{1,0:T(8,128)(2,1)S(1)} %slice.28), channel_id=1, source_target_pairs={{0,1},{1,0},{2,3},{3,2},{4,5},{5,4},{6,7},{7,6},{8,9},{9,8},{10,11... | collective-permute-start | bytes 1572872 | tf_op jit(solution)/shard_map/cond/branch_1_fun/ppermute | solution.py:1012
  190.1 28.4 %all-to-all-start = ((bf16[16,128,128]{2,1,0:T(8,128)(2,1)}), bf16[16,128,128]{2,1,0:T(8,128)(2,1)S(1)}, u32[]{:S(2)}, u32[]{:S(2)}) async-start(bf16[16,128,128]{2,1,0:T(8,128)(2,1)} %bitcast.49), calls=%async_computation | async-start | bytes 1048576 | tf_op jit(solution)/shard_map/cond/branch_1_fun/all_to_all | solution.py:1214
  198.0 92.9 %collective-permute-start.3 = (bf16[2048,1024]{1,0:T(8,128)(2,1)}, bf16[2048,1024]{1,0:T(8,128)(2,1)}, u32[]{:S(2)}, u32[]{:S(2)}) collective-permute-start(bf16[2048,1024]{1,0:T(8,128)(2,1)} %get-tuple-element.82), channel_id=1, source_target_pairs={{0,1},{1,0},{2,3},{3,2},{4,5},{5,4},{6,7},{7,6},{8,9},{9,8},{10,11... | collective-permute-start | bytes 12582920 | tf_op jit(solution)/shard_map/cond/branch_1_fun/ppermute | solution.py:1012
  219.5 38.2 %all-to-all-start.1 = ((bf16[8,32,1024]{2,1,0:T(8,128)(2,1)}), bf16[8,32,1024]{2,1,0:T(8,128)(2,1)S(1)}, u32[]{:S(2)}, u32[]{:S(2)}) async-start(bf16[8,32,1024]{2,1,0:T(8,128)(2,1)} %bitcast.3), calls=%async_computation.1 | async-start | bytes 1048576 | tf_op jit(solution)/shard_map/cond/branch_1_fun/all_to_all | solution.py:1039
  257.7 2.9 collective-permute-start.2
  266.6 49.8 %all-to-all-start.2 = ((bf16[16,384,128]{2,1,0:T(8,128)(2,1)}), bf16[16,384,128]{2,1,0:T(8,128)(2,1)}, u32[]{:S(2)}, u32[]{:S(2)}) async-start(bf16[16,384,128]{2,1,0:T(8,128)(2,1)} %fold.1), calls=%async_computation.2 | async-start | bytes 3145728 | tf_op jit(solution)/shard_map/cond/branch_1_fun/all_to_all | solution.py:1233
  291.0 24.4 %collective-permute-start.4 = (bf16[512,1024]{1,0:T(8,128)(2,1)S(1)}, bf16[512,1024]{1,0:T(8,128)(2,1)}, u32[]{:S(2)}, u32[]{:S(2)}) collective-permute-start(bf16[512,1024]{1,0:T(8,128)(2,1)S(1)} %copy-done.9), channel_id=1, source_target_pairs={{0,1},{1,0},{2,3},{3,2},{4,5},{5,4},{6,7},{7,6},{8,9},{9,8},{10,11... | collective-permute-start | bytes 3145736 | tf_op jit(solution)/shard_map/cond/branch_1_fun/ppermute | solution.py:1012
  322.8 26.3 %collective-permute-start.6 = (bf16[512,1024]{1,0:T(8,128)(2,1)}, bf16[512,1024]{1,0:T(8,128)(2,1)}, u32[]{:S(2)}, u32[]{:S(2)}) collective-permute-start(bf16[512,1024]{1,0:T(8,128)(2,1)} %get-tuple-element.93), channel_id=1, source_target_pairs={{0,1},{1,0},{2,3},{3,2},{4,5},{5,4},{6,7},{7,6},{8,9},{9,8},{10,11... | collective-permute-start | bytes 3145736 | tf_op jit(solution)/shard_map/cond/branch_1_fun/ppermute | solution.py:1012
  324.2 46.3 %all-to-all-start.3 = ((bf16[4,128,1024]{2,1,0:T(8,128)(2,1)}), bf16[4,128,1024]{2,1,0:T(8,128)(2,1)}, u32[]{:S(2)}, u32[]{:S(2)}) async-start(bf16[4,128,1024]{2,1,0:T(8,128)(2,1)} %broadcast_in_dim.0), calls=%async_computation.3 | async-start | bytes 2097152 | tf_op jit(solution)/shard_map/cond/branch_1_fun/all_to_all | solution.py:1051
  352.5 23.0 %collective-permute-start.8 = (f32[2,1024]{1,0:T(2,128)S(1)}, f32[2,1024]{1,0:T(2,128)S(1)}, u32[]{:S(2)}, u32[]{:S(2)}) collective-permute-start(f32[2,1024]{1,0:T(2,128)S(1)} %fusion.12), channel_id=1, source_target_pairs={{0,4},{2,6},{4,0},{6,2},{8,12},{10,14},{12,8},{14,10},{16,20},{18,... | collective-permute-start | bytes 24584 | tf_op jit(solution)/shard_map/cond/branch_1_fun/ppermute | solution.py:1016
  370.6 23.9 %collective-permute-start.11 = (bf16[4,128,1024]{2,1,0:T(8,128)(2,1)}, bf16[4,128,1024]{2,1,0:T(8,128)(2,1)}, u32[]{:S(2)}, u32[]{:S(2)}) collective-permute-start(bf16[4,128,1024]{2,1,0:T(8,128)(2,1)} %all-to-all-done.3), channel_id=1, source_target_pairs={{0,4},{2,6},{4,0},{6,2},{8,12},{10,14},{12,8},{14,10},{16,20},{18,... | collective-permute-start | bytes 3145736 | tf_op jit(solution)/shard_map/cond/branch_1_fun/ppermute | solution.py:1016
  375.5 3.8 collective-permute-start.9
  379.3 4.7 %collective-permute-start.10 = (f32[2,1024]{1,0:T(2,128)S(1)}, f32[2,1024]{1,0:T(2,128)S(1)}, u32[]{:S(2)}, u32[]{:S(2)}) collective-permute-start(f32[2,1024]{1,0:T(2,128)S(1)} %add.107), channel_id=1, source_target_pairs={{0,16},{2,18},{4,20},{6,22},{8,24},{10,26},{12,28},{14,30},{16,0},... | collective-permute-start | bytes 24584 | tf_op jit(solution)/shard_map/cond/branch_1_fun/ppermute | solution.py:1016
  384.6 12.6 %collective-permute-start.12 = (bf16[4,128,1024]{2,1,0:T(8,128)(2,1)}, bf16[4,128,1024]{2,1,0:T(8,128)(2,1)}, u32[]{:S(2)}, u32[]{:S(2)}) collective-permute-start(bf16[4,128,1024]{2,1,0:T(8,128)(2,1)} %all-to-all-done.3), channel_id=1, source_target_pairs={{0,2},{2,0},{4,6},{6,4},{8,10},{10,8},{12,14},{14,12},{16,18},{18,... | collective-permute-start | bytes 3145736 | tf_op jit(solution)/shard_map/cond/branch_1_fun/ppermute | solution.py:1016
  394.4 3.0 collective-permute-start.13
  (31 other events, 467.7 us)
Sparse Core Ops, SparseCore 0:
  53.8 82.6 all-gather.1
  165.9 232.3 all-reduce.2
